TPU v7x, 32 devices: a whole 2x2x4 slice. The times are simulated.
32 devices in a mesh: dp: 2 (over x), fsdp: 16 (over z, y, core).
Axes of the slice: x: 2, y: 2, z: 4, core: 2. Of those that a mesh axis runs over, the one named last changes fastest.
Arguments:
- tokens: bfloat16 [32, 512, 1024], P(('dp', 'fsdp')), may hold values from -6 to 6
- lengths: int32 [32], P(('dp', 'fsdp')), may hold values from 128 to 512, as said below
- time_embed: bfloat16 [32, 256], P(('dp', 'fsdp')), may hold values from -6 to 6
- cotangent: bfloat16 [32, 512, 1024], P(('dp', 'fsdp')), may hold values from -6 to 6
- time_weight: bfloat16 [256, 1024], P('fsdp'), may hold values from -0.1875 to 0.1875
- attn_gain: bfloat16 [1024], P('fsdp'), may hold values from 0.099609375 to 1.8984375
- attn_shift: bfloat16 [1024], P('fsdp'), may hold values from -3 to 3
- qkv_weight: bfloat16 [1024, 3072], P('fsdp'), may hold values from -0.1875 to 0.1875
- out_weight: bfloat16 [1024, 1024], P('fsdp'), may hold values from -0.75 to 0.75
- mlp_gain: bfloat16 [1024], P('fsdp'), may hold values from 0.099609375 to 1.8984375
- mlp_shift: bfloat16 [1024], P('fsdp'), may hold values from -3 to 3
- up_weight: bfloat16 [1024, 4096], P('fsdp'), may hold values from -0.1875 to 0.1875
- up_bias: bfloat16 [4096], P('fsdp'), may hold values from -3 to 3
- down_weight: bfloat16 [4096, 1024], P('fsdp'), may hold values from -0.09375 to 0.09375
- down_bias: bfloat16 [1024], P('fsdp'), may hold values from -3 to 3
Outputs:
- layer_out: bfloat16 [32, 512, 1024], P(('dp', 'fsdp'))
- token_grad: bfloat16 [32, 512, 1024], P(('dp', 'fsdp'))
- time_weight_grad: float32 [256, 1024], P('fsdp')
- attn_gain_grad: float32 [1024], P('fsdp')
- attn_shift_grad: float32 [1024], P('fsdp')
- qkv_weight_grad: float32 [1024, 3072], P('fsdp')
- out_weight_grad: float32 [1024, 1024], P('fsdp')
- mlp_gain_grad: float32 [1024], P('fsdp')
- mlp_shift_grad: float32 [1024], P('fsdp')
- up_weight_grad: float32 [1024, 4096], P('fsdp')
- up_bias_grad: float32 [4096], P('fsdp')
- down_weight_grad: float32 [4096, 1024], P('fsdp')
- down_bias_grad: float32 [1024], P('fsdp')
Inputs may be any that keep to these rules, and one draw needn't show every extreme that they name: `lengths`: each sequence's count of real tokens; one sequence of every draw has 512.
All inputs are finite; a program needn't handle non-finite values.
Results may differ from a plain program's by a relative error of at most 0.02.
Values may be sent and summed in bfloat16 or wider, within the bound.
No kernel may reach another device: no remote copies, remote signals or barrier semaphores. Data moves between devices by JAX's collectives and lax.ppermute only.
A program may use at most 192 MiB of HBM per device.

v0:
```python
import math

import jax
import jax.numpy as jnp
from jax import lax
from jax.sharding import PartitionSpec as P

HEADS = 16
HD = 64


def normalize(values_in):
    center = values_in - jnp.mean(values_in, axis=-1, keepdims=True)
    inverse = lax.rsqrt(jnp.mean(center * center, axis=-1, keepdims=True) + 1e-05)
    return (center * inverse, inverse)


def norm_back(grad_hat, normed, inverse):
    return inverse * (
        grad_hat
        - jnp.mean(grad_hat, axis=-1, keepdims=True)
        - normed * jnp.mean(grad_hat * normed, axis=-1, keepdims=True)
    )


def rotary_tables(length, head_size):
    half_size = head_size // 2
    frequency = jnp.exp(
        jnp.arange(half_size, dtype=jnp.float32) * (-2.0 * math.log(10000.0) / head_size)
    )
    angles = jnp.arange(length, dtype=jnp.float32)[:, None] * frequency[None, :]
    angles = jnp.concatenate([angles, angles], axis=-1)
    return (jnp.cos(angles)[:, None, :], jnp.sin(angles)[:, None, :])


def rotate(values_in, cosine_table, sine_table):
    half_size = values_in.shape[-1] // 2
    turned = jnp.concatenate([-values_in[..., half_size:], values_in[..., :half_size]], axis=-1)
    return values_in * cosine_table + turned * sine_table


def rotate_back(grad_in, cosine_table, sine_table):
    half_size = grad_in.shape[-1] // 2
    sined = grad_in * sine_table
    return grad_in * cosine_table + jnp.concatenate(
        [sined[..., half_size:], -sined[..., :half_size]], axis=-1
    )


def rows_dot(left, right):
    return lax.dot_general(
        left, right, (((0,), (0,)), ((), ())), preferred_element_type=jnp.float32
    )


def back_dot(grad_in, weight):
    return lax.dot_general(
        grad_in, weight, (((1,), (1,)), ((), ())), preferred_element_type=jnp.float32
    )


def scores_of(query_pair, key_pair, key_mask, factor):
    raw_scores = (
        jnp.einsum("bqgd,bkgd->bgqk", query_pair, key_pair, preferred_element_type=jnp.float32)
        * factor
    )
    return jnp.where(key_mask[:, None, None, :], raw_scores, -1000000000.0)


def per_device(
    tokens,
    lengths,
    time_embed,
    cotangent,
    time_weight,
    attn_gain,
    attn_shift,
    qkv_weight,
    out_weight,
    mlp_gain,
    mlp_shift,
    up_weight,
    up_bias,
    down_weight,
    down_bias,
):
    seq_count, length, features = tokens.shape
    flat_rows = seq_count * length
    pair_count = HEADS // 2
    factor = HD ** (-0.5)
    time_full, gain_one, shift_one, qkv_full, out_full = (
        lax.all_gather(time_weight, "fsdp", axis=0, tiled=True),
        lax.all_gather(attn_gain, "fsdp", axis=0, tiled=True),
        lax.all_gather(attn_shift, "fsdp", axis=0, tiled=True),
        lax.all_gather(qkv_weight, "fsdp", axis=0, tiled=True),
        lax.all_gather(out_weight, "fsdp", axis=0, tiled=True),
    )
    gain_two, shift_two, up_full, up_bias_full, down_full, down_bias_full = (
        lax.all_gather(mlp_gain, "fsdp", axis=0, tiled=True),
        lax.all_gather(mlp_shift, "fsdp", axis=0, tiled=True),
        lax.all_gather(up_weight, "fsdp", axis=0, tiled=True),
        lax.all_gather(up_bias, "fsdp", axis=0, tiled=True),
        lax.all_gather(down_weight, "fsdp", axis=0, tiled=True),
        lax.all_gather(down_bias, "fsdp", axis=0, tiled=True),
    )
    key_mask = jnp.arange(length, dtype=jnp.int32)[None, :] < lengths[:, None]
    residual = tokens.astype(jnp.float32)
    time_scale = (
        1.0 + jnp.dot(time_embed, time_full, preferred_element_type=jnp.float32)[:, None, :]
    )
    normed_one, inverse_one = normalize(residual)
    affine_one = normed_one * gain_one.astype(jnp.float32) + shift_one.astype(jnp.float32)
    attn_in = (affine_one * time_scale).astype(jnp.bfloat16).reshape(flat_rows, features)
    qkv = jnp.dot(attn_in, qkv_full, preferred_element_type=jnp.float32).reshape(
        seq_count, length, 3, HEADS, HD
    )
    cosine_table, sine_table = rotary_tables(length, HD)
    query_rows = rotate(qkv[:, :, 0], cosine_table, sine_table).astype(jnp.bfloat16)
    key_rows = rotate(qkv[:, :, 1], cosine_table, sine_table).astype(jnp.bfloat16)
    value_rows = qkv[:, :, 2].astype(jnp.bfloat16)

    def by_pairs(values_in):
        return values_in.reshape(seq_count, length, pair_count, 2, HD).transpose(2, 0, 1, 3, 4)

    def from_pairs(values_in):
        return values_in.transpose(1, 2, 0, 3, 4).reshape(seq_count, length, features)

    query_group = by_pairs(query_rows)
    key_group = by_pairs(key_rows)
    value_group = by_pairs(value_rows)

    def attend(operands):
        query_pair, key_pair, value_pair = operands
        scores = scores_of(query_pair, key_pair, key_mask, factor)
        row_max = jnp.max(scores, axis=-1, keepdims=True)
        exponent = jnp.exp(scores - row_max)
        row_total = jnp.sum(exponent, axis=-1, keepdims=True)
        attn_probs = (exponent / row_total).astype(jnp.bfloat16)
        mixed_rows = jnp.einsum(
            "bgqk,bkgd->bqgd", attn_probs, value_pair, preferred_element_type=jnp.float32
        )
        return (mixed_rows.astype(jnp.bfloat16), (row_max + jnp.log(row_total))[..., 0])

    context_group, log_totals = lax.map(attend, (query_group, key_group, value_group))
    context = from_pairs(context_group).reshape(flat_rows, features)
    hidden = residual + jnp.dot(context, out_full, preferred_element_type=jnp.float32).reshape(
        seq_count, length, features
    )
    normed_two, inverse_two = normalize(hidden)
    affine_two = normed_two * gain_two.astype(jnp.float32) + shift_two.astype(jnp.float32)
    mlp_in = (affine_two * time_scale).astype(jnp.bfloat16).reshape(flat_rows, features)
    pre_act = jnp.dot(mlp_in, up_full, preferred_element_type=jnp.float32) + up_bias_full.astype(
        jnp.float32
    )
    active = jax.nn.gelu(pre_act).astype(jnp.bfloat16)
    branch_out = jnp.dot(
        active, down_full, preferred_element_type=jnp.float32
    ) + down_bias_full.astype(jnp.float32)
    layer_out = (hidden + branch_out.reshape(seq_count, length, features)).astype(jnp.bfloat16)
    gain_two, shift_two, up_full, up_bias_full, down_full, down_bias_full = (
        lax.all_gather(mlp_gain, "fsdp", axis=0, tiled=True),
        lax.all_gather(mlp_shift, "fsdp", axis=0, tiled=True),
        lax.all_gather(up_weight, "fsdp", axis=0, tiled=True),
        lax.all_gather(up_bias, "fsdp", axis=0, tiled=True),
        lax.all_gather(down_weight, "fsdp", axis=0, tiled=True),
        lax.all_gather(down_bias, "fsdp", axis=0, tiled=True),
    )
    grad_out = cotangent.astype(jnp.float32) * key_mask[:, :, None].astype(jnp.float32)
    grad_branch = grad_out.astype(jnp.bfloat16).reshape(flat_rows, features)
    down_weight_grad = rows_dot(active, grad_branch)
    down_bias_grad = jnp.sum(grad_branch.astype(jnp.float32), axis=0)
    grad_active = back_dot(grad_branch, down_full)
    gelu_value, gelu_pull = jax.vjp(jax.nn.gelu, pre_act)
    grad_pre = gelu_pull(grad_active)[0].astype(jnp.bfloat16)
    up_bias_grad = jnp.sum(grad_pre.astype(jnp.float32), axis=0)
    up_weight_grad = rows_dot(mlp_in, grad_pre)
    grad_mlp_in = back_dot(grad_pre, up_full).reshape(seq_count, length, features)
    grad_affine_two = grad_mlp_in * time_scale
    grad_scale = jnp.sum(grad_mlp_in * affine_two, axis=1)
    mlp_gain_grad = jnp.sum(grad_affine_two * normed_two, axis=(0, 1))
    mlp_shift_grad = jnp.sum(grad_affine_two, axis=(0, 1))
    grad_hidden = grad_out + norm_back(
        grad_affine_two * gain_two.astype(jnp.float32), normed_two, inverse_two
    )
    time_full, gain_one, shift_one, qkv_full, out_full = (
        lax.all_gather(time_weight, "fsdp", axis=0, tiled=True),
        lax.all_gather(attn_gain, "fsdp", axis=0, tiled=True),
        lax.all_gather(attn_shift, "fsdp", axis=0, tiled=True),
        lax.all_gather(qkv_weight, "fsdp", axis=0, tiled=True),
        lax.all_gather(out_weight, "fsdp", axis=0, tiled=True),
    )
    grad_attn = grad_hidden.astype(jnp.bfloat16).reshape(flat_rows, features)
    out_weight_grad = rows_dot(context, grad_attn)
    grad_context = back_dot(grad_attn, out_full).astype(jnp.bfloat16)

    def attend_back(operands):
        query_pair, key_pair, value_pair, log_pair, grad_pair = operands
        scores = scores_of(query_pair, key_pair, key_mask, factor)
        probs_full = jnp.exp(scores - log_pair[..., None])
        attn_probs = probs_full.astype(jnp.bfloat16)
        grad_value = jnp.einsum(
            "bgqk,bqgd->bkgd", attn_probs, grad_pair, preferred_element_type=jnp.float32
        )
        grad_probs = jnp.einsum(
            "bqgd,bkgd->bgqk", grad_pair, value_pair, preferred_element_type=jnp.float32
        )
        grad_scores = probs_full * (
            grad_probs - jnp.sum(grad_probs * probs_full, axis=-1, keepdims=True)
        )
        grad_scores = grad_scores.astype(jnp.bfloat16)
        grad_query = (
            jnp.einsum("bgqk,bkgd->bqgd", grad_scores, key_pair, preferred_element_type=jnp.float32)
            * factor
        )
        grad_key = (
            jnp.einsum(
                "bgqk,bqgd->bkgd", grad_scores, query_pair, preferred_element_type=jnp.float32
            )
            * factor
        )
        return (grad_query, grad_key, grad_value)

    grad_query_group, grad_key_group, grad_value_group = lax.map(
        attend_back, (query_group, key_group, value_group, log_totals, by_pairs(grad_context))
    )
    head_shape = (seq_count, length, HEADS, HD)
    grad_query_raw = rotate_back(
        from_pairs(grad_query_group).reshape(head_shape), cosine_table, sine_table
    )
    grad_key_raw = rotate_back(
        from_pairs(grad_key_group).reshape(head_shape), cosine_table, sine_table
    )
    grad_value_raw = from_pairs(grad_value_group).reshape(head_shape)
    grad_qkv = (
        jnp.stack([grad_query_raw, grad_key_raw, grad_value_raw], axis=2)
        .astype(jnp.bfloat16)
        .reshape(flat_rows, 3 * features)
    )
    qkv_weight_grad = rows_dot(attn_in, grad_qkv)
    grad_attn_in = back_dot(grad_qkv, qkv_full).reshape(seq_count, length, features)
    grad_affine_one = grad_attn_in * time_scale
    grad_scale = grad_scale + jnp.sum(grad_attn_in * affine_one, axis=1)
    attn_gain_grad = jnp.sum(grad_affine_one * normed_one, axis=(0, 1))
    attn_shift_grad = jnp.sum(grad_affine_one, axis=(0, 1))
    token_grad = (
        grad_hidden
        + norm_back(grad_affine_one * gain_one.astype(jnp.float32), normed_one, inverse_one)
    ).astype(jnp.bfloat16)
    time_weight_grad = jnp.dot(
        time_embed.astype(jnp.float32).T, grad_scale, precision=lax.Precision.HIGHEST
    )
    parts_all = (
        lax.psum_scatter(
            time_weight_grad.astype(jnp.bfloat16), "fsdp", scatter_dimension=0, tiled=True
        ).astype(jnp.float32),
        lax.psum_scatter(
            attn_gain_grad.astype(jnp.bfloat16), "fsdp", scatter_dimension=0, tiled=True
        ).astype(jnp.float32),
        lax.psum_scatter(
            attn_shift_grad.astype(jnp.bfloat16), "fsdp", scatter_dimension=0, tiled=True
        ).astype(jnp.float32),
        lax.psum_scatter(
            qkv_weight_grad.astype(jnp.bfloat16), "fsdp", scatter_dimension=0, tiled=True
        ).astype(jnp.float32),
        lax.psum_scatter(
            out_weight_grad.astype(jnp.bfloat16), "fsdp", scatter_dimension=0, tiled=True
        ).astype(jnp.float32),
        lax.psum_scatter(
            mlp_gain_grad.astype(jnp.bfloat16), "fsdp", scatter_dimension=0, tiled=True
        ).astype(jnp.float32),
        lax.psum_scatter(
            mlp_shift_grad.astype(jnp.bfloat16), "fsdp", scatter_dimension=0, tiled=True
        ).astype(jnp.float32),
        lax.psum_scatter(
            up_weight_grad.astype(jnp.bfloat16), "fsdp", scatter_dimension=0, tiled=True
        ).astype(jnp.float32),
        lax.psum_scatter(
            up_bias_grad.astype(jnp.bfloat16), "fsdp", scatter_dimension=0, tiled=True
        ).astype(jnp.float32),
        lax.psum_scatter(
            down_weight_grad.astype(jnp.bfloat16), "fsdp", scatter_dimension=0, tiled=True
        ).astype(jnp.float32),
        lax.psum_scatter(
            down_bias_grad.astype(jnp.bfloat16), "fsdp", scatter_dimension=0, tiled=True
        ).astype(jnp.float32),
    )
    attn_parts = parts_all[:5]
    mlp_parts = parts_all[5:]
    summed = (
        lax.psum(attn_parts[0].astype(jnp.bfloat16), "dp").astype(jnp.float32),
        lax.psum(attn_parts[1].astype(jnp.bfloat16), "dp").astype(jnp.float32),
        lax.psum(attn_parts[2].astype(jnp.bfloat16), "dp").astype(jnp.float32),
        lax.psum(attn_parts[3].astype(jnp.bfloat16), "dp").astype(jnp.float32),
        lax.psum(attn_parts[4].astype(jnp.bfloat16), "dp").astype(jnp.float32),
        lax.psum(mlp_parts[0].astype(jnp.bfloat16), "dp").astype(jnp.float32),
        lax.psum(mlp_parts[1].astype(jnp.bfloat16), "dp").astype(jnp.float32),
        lax.psum(mlp_parts[2].astype(jnp.bfloat16), "dp").astype(jnp.float32),
        lax.psum(mlp_parts[3].astype(jnp.bfloat16), "dp").astype(jnp.float32),
        lax.psum(mlp_parts[4].astype(jnp.bfloat16), "dp").astype(jnp.float32),
        lax.psum(mlp_parts[5].astype(jnp.bfloat16), "dp").astype(jnp.float32),
    )
    return (
        layer_out,
        token_grad,
        summed[0],
        summed[1],
        summed[2],
        summed[3],
        summed[4],
        summed[5],
        summed[6],
        summed[7],
        summed[8],
        summed[9],
        summed[10],
    )


def solution(mesh):
    return jax.shard_map(
        per_device,
        mesh=mesh,
        in_specs=(
            P(("dp", "fsdp"), None, None),
            P(("dp", "fsdp")),
            P(("dp", "fsdp"), None),
            P(("dp", "fsdp"), None, None),
            P("fsdp", None),
            P("fsdp"),
            P("fsdp"),
            P("fsdp", None),
            P("fsdp", None),
            P("fsdp"),
            P("fsdp"),
            P("fsdp", None),
            P("fsdp"),
            P("fsdp", None),
            P("fsdp"),
        ),
        out_specs=(
            P(("dp", "fsdp"), None, None),
            P(("dp", "fsdp"), None, None),
            P("fsdp", None),
            P("fsdp"),
            P("fsdp"),
            P("fsdp", None),
            P("fsdp", None),
            P("fsdp"),
            P("fsdp"),
            P("fsdp", None),
            P("fsdp"),
            P("fsdp", None),
            P("fsdp"),
        ),
        check_vma=False,
    )
```

profile of v0, /device:TPU:0, one launch (start us, length us, event | category | flops | bytes accessed | tf_op | source)
XLA Modules:
  0.0 823.9 jit_solution(15790023884834420819)
XLA Ops:
  15.5 37.3 %all-reduce.12 = (bf16[1024]{0:T(1024)(128)(2,1)S(1)}, bf16[1024]{0:T(1024)(128)(2,1)S(1)}, bf16[1024]{0:T(1024)(128)(2,1)S(1)}, bf16[1024]{0:T(1024)(128)(2,1)S(1)}) all-reduce(bf16[1024]{0:T(1024)(128)(2,1)S(1)} %dynamic-update-slice.1, bf16[1024]{0:T(1024)(128)(2,1)S(1)} %dynamic-update-slice, ...), channel_id=1, replica_groups=mesh['dp'=2,'fsdp'=16] {'fsdp'}, use_global_device_ids=true, to_apply=%add.1 | all-reduce | flops 4096 | bytes 16384
  53.6 17.7 %all-gather = bf16[16,1,256]{2,1,0:T(2,128)(2,1)S(1)} all-gather(bf16[1,1,256]{2,1,0:T(2,128)(2,1)S(1)} %reshape.823), channel_id=1, replica_groups=mesh['dp'=2,'fsdp'=16] {'fsdp'}, dimensions={0}, use_global_device_ids=true | all-gather | bytes 8704 | tf_op jit(solution)/shard_map/all_gather | solution.py:102
  72.9 21.5 %all_gather.41 = bf16[256,1024]{1,0:T(8,128)(2,1)S(1)} all-gather(bf16[16,1024]{1,0:T(8,128)(2,1)S(1)} %copy-done.9), channel_id=1, replica_groups=mesh['dp'=2,'fsdp'=16] {'fsdp'}, dimensions={0}, use_global_device_ids=true | all-gather | bytes 557056 | tf_op jit(solution)/shard_map/all_gather | solution.py:92
  94.6 8.6 %copy.59 = bf16[3072,1024]{1,0:T(8,128)(2,1)} copy(bf16[3072,1024]{0,1:T(8,128)(2,1)} %bitcast.284) | data formatting | bytes 12582912 | tf_op jit(solution)/shard_map/dot_general | solution.py:114
  103.2 6.4 convolution_bitcast_fusion.1
  112.3 2.5 fusion.89
  114.8 39.9 %while.28 = (s32[]{:T(128)}, bf16[8,1,512,2,64]{2,4,3,1,0:T(8,128)(2,1)}, f32[8,1,2,512]{3,2,1,0:T(2,128)S(1)}, bf16[8,1,512,2,64]{2,4,3,1,0:T(8,128)(2,1)}, bf1...) while((s32[]{:T(128)}, ...), condition=%wide.region_5.6_spmd.clone, body=%wide.region_2.5_spmd.clone.sunk | while | flops 140574208 | bytes 6852709 | solution.py:144
  117.5 2.3 fusion.159
  122.5 2.3 fusion.159
  127.5 2.3 fusion.159
  132.5 2.3 fusion.159
  137.4 2.3 fusion.159
  142.4 2.3 fusion.159
  147.4 2.3 fusion.159
  152.4 2.3 fusion.159
  154.8 3.3 fusion.122
  158.4 34.5 %all-gather.10.cloned.1.call-done = bf16[1024,4096]{1,0:T(8,128)(2,1)} async-done(((bf16[64,4096]{1,0:T(8,128)(2,1)}), bf16[1024,4096]{1,0:T(8,128)(2,1)}) %all-gather.10.cloned.1.call-update) | async-done | bytes 8388624 | tf_op jit(solution)/shard_map/all_gather | solution.py:101
  192.9 10.3 %fusion.118 = f32[512,4096]{1,0:T(8,128)} fusion(bf16[1024,4096]{1,0:T(8,128)(2,1)} %all-gather.10.cloned.1.call-done, f32[1,512,1024]{2,1,0:T(8,128)S(1)} %get-tuple-element.271, f32[1024]{0:T(1024)S(1)} %convert_element_type.239, f32[1024]{0:T(1024)S(1)} %convert_element_type.238, f32[512]{0:T(512)S(1)} %add_rsqrt_fusion, ...), kind=kOutput, calls=%fused_computation.184 | convolution fusion | flops 4298113024 | bytes 18890752 | tf_op jit(solution)/shard_map/dot_general | solution.py:152
  203.3 64.6 %all-gather.12.cloned.1.call-done = bf16[4096,1024]{1,0:T(8,128)(2,1)} async-done(((bf16[256,1024]{1,0:T(8,128)(2,1)}), bf16[4096,1024]{1,0:T(8,128)(2,1)}) %all-gather.12.cloned.1.call-update) | async-done | bytes 8388624 | tf_op jit(solution)/shard_map/all_gather | solution.py:103
  267.8 14.0 %fusion.123 = (bf16[4096]{0:T(1024)(128)(2,1)S(1)}, bf16[512,4096]{1,0:T(8,128)(2,1)S(1)}) fusion(f32[512,4096]{1,0:T(8,128)} %fusion.118, f32[4096]{0:T(1024)S(1)} %bitcast.298, bf16[4096,1024]{1,0:T(8,128)(2,1)} %all-gather.12.cloned.1.call-done, f32[512]{0:T(512)S(1)} %fusion.109, bf16[1,512,1024]{2,1,0:T(8,128)(2,1)} %param.22), kind=kOutput, calls=%fused_computation.188 | convolution fusion | flops 4342673408 | bytes 22046720 | tf_op jit(solution)/shard_map/dot_general | solution.py:57
  281.9 5.2 fusion.79
  290.6 2.6 convolution_convert_fusion.4
  293.2 4.5 convolution_convert_fusion.5
  297.7 2.3 copy.67
  300.0 82.7 %while.29 = (s32[]{:T(128)}, f32[8,1,512,2,64]{2,4,3,1,0:T(8,128)}, f32[8,1,512,2,64]{2,4,3,1,0:T(8,128)}, bf16[8,1,512,2,64]{2,4,3,1,0:T(8,128)(2,1)}, bf16[8,1...) while((s32[]{:T(128)}, f32[8,1,512,2,64]{2,4,3,1,0:T(8,128)}, ...), condition=%wide.region_12.13_spmd.clone, body=%wide.region_10.12_spmd.clone.sunk | while | flops 340393472 | bytes 17459324 | solution.py:223
  306.5 2.1 fusion.169
  316.8 2.1 fusion.169
  327.2 2.1 fusion.169
  337.5 2.0 fusion.169
  347.8 2.1 fusion.169
  358.1 2.0 fusion.169
  368.4 2.0 fusion.169
  378.7 2.0 fusion.169
  382.7 2.9 broadcast_multiply_fusion.1
  390.9 2.0 pad_maximum_fusion
  392.9 6.1 convolution_convert_fusion.3
  399.0 9.2 %convolution_convert_fusion.2 = bf16[1024,4096]{1,0:T(8,128)(2,1)} fusion(bf16[512,4096]{1,0:T(8,128)(2,1)} %copy-done.14, f32[1,512,1024]{2,1,0:T(8,128)S(1)} %get-tuple-element.271, f32[1024]{0:T(1024)S(1)} %convert_element_type.239, f32[1024]{0:T(1024)S(1)} %convert_element_type.238, f32[512]{0:T(512)S(1)} %add_rsqrt_fusion, ...), kind=kOutput, calls=%fused_computation.69 | convolution fusion | flops 4302307328 | bytes 14696448 | tf_op jit(solution)/shard_map/dot_general | solution.py:51
  408.5 14.1 %convolution_convert_fusion.1 = bf16[4096,1024]{1,0:T(8,128)(2,1)} fusion(bf16[1,512,1024]{2,1,0:T(8,128)(2,1)} %param.22, f32[512]{0:T(512)S(1)} %fusion.109, f32[512,4096]{1,0:T(8,128)} %fusion.118, f32[4096]{0:T(1024)S(1)} %bitcast.299), kind=kOutput, calls=%fused_computation.68 | convolution fusion | flops 4321705984 | bytes 17844224 | tf_op jit(solution)/shard_map/dot_general | solution.py:51
  426.4 8.2 fusion.69
  436.4 59.8 %all-reduce.11 = (bf16[1024]{0:T(1024)(128)(2,1)S(1)}, bf16[1024]{0:T(1024)(128)(2,1)S(1)}, bf16[1024]{0:T(1024)(128)(2,1)S(1)}, bf16[1024]{0:T(1024)(128)(2,1)S...) all-reduce(bf16[1024]{0:T(1024)(128)(2,1)S(1)} %dynamic-update-slic, ...), channel_id=1, replica_groups=mesh['dp'=2,'fsdp'=16] {'fsdp'}, use_global_device_ids=true, to_apply=%add.4 | all-reduce | flops 10240 | bytes 40960
  497.9 4.4 fusion.68
  502.4 87.5 %reduce-scatter.12.cloned.1.call-done = bf16[64,4096]{1,0:T(8,128)(2,1)} async-done(((bf16[1024,4096]{1,0:T(8,128)(2,1)}), bf16[64,4096]{1,0:T(8,128)(2,1)}) %reduce-scatter.12.cloned.1.call-update) | async-done | bytes 524304 | tf_op jit(solution)/shard_map/reduce_scatter | solution.py:274
  589.9 107.2 %reduce-scatter.14.cloned.1.call-done = bf16[256,1024]{1,0:T(8,128)(2,1)} async-done(((bf16[4096,1024]{1,0:T(8,128)(2,1)}), bf16[256,1024]{1,0:T(8,128)(2,1)}) %reduce-scatter.14.cloned.1.call-update) | async-done | bytes 524304 | tf_op jit(solution)/shard_map/reduce_scatter | solution.py:280
  697.1 12.2 %fusion.84 = bf16[1,512,1024]{2,1,0:T(8,128)(2,1)} fusion(f32[1,512,1024]{2,1,0:T(8,128)S(1)} %get-tuple-element.271, bf16[4096,1024]{1,0:T(8,128)(2,1)} %all-gather.12.cloned.1.call-done, f32[1024]{0:T(1024)S(1)} %convert_element_type.243, f32[512,4096]{1,0:T(8,128)} %fusion.118, f32[4096]{0:T(1024)S(1)} %bitcast.300), kind=kOutput, calls=%fused_computation.120 | convolution fusion | flops 4317511680 | bytes 19943424 | tf_op jit(solution)/shard_map/dot_general | solution.py:156
  709.3 47.8 %reduce-scatter.6.cloned.1.call-done = bf16[16,1024]{1,0:T(8,128)(2,1)} async-done(((bf16[256,1024]{1,0:T(8,128)(2,1)}), bf16[16,1024]{1,0:T(8,128)(2,1)}) %reduce-scatter.6.cloned.1.call-update) | async-done | bytes 32784 | tf_op jit(solution)/shard_map/reduce_scatter | solution.py:253
  757.1 9.3 %all-reduce.13 = (bf16[16,1024]{1,0:T(8,128)(2,1)S(1)}, bf16[64]{0:T(256)(128)(2,1)S(1)}, bf16[64]{0:T(256)(128)(2,1)S(1)}, bf16[64]{0:T(256)(128)(2,1)S(1)}, bf...) all-reduce(bf16[16,1024]{1,0:T(8,128)(2,1)} %reduce-scatter.6.clone, ...), channel_id=1, replica_groups=mesh['dp'=2,'fsdp'=16] {'dp'}, use_global_device_ids=true, to_apply=%region_18.19 | all-reduce | flops 16960 | bytes 67840 | tf_op jit(solution)/shard_map/psum | solution.py:290
  770.1 39.9 %all-reduce.17.cloned.1.call-done = (bf16[64,3072]{1,0:T(8,128)(2,1)}, bf16[64,1024]{1,0:T(8,128)(2,1)}, bf16[64,4096]{1,0:T(8,128)(2,1)}, bf16[256,1024]{1,0:T(8,128)(2,1)}) async-done(((bf16[64,3072]{1,0:T(8,128)(2,1)}, bf16[64,1024]{1,0:T(8,128)(2,1)}, bf16[64,4096]{1,0:T(8,128)(2,1)}, bf16[256,1024]{1,0:T(8,128)(2,1)}), (bf16[64,3072]{1,0:T(8,128)(2,1)}, bf16[64,1024]{1,0:T(8,128)(2,1)}, ...) | async-done | bytes 1572880 | tf_op jit(solution)/shard_map/psum | solution.py:293
  813.7 2.1 convert_element_type.270
  (213 shorter events, 123.1 us)
Async XLA Ops:
  7.2 65.0 %copy-start.2 = (bf16[1,512,1024]{2,1,0:T(8,128)(2,1)S(1)}, bf16[1,512,1024]{2,1,0:T(8,128)(2,1)}, u32[]{:S(2)}) copy-start(bf16[1,512,1024]{2,1,0:T(8,128)(2,1)} %param.19) | copy-start | bytes 3145732
  7.2 65.7 %copy-start.9 = (bf16[16,1024]{1,0:T(8,128)(2,1)S(1)}, bf16[16,1024]{1,0:T(8,128)(2,1)}, u32[]{:S(2)}) copy-start(bf16[16,1024]{1,0:T(8,128)(2,1)} %param.23) | copy-start | bytes 98308
  7.2 87.4 %all-gather.6.cloned.1.call-start = ((), (), s32[]{:S(2)}) async-start(), calls=%async_computation.5 | async-start | bytes 6684672 | tf_op jit(solution)/shard_map/all_gather | solution.py:95
  7.9 146.8 %all-gather.8.cloned.1.call-start = ((), (), s32[]{:S(2)}) async-start(), calls=%async_computation.6 | async-start | bytes 2228224 | tf_op jit(solution)/shard_map/all_gather | solution.py:96
  8.7 85.7 %copy-start.10 = (bf16[1,256]{1,0:T(2,128)(2,1)S(1)}, bf16[1,256]{1,0:T(2,128)(2,1)}, u32[]{:S(2)}) copy-start(bf16[1,256]{1,0:T(2,128)(2,1)} %param.21) | copy-start | bytes 1540
  8.7 184.2 %all-gather.10.cloned.1.call-start = ((), (), s32[]{:S(2)}) async-start(), calls=%async_computation.7 | async-start | bytes 8912896 | tf_op jit(solution)/shard_map/all_gather | solution.py:101
  9.4 258.4 %all-gather.12.cloned.1.call-start = ((), (), s32[]{:S(2)}) async-start(), calls=%async_computation.8 | async-start | bytes 8912896 | tf_op jit(solution)/shard_map/all_gather | solution.py:103
  10.0 492.3 %reduce-scatter.10.cloned.1.call-start = ((), (), s32[]{:S(2)}) async-start(), calls=%async_computation.11 | async-start | bytes 2228224 | tf_op jit(solution)/shard_map/reduce_scatter | solution.py:265
  267.8 14.1 %copy-start.12 = (bf16[1024,4096]{1,0:T(8,128)(2,1)S(1)}, bf16[1024,4096]{1,0:T(8,128)(2,1)}, u32[]{:S(2)}) copy-start(bf16[1024,4096]{1,0:T(8,128)(2,1)} %all-gather.10.cloned.1.call-done) | copy-start | bytes 25165828
  281.9 5.2 copy-start.14
  287.1 1.2 copy-start.5
  288.4 2.2 copy-start.6
  289.3 1.3 copy-start.4
  300.0 202.4 %reduce-scatter.8.cloned.1.call-start = ((), (), s32[]{:S(2)}) async-start(), calls=%async_computation.10 | async-start | bytes 6684672 | tf_op jit(solution)/shard_map/reduce_scatter | solution.py:262
  386.2 1.6 copy-start
  386.2 2.2 copy-start.1
  389.6 1.2 copy-start.7
  399.0 190.9 %reduce-scatter.12.cloned.1.call-start = ((), (), s32[]{:S(2)}) async-start(), calls=%async_computation.12 | async-start | bytes 8912896 | tf_op jit(solution)/shard_map/reduce_scatter | solution.py:274
  408.3 288.8 %reduce-scatter.14.cloned.1.call-start = ((), (), s32[]{:S(2)}) async-start(), calls=%async_computation.13 | async-start | bytes 8912896 | tf_op jit(solution)/shard_map/reduce_scatter | solution.py:280
  422.7 0.7 copy-start.11
  422.7 2.0 copy-start.13
  422.7 334.4 %reduce-scatter.6.cloned.1.call-start = ((), (), s32[]{:S(2)}) async-start(), calls=%async_computation.9 | async-start | bytes 557056 | tf_op jit(solution)/shard_map/reduce_scatter | solution.py:253
  434.7 1.4 copy-start.3
  497.6 312.5 %all-reduce.17.cloned.1.call-start = ((), (), s32[]{:S(2)}) async-start(), calls=%async_computation.14 | async-start | bytes 3145728 | tf_op jit(solution)/shard_map/psum | solution.py:293
  810.1 5.7 copy-start.8
Sparse Core Ops, SparseCore 0:
  10.3 64.5 all-gather.5
  77.0 40.6 all-gather.7
  119.9 73.0 all-gather.9
  194.9 72.8 all-gather.11
  300.1 60.3 reduce-scatter.9
  399.1 84.4 reduce-scatter.7
  487.6 102.2 reduce-scatter.11
  594.0 103.0 reduce-scatter.13
  701.2 55.8 reduce-scatter.5
  759.4 50.5 all-reduce.16
where the time goes:
time: 828 us; the launch traced here: 824 us
  waiting for transfers between devices  384 us (46%)
  matrix products  199 us (24%)
  blocking collectives  146 us (18%)
  other arithmetic  51.5 us (6%)
  local copies, waits for them, and re-layouts  24.6 us (3%)
  between operations  17.5 us (2%)
    reduce_scatter x1, waiting for transfers between devices, per_device(): lax.psum_scatter(down_weight_grad.astype(jnp.bfloat16), 'fsdp', scatter_d...  107 us
    unnamed x2, blocking collectives  97.1 us
    reduce_scatter x1, waiting for transfers between devices, per_device(): lax.psum_scatter(up_weight_grad.astype(jnp.bfloat16), 'fsdp', scatter_dim...  87.5 us
    all_gather x1, waiting for transfers between devices, per_device(): lax.all_gather(down_weight, 'fsdp', axis=0, tiled=True)  64.6 us
    reduce_scatter x1, waiting for transfers between devices, per_device(): lax.psum_scatter(time_weight_grad.astype(jnp.bfloat16), 'fsdp', scatter_d...  47.8 us
    psum x1, waiting for transfers between devices, per_device(): lax.psum(attn_parts[3].astype(jnp.bfloat16), 'dp').astype(jnp.float32)  39.9 us
    all_gather x1, waiting for transfers between devices, per_device(): lax.all_gather(up_weight, 'fsdp', axis=0, tiled=True)  34.5 us
    dot_general x4, matrix products, rows_dot(): lax.dot_general(left, right, (((0,), (0,)), ((), ())), preferred_element_...  32 us
  transfers between devices with their start and end apart: 10, of which 6 were waited for; matrix products, arithmetic and copies ran while one was open for 28% of the time, Pallas kernels for 0%

commit v1 on v0

v1 whole, which is shorter than its diff:
```python
import functools
import math

import jax
import jax.numpy as jnp
from jax import lax
from jax.experimental import pallas as pl
from jax.experimental.pallas import tpu as pltpu
from jax.sharding import PartitionSpec as P

HEADS = 16
HD = 64
ZN = 4
F32 = jnp.float32
BF16 = jnp.bfloat16


def normalize(values_in):
    center = values_in - jnp.mean(values_in, axis=-1, keepdims=True)
    inverse = lax.rsqrt(jnp.mean(center * center, axis=-1, keepdims=True) + 1e-05)
    return (center * inverse, inverse)


def norm_back(grad_hat, normed, inverse):
    return inverse * (
        grad_hat
        - jnp.mean(grad_hat, axis=-1, keepdims=True)
        - normed * jnp.mean(grad_hat * normed, axis=-1, keepdims=True)
    )


def rotary_tables(length, head_size):
    half_size = head_size // 2
    frequency = jnp.exp(
        jnp.arange(half_size, dtype=F32) * (-2.0 * math.log(10000.0) / head_size)
    )
    angles = jnp.arange(length, dtype=F32)[:, None] * frequency[None, :]
    angles = jnp.concatenate([angles, angles], axis=-1)
    return (jnp.cos(angles)[:, None, :], jnp.sin(angles)[:, None, :])


def rotate(values_in, cosine_table, sine_table):
    half_size = values_in.shape[-1] // 2
    turned = jnp.concatenate([-values_in[..., half_size:], values_in[..., :half_size]], axis=-1)
    return values_in * cosine_table + turned * sine_table


def rotate_back(grad_in, cosine_table, sine_table):
    half_size = grad_in.shape[-1] // 2
    sined = grad_in * sine_table
    return grad_in * cosine_table + jnp.concatenate(
        [sined[..., half_size:], -sined[..., :half_size]], axis=-1
    )


def rows_dot(left, right):
    return lax.dot_general(
        left, right, (((0,), (0,)), ((), ())), preferred_element_type=F32
    )


def back_dot(grad_in, weight):
    return lax.dot_general(
        grad_in, weight, (((1,), (1,)), ((), ())), preferred_element_type=F32
    )


class Net:
    def __init__(self, dp, fs):
        self.dp, self.fs = dp, fs
        self.yn = fs // (2 * ZN)
        index = lax.axis_index("fsdp")
        self.me = index
        self.z0 = index // (2 * self.yn)
        self.y0 = (index // 2) % self.yn
        self.c0 = index % 2
        self.p0 = lax.axis_index("dp") % 2

    def place(self, z, y, c):
        return ((z % ZN) * self.yn + y % self.yn) * 2 + c % 2

    def split(self, i):
        return i // (2 * self.yn), (i // 2) % self.yn, i % 2

    def perm(self, values_in, dz, dy, dc):
        pairs = []
        for i in range(self.fs):
            z, y, c = self.split(i)
            pairs.append((i, self.place(z + dz, y + dy, c + dc)))
        return lax.ppermute(values_in, "fsdp", pairs)

    def z(self, values_in, k):
        return self.perm(values_in, k, 0, 0)

    def y(self, values_in, s):
        return self.perm(values_in, 0, s, 0)

    def c(self, values_in):
        return self.perm(values_in, 0, 0, 1)

    def x(self, values_in):
        return lax.ppermute(values_in, "dp", [(i, i ^ 1) for i in range(self.dp)])


def assemble_kernel(plan, rows, half, yn, where_ref, *refs):
    pieces, out_ref, held, sems, out_sem = refs[: len(plan)], refs[-4], refs[-3], refs[-2], refs[-1]
    z0, y0, c0, p0 = where_ref[0], where_ref[1], where_ref[2], where_ref[3]
    copies = []
    for piece_ref, (s, q, cq, first, count) in zip(pieces, plan):
        y = lax.rem(y0 + yn - s, yn)
        p = lax.rem(p0 + q, 2)
        c = lax.rem(c0 + cq, 2)
        for k in range(count):
            z = lax.rem(z0 + ZN - (first + k), ZN)
            start = pl.multiple_of(((z * yn + y) * 2 + c) * rows + p * half, half)
            copies.append(
                pltpu.make_async_copy(
                    piece_ref.at[pl.ds(k * half, half), :],
                    held.at[pl.ds(start, half), :],
                    sems.at[len(copies)],
                )
            )
    for copy in copies:
        copy.start()
    for copy in copies:
        copy.wait()
    back = pltpu.make_async_copy(held, out_ref, out_sem)
    back.start()
    back.wait()


def assemble(net, plan, pieces, rows, columns):
    half = rows // 2
    where = jnp.stack([net.z0, net.y0, net.c0, net.p0]).astype(jnp.int32)
    blocks = sum(entry[4] for entry in plan)
    total = net.fs * rows
    return pl.pallas_call(
        functools.partial(assemble_kernel, plan, rows, half, net.yn),
        out_shape=jax.ShapeDtypeStruct((total, columns), BF16),
        grid_spec=pltpu.PrefetchScalarGridSpec(
            num_scalar_prefetch=1,
            grid=(1,),
            in_specs=[pl.BlockSpec(memory_space=pl.ANY)] * len(pieces),
            out_specs=pl.BlockSpec(memory_space=pl.ANY),
            scratch_shapes=[
                pltpu.VMEM((total, columns), BF16),
                pltpu.SemaphoreType.DMA((blocks,)),
                pltpu.SemaphoreType.DMA,
            ],
        ),
        compiler_params=pltpu.CompilerParams(vmem_limit_bytes=24 * 2**20),
        cost_estimate=pl.CostEstimate(
            flops=0, bytes_accessed=4 * total * columns, transcendentals=0
        ),
        name="assemble",
    )(where, *pieces)


def gather_weight(net, shard):
    rows, columns = shard.shape
    half = rows // 2
    own = lax.dynamic_slice_in_dim(shard, net.p0 * half, half, 0)
    line = jnp.concatenate([own] + [net.z(own, k) for k in range(1, ZN)], axis=0)
    across = net.x(line)
    beside = [net.y(line, s) for s in range(1, net.yn)]
    mid = (ZN // 2) * half
    corner_one = [net.x(item[:mid]) for item in beside]
    corner_two = [net.y(across[mid:], s) for s in range(1, net.yn)]
    plan = [(0, 0, 0, ZN), (0, 1, 0, ZN)]
    pieces = [line, across]
    for s in range(1, net.yn):
        plan += [(s, 0, 0, ZN), (s, 1, 0, ZN // 2), (s, 1, ZN // 2, ZN - ZN // 2)]
        pieces += [beside[s - 1], corner_one[s - 1], corner_two[s - 1]]
    full_plan = [(s, q, 0, first, count) for s, q, first, count in plan]
    full_plan += [(s, q, 1, first, count) for s, q, first, count in plan]
    return assemble(net, full_plan, pieces + [net.c(item) for item in pieces], rows, columns)


def gather_small(net, shard):
    rows, columns = shard.shape
    line = jnp.stack([shard] + [net.z(shard, k) for k in range(1, ZN)])
    sides = jnp.stack([line] + [net.y(line, s) for s in range(1, net.yn)], axis=1)
    both = jnp.stack([sides, net.c(sides)], axis=2)
    z_order = (net.z0 - jnp.arange(ZN)) % ZN
    y_order = (net.y0 - jnp.arange(net.yn)) % net.yn
    c_order = (net.c0 - jnp.arange(2)) % 2
    both = both[z_order][:, y_order][:, :, c_order]
    return both.reshape(net.fs, rows, columns)


def relative_order(net, rows, total):
    half = rows // 2
    d = jnp.arange(total, dtype=jnp.int32)
    f, i = d // rows, d % rows
    z, y, c = f // (2 * net.yn), (f // 2) % net.yn, f % 2
    p, j = i // half, i % half
    c, y, p, z = (c - net.c0) % 2, (y - net.y0) % net.yn, (p - net.p0) % 2, (z - net.z0) % ZN
    return (((c * net.yn + y) * 2 + p) * ZN + z) * half + j


def scatter_grad(net, keep, send, rows):
    half = rows // 2
    sent = net.c(send().astype(BF16))
    columns = sent.shape[1]
    total = (keep() + sent.astype(F32)).astype(BF16)
    blocks = total.reshape(net.yn, 2, ZN, half, columns)
    mid = ZN // 2
    zero_other, own = blocks[0, 1], blocks[0, 0].astype(F32)
    side = []
    for s in range(1, net.yn):
        came_x = net.x(blocks[s, 1, :mid])
        came_y = net.y(blocks[s, 1, mid:], s)
        head = (blocks[s, 0, :mid].astype(F32) + came_x.astype(F32)).astype(BF16)
        side.append(jnp.concatenate([head, blocks[s, 0, mid:]], axis=0))
        tail = (zero_other[mid:].astype(F32) + came_y.astype(F32)).astype(BF16)
        zero_other = jnp.concatenate([zero_other[:mid], tail], axis=0)
    own = own + net.x(zero_other).astype(F32)
    for s in range(1, net.yn):
        own = own + net.y(side[s - 1], s).astype(F32)
    own = own.astype(BF16)
    mine = own[0].astype(F32)
    for k in range(1, ZN):
        mine = mine + net.z(own[k], k).astype(F32)
    mine = mine.astype(BF16)
    if net.dp > 2:
        groups = [list(range(q, net.dp, 2)) for q in range(2)]
        mine = lax.psum(mine, "dp", axis_index_groups=groups)
    other = net.x(mine)
    first = jnp.where(net.p0 == 0, mine, other)
    second = jnp.where(net.p0 == 0, other, mine)
    return jnp.concatenate([first, second], axis=0).astype(F32)


def reduce_small(net, sums, rows):
    count = sums.shape[0]
    packed = jnp.concatenate([sums, rows], axis=0)
    if net.dp == 2:
        came = net.x(packed)
        low = jnp.where(net.p0 == 0, packed, came)
        high = jnp.where(net.p0 == 0, came, packed)
        packed = jnp.concatenate([low[:count] + high[:count], low[count:], high[count:]], axis=0)
    else:
        packed = jnp.concatenate(
            [lax.psum(sums, "dp"), lax.all_gather(rows, "dp", axis=0, tiled=True)], axis=0
        )

    def join(came_all):
        total = came_all[0][:count]
        for item in came_all[1:]:
            total = total + item[:count]
        return jnp.concatenate([total] + [item[count:] for item in came_all], axis=0)

    packed = join([packed, net.c(packed)])
    packed = join([packed] + [net.y(packed, s) for s in range(1, net.yn)])
    packed = join([packed] + [net.z(packed, k) for k in range(1, ZN)])
    return packed[:count], packed[count:]


def rows_kernel(order_ref, *refs):
    grad_ref, out_ref = refs[-2], refs[-1]
    for i, left_ref in enumerate(refs[:-2]):
        size = left_ref.shape[1]
        out_ref[i * size : (i + 1) * size, :] = lax.dot_general(
            left_ref[...], grad_ref[...], (((0,), (0,)), ((), ())), preferred_element_type=F32
        ).astype(BF16)


def rows_by_block(order, left, grad, block, per_step):
    depth, columns = grad.shape
    count = order.shape[0]

    def pick(j):
        return lambda i, order_ref: (0, order_ref[i * per_step + j])

    return pl.pallas_call(
        rows_kernel,
        out_shape=jax.ShapeDtypeStruct((count * block, columns), BF16),
        grid_spec=pltpu.PrefetchScalarGridSpec(
            num_scalar_prefetch=1,
            grid=(count // per_step,),
            in_specs=[pl.BlockSpec((depth, block), pick(j)) for j in range(per_step)]
            + [pl.BlockSpec((depth, columns), lambda i, order_ref: (0, 0))],
            out_specs=pl.BlockSpec((per_step * block, columns), lambda i, order_ref: (i, 0)),
        ),
        cost_estimate=pl.CostEstimate(
            flops=2 * depth * count * block * columns,
            bytes_accessed=2 * (depth * columns + count * block * (columns + depth)),
            transcendentals=0,
        ),
        name="rows_by_block",
    )(order, *([left] * per_step), grad)


def scores_of(query_pair, key_pair, key_mask, factor):
    raw_scores = (
        jnp.einsum("bqgd,bkgd->bgqk", query_pair, key_pair, preferred_element_type=F32)
        * factor
    )
    return jnp.where(key_mask[:, None, None, :], raw_scores, -1000000000.0)


def per_device(
    dp,
    fs,
    tokens,
    lengths,
    time_embed,
    cotangent,
    time_weight,
    attn_gain,
    attn_shift,
    qkv_weight,
    out_weight,
    mlp_gain,
    mlp_shift,
    up_weight,
    up_bias,
    down_weight,
    down_bias,
):
    net = Net(dp, fs)
    seq_count, length, features = tokens.shape
    flat_rows = seq_count * length
    pair_count = HEADS // 2
    factor = HD ** (-0.5)
    width = features
    vectors = [attn_gain, attn_shift, mlp_gain, mlp_shift, down_bias, up_bias]
    edges = [0]
    for item in vectors:
        edges.append(edges[-1] + item.shape[0])
    lanes = -(-edges[-1] // width) * width
    strip = jnp.concatenate(vectors + [jnp.zeros((lanes - edges[-1],), BF16)])
    small = jnp.concatenate([time_weight, strip.reshape(-1, width)], axis=0)
    pad = -small.shape[0] % 16
    small = jnp.concatenate([small, jnp.zeros((pad, width), BF16)], axis=0)
    small_full = gather_small(net, small)
    te_rows = time_weight.shape[0]
    time_full = small_full[:, :te_rows].reshape(fs * te_rows, width)
    strips = small_full[:, te_rows : te_rows + lanes // width].reshape(fs, lanes)
    gain_one, shift_one, gain_two, shift_two, down_bias_full, up_bias_full = (
        strips[:, a:b].reshape(-1).astype(F32) for a, b in zip(edges[:-1], edges[1:])
    )
    qkv_full = gather_weight(net, qkv_weight)
    out_full = gather_weight(net, out_weight)
    up_full = gather_weight(net, up_weight)
    down_full = gather_weight(net, down_weight)

    wide_rows = qkv_weight.shape[0]
    order = relative_order(net, wide_rows, features)
    permute = (order[:, None] == jnp.arange(features, dtype=jnp.int32)[None, :]).astype(BF16)

    def reorder(values_in):
        return jnp.dot(values_in, permute, preferred_element_type=F32).astype(BF16)

    key_mask = jnp.arange(length, dtype=jnp.int32)[None, :] < lengths[:, None]
    residual = tokens.astype(F32)
    time_scale = (
        1.0 + jnp.dot(time_embed, time_full, preferred_element_type=F32)[:, None, :]
    )
    normed_one, inverse_one = normalize(residual)
    affine_one = normed_one * gain_one + shift_one
    attn_in = (affine_one * time_scale).astype(BF16).reshape(flat_rows, features)
    qkv = jnp.dot(attn_in, qkv_full, preferred_element_type=F32).reshape(
        seq_count, length, 3, HEADS, HD
    )
    cosine_table, sine_table = rotary_tables(length, HD)
    query_rows = rotate(qkv[:, :, 0], cosine_table, sine_table).astype(BF16)
    key_rows = rotate(qkv[:, :, 1], cosine_table, sine_table).astype(BF16)
    value_rows = qkv[:, :, 2].astype(BF16)

    def by_pairs(values_in):
        return values_in.reshape(seq_count, length, pair_count, 2, HD).transpose(2, 0, 1, 3, 4)

    def from_pairs(values_in):
        return values_in.transpose(1, 2, 0, 3, 4).reshape(seq_count, length, features)

    query_group = by_pairs(query_rows)
    key_group = by_pairs(key_rows)
    value_group = by_pairs(value_rows)

    def attend(operands):
        query_pair, key_pair, value_pair = operands
        scores = scores_of(query_pair, key_pair, key_mask, factor)
        row_max = jnp.max(scores, axis=-1, keepdims=True)
        exponent = jnp.exp(scores - row_max)
        row_total = jnp.sum(exponent, axis=-1, keepdims=True)
        attn_probs = (exponent / row_total).astype(BF16)
        mixed_rows = jnp.einsum(
            "bgqk,bkgd->bqgd", attn_probs, value_pair, preferred_element_type=F32
        )
        return (mixed_rows.astype(BF16), (row_max + jnp.log(row_total))[..., 0])

    context_group, log_totals = lax.map(attend, (query_group, key_group, value_group))
    context = from_pairs(context_group).reshape(flat_rows, features)
    hidden = residual + jnp.dot(context, out_full, preferred_element_type=F32).reshape(
        seq_count, length, features
    )
    normed_two, inverse_two = normalize(hidden)
    affine_two = normed_two * gain_two + shift_two
    mlp_in = (affine_two * time_scale).astype(BF16).reshape(flat_rows, features)
    pre_act = jnp.dot(mlp_in, up_full, preferred_element_type=F32) + up_bias_full
    active = jax.nn.gelu(pre_act).astype(BF16)
    branch_out = jnp.dot(active, down_full, preferred_element_type=F32) + down_bias_full
    layer_out = (hidden + branch_out.reshape(seq_count, length, features)).astype(BF16)

    grad_out = cotangent.astype(F32) * key_mask[:, :, None].astype(F32)
    grad_branch = grad_out.astype(BF16).reshape(flat_rows, features)
    tall_rows = down_weight.shape[0]
    tall_half = tall_rows // 2
    spots = relative_order(net, tall_rows, fs * tall_rows)[::tall_half] // tall_half
    block_order = jnp.argsort(spots).astype(jnp.int32)

    def tall_grad(first, last):
        if tall_half % 128 == 0:
            return rows_by_block(block_order[first:last], active, grad_branch, tall_half, 2)
        whole = rows_dot(active, grad_branch).astype(BF16)
        picked = whole.reshape(-1, tall_half, features)[block_order[first:last]]
        return picked.reshape(-1, features)

    down_weight_grad = scatter_grad(
        net,
        lambda: tall_grad(0, fs).astype(F32),
        lambda: tall_grad(fs, 2 * fs),
        tall_rows,
    )
    down_bias_grad = jnp.sum(grad_branch.astype(F32), axis=0)
    grad_active = back_dot(grad_branch, down_full)
    gelu_value, gelu_pull = jax.vjp(jax.nn.gelu, pre_act)
    grad_pre = gelu_pull(grad_active)[0].astype(BF16)
    up_bias_grad = jnp.sum(grad_pre.astype(F32), axis=0)

    def wide_grad(left, right):
        moved = reorder(left)
        half_width = features // 2
        return scatter_grad(
            net,
            lambda: rows_dot(moved[:, :half_width], right),
            lambda: rows_dot(moved[:, half_width:], right),
            wide_rows,
        )

    up_weight_grad = wide_grad(mlp_in, grad_pre)
    grad_mlp_in = back_dot(grad_pre, up_full).reshape(seq_count, length, features)
    grad_affine_two = grad_mlp_in * time_scale
    grad_scale = jnp.sum(grad_mlp_in * affine_two, axis=1)
    mlp_gain_grad = jnp.sum(grad_affine_two * normed_two, axis=(0, 1))
    mlp_shift_grad = jnp.sum(grad_affine_two, axis=(0, 1))
    grad_hidden = grad_out + norm_back(grad_affine_two * gain_two, normed_two, inverse_two)
    grad_attn = grad_hidden.astype(BF16).reshape(flat_rows, features)
    out_weight_grad = wide_grad(context, grad_attn)
    grad_context = back_dot(grad_attn, out_full).astype(BF16)

    def attend_back(operands):
        query_pair, key_pair, value_pair, log_pair, grad_pair = operands
        scores = scores_of(query_pair, key_pair, key_mask, factor)
        probs_full = jnp.exp(scores - log_pair[..., None])
        attn_probs = probs_full.astype(BF16)
        grad_value = jnp.einsum(
            "bgqk,bqgd->bkgd", attn_probs, grad_pair, preferred_element_type=F32
        )
        grad_probs = jnp.einsum(
            "bqgd,bkgd->bgqk", grad_pair, value_pair, preferred_element_type=F32
        )
        grad_scores = probs_full * (
            grad_probs - jnp.sum(grad_probs * probs_full, axis=-1, keepdims=True)
        )
        grad_scores = grad_scores.astype(BF16)
        grad_query = (
            jnp.einsum("bgqk,bkgd->bqgd", grad_scores, key_pair, preferred_element_type=F32)
            * factor
        )
        grad_key = (
            jnp.einsum("bgqk,bqgd->bkgd", grad_scores, query_pair, preferred_element_type=F32)
            * factor
        )
        return (grad_query, grad_key, grad_value)

    grad_query_group, grad_key_group, grad_value_group = lax.map(
        attend_back, (query_group, key_group, value_group, log_totals, by_pairs(grad_context))
    )
    head_shape = (seq_count, length, HEADS, HD)
    grad_query_raw = rotate_back(
        from_pairs(grad_query_group).reshape(head_shape), cosine_table, sine_table
    )
    grad_key_raw = rotate_back(
        from_pairs(grad_key_group).reshape(head_shape), cosine_table, sine_table
    )
    grad_value_raw = from_pairs(grad_value_group).reshape(head_shape)
    grad_qkv = (
        jnp.stack([grad_query_raw, grad_key_raw, grad_value_raw], axis=2)
        .astype(BF16)
        .reshape(flat_rows, 3 * features)
    )
    qkv_weight_grad = wide_grad(attn_in, grad_qkv)
    grad_attn_in = back_dot(grad_qkv, qkv_full).reshape(seq_count, length, features)
    grad_affine_one = grad_attn_in * time_scale
    grad_scale = grad_scale + jnp.sum(grad_attn_in * affine_one, axis=1)
    attn_gain_grad = jnp.sum(grad_affine_one * normed_one, axis=(0, 1))
    attn_shift_grad = jnp.sum(grad_affine_one, axis=(0, 1))
    token_grad = (
        grad_hidden + norm_back(grad_affine_one * gain_one, normed_one, inverse_one)
    ).astype(BF16)

    sums = [attn_gain_grad, attn_shift_grad, mlp_gain_grad, mlp_shift_grad, down_bias_grad]
    embed = time_embed.shape[1]
    wide = jnp.concatenate(
        [jnp.stack(sums), up_bias_grad.reshape(-1, features)], axis=0
    )
    wide = jnp.concatenate([wide, jnp.zeros((wide.shape[0], embed), F32)], axis=1)
    row = jnp.concatenate([grad_scale, time_embed.astype(F32)], axis=1)
    totals, collected = reduce_small(net, wide, row)
    totals = totals[:, :features]
    vector_grads = [
        lax.dynamic_slice_in_dim(totals[i], net.me * attn_gain.shape[0], attn_gain.shape[0])
        for i in range(5)
    ]
    up_bias_out = lax.dynamic_slice_in_dim(
        totals[5:].reshape(-1), net.me * up_bias.shape[0], up_bias.shape[0]
    )
    embeds = lax.dynamic_slice_in_dim(collected[:, features:], net.me * te_rows, te_rows, 1)
    time_weight_grad = lax.dot_general(
        embeds,
        collected[:, :features],
        (((0,), (0,)), ((), ())),
        precision=lax.Precision.HIGHEST,
        preferred_element_type=F32,
    )
    return (
        layer_out,
        token_grad,
        time_weight_grad,
        vector_grads[0],
        vector_grads[1],
        qkv_weight_grad,
        out_weight_grad,
        vector_grads[2],
        vector_grads[3],
        up_weight_grad,
        up_bias_out,
        down_weight_grad,
        vector_grads[4],
    )


def solution(mesh):
    return jax.shard_map(
        functools.partial(per_device, mesh.shape["dp"], mesh.shape["fsdp"]),
        mesh=mesh,
        in_specs=(
            P(("dp", "fsdp"), None, None),
            P(("dp", "fsdp")),
            P(("dp", "fsdp"), None),
            P(("dp", "fsdp"), None, None),
            P("fsdp", None),
            P("fsdp"),
            P("fsdp"),
            P("fsdp", None),
            P("fsdp", None),
            P("fsdp"),
            P("fsdp"),
            P("fsdp", None),
            P("fsdp"),
            P("fsdp", None),
            P("fsdp"),
        ),
        out_specs=(
            P(("dp", "fsdp"), None, None),
            P(("dp", "fsdp"), None, None),
            P("fsdp", None),
            P("fsdp"),
            P("fsdp"),
            P("fsdp", None),
            P("fsdp", None),
            P("fsdp"),
            P("fsdp"),
            P("fsdp", None),
            P("fsdp"),
            P("fsdp", None),
            P("fsdp"),
        ),
        check_vma=False,
    )
```

time: 828 us -> 665 us (0.80)
  waiting for transfers between devices: 384 us -> 169 us
  blocking collectives: 146 us -> 0 us
  starting transfers between devices: 0.86 us -> 125 us
  local copies, waits for them, and re-layouts: 24.6 us -> 63.5 us
  Pallas kernels: 0 us -> 35.6 us
  other arithmetic: 51.5 us -> 68.8 us
  between operations: 17.5 us -> 3.05 us
  matrix products: 199 us -> 188 us
    reduce_scatter x5 -> x0, waiting for transfers between devices: 243 us -> none  [the longest x1 107 us: per_device(): lax.psum_scatter(down_weight_grad.astype(jnp.bfloat16), 'fsdp', scatter_d...]
    ppermute x0 -> x95, waiting for transfers between devices: none -> 169 us  [the longest x21 97.9 us: x(): return lax.ppermute(values_in, 'dp', [(i, i ^ 1) for i in range(self.dp)])]
    ppermute x0 -> x95, starting transfers between devices: none -> 125 us  [the longest x74 102 us: perm(): return lax.ppermute(values_in, 'fsdp', pairs)]
    all_gather x4 -> x0, waiting for transfers between devices: 99.1 us -> none  [the longest x1 64.6 us: per_device(): lax.all_gather(down_weight, 'fsdp', axis=0, tiled=True)]
    unnamed x2 -> x0, blocking collectives: 97.1 us -> none
    psum x1 -> x0, waiting for transfers between devices: 39.9 us -> none  [per_device(): lax.psum(attn_parts[3].astype(jnp.bfloat16), 'dp').astype(jnp.float32)]
    all_gather x2 -> x0, blocking collectives: 39.2 us -> none  [the longest x1 21.5 us: per_device(): lax.all_gather(time_weight, 'fsdp', axis=0, tiled=True)]
    pallas_call x0 -> x6, Pallas kernels: none -> 35.6 us  [the longest x2 18.4 us: rows_by_block(): pl.pallas_call(rows_kernel, out_shape=jax.ShapeDtypeStruct((count * block...]
  transfers between devices with their start and end apart: 10 -> 95, of which waited for: 6 -> 34; matrix products, arithmetic and copies ran while one was open for 28% -> 44% of each run, Pallas kernels for 0% -> 3%
where the time goes in v1:
time: 665 us; the launch traced here: 654 us
  matrix products  188 us (28%)
  waiting for transfers between devices  169 us (25%)
  starting transfers between devices  125 us (19%)
  other arithmetic  68.8 us (10%)
  local copies, waits for them, and re-layouts  63.5 us (10%)
  Pallas kernels  35.6 us (5%)
    ppermute x74, starting transfers between devices, perm(): return lax.ppermute(values_in, 'fsdp', pairs)  102 us
    ppermute x21, waiting for transfers between devices, x(): return lax.ppermute(values_in, 'dp', [(i, i ^ 1) for i in range(self.dp)])  97.9 us
    ppermute x74, waiting for transfers between devices, perm(): return lax.ppermute(values_in, 'fsdp', pairs)  71.4 us
    dot_general x4, matrix products, back_dot(): lax.dot_general(grad_in, weight, (((1,), (1,)), ((), ())), preferred_elem...  34.6 us
    dot_general x16, matrix products, scores_of(): jnp.einsum('bqgd,bkgd->bgqk', query_pair, key_pair, preferred_element_typ...  24.9 us
    ppermute x21, starting transfers between devices, x(): return lax.ppermute(values_in, 'dp', [(i, i ^ 1) for i in range(self.dp)])  23.1 us
    dot_general x6, matrix products, rows_dot(): lax.dot_general(left, right, (((0,), (0,)), ((), ())), preferred_element_...  18.6 us
    pallas_call x2, Pallas kernels, rows_by_block(): pl.pallas_call(rows_kernel, out_shape=jax.ShapeDtypeStruct((count * block...  18.4 us
  transfers between devices with their start and end apart: 95, of which 34 were waited for; matrix products, arithmetic and copies ran while one was open for 44% of the time, Pallas kernels for 3%

profile of v1, /device:TPU:0, one launch (start us, length us, event | category | flops | bytes accessed | tf_op | source)
XLA Modules:
  0.0 654.4 jit_solution(16427174272407864528)
XLA Ops:
  13.5 4.1 concatenate.168
  30.5 4.4 collective-permute-start.2
  38.4 4.1 collective-permute-start.30
  49.0 11.9 %collective-permute-start.42 = (bf16[128,1024]{1,0:T(8,128)(2,1)S(1)}, bf16[128,1024]{1,0:T(8,128)(2,1)S(1)}, u32[]{:S(2)}, u32[]{:S(2)}) collective-permute-start(bf16[128,1024]{1,0:T(8,128)(2,1)S(1)} %constant_dynamic-slice_fusion.5), channel_id=1, source_target_pairs={{0,8},{1,9},{2,10},{3,11},{4,12},{5,13},{6,14},{7,15},{8,0},{9,1},... | collective-permute-start | bytes 786440 | tf_op jit(solution)/shard_map/ppermute | solution.py:90
  63.4 10.4 %collective-permute-start.43 = (bf16[128,1024]{1,0:T(8,128)(2,1)S(1)}, bf16[128,1024]{1,0:T(8,128)(2,1)S(1)}, u32[]{:S(2)}, u32[]{:S(2)}) collective-permute-start(bf16[128,1024]{1,0:T(8,128)(2,1)S(1)} %constant_dynamic-slice_fusion.5), channel_id=1, source_target_pairs={{0,12},{1,13},{2,14},{3,15},{4,0},{5,1},{6,2},{7,3},{8,4},{9,5},{1... | collective-permute-start | bytes 786440 | tf_op jit(solution)/shard_map/ppermute | solution.py:90
  76.8 4.7 collective-permute-done.20.refs_1_
  86.9 14.8 %collective-permute-done.23.refs_4_ = bf16[64,1024]{1,0:T(8,128)(2,1)S(1)} collective-permute-done((bf16[64,1024]{1,0:T(8,128)(2,1)S(1)}, bf16[64,1024]{1,0:T(8,128)(2,1)S(1)}, u32[]{:S(2)}, u32[]{:S(2)}) %collective-permute-start.23) | collective-permute-done | bytes 131104 | tf_op jit(solution)/shard_map/ppermute | solution.py:90
  117.6 4.5 assemble.5
  140.3 8.3 %collective-permute-done.32.refs_1_ = bf16[128,4096]{1,0:T(8,128)(2,1)} collective-permute-done((bf16[128,4096]{1,0:T(8,128)(2,1)}, bf16[128,4096]{1,0:T(8,128)(2,1)}, u32[]{:S(2)}, u32[]{:S(2)}) %collective-permute-start.32) | collective-permute-done | bytes 1048608 | tf_op jit(solution)/shard_map/ppermute | solution.py:102
  149.2 22.0 %collective-permute-done.44.refs_1_ = bf16[512,1024]{1,0:T(8,128)(2,1)} collective-permute-done((bf16[512,1024]{1,0:T(8,128)(2,1)}, bf16[512,1024]{1,0:T(8,128)(2,1)}, u32[]{:S(2)}, u32[]{:S(2)}) %collective-permute-start.44) | collective-permute-done | bytes 1048608 | tf_op jit(solution)/shard_map/ppermute | solution.py:102
  171.2 7.4 %collective-permute-done.10.refs_3_ = bf16[64,3072]{1,0:T(8,128)(2,1)S(1)} collective-permute-done((bf16[64,3072]{1,0:T(8,128)(2,1)S(1)}, bf16[64,3072]{1,0:T(8,128)(2,1)S(1)}, u32[]{:S(2)}, u32[]{:S(2)}) %collective-permute-start.10) | collective-permute-done | bytes 393248 | tf_op jit(solution)/shard_map/ppermute | solution.py:102
  180.0 4.0 fusion.96
  194.2 5.0 assemble.4
  201.8 8.7 %copy.94 = bf16[3072,1024]{1,0:T(8,128)(2,1)} copy(bf16[3072,1024]{0,1:T(8,128)(2,1)} %bitcast.452) | data formatting | bytes 12582912 | tf_op jit(solution)/shard_map/dot_general | solution.py:363
  210.5 6.7 %convolution_bitcast_fusion.1 = f32[1,512,3,16,64]{1,4,3,2,0:T(8,128)S(1)} fusion(bf16[3,16,64,1024]{3,2,1,0:T(8,128)(2,1)} %bitcast.467, bf16[1,512,1024]{2,1,0:T(8,128)(2,1)} %param.19, f32[1024]{0:T(1024)S(1)} %broadcast_add_fusion, f32[1024]{0:T(1024)S(1)} %reshape.1099, f32[1024]{0:T(1024)S(1)} %reshape.1098, f32[512]{0:T(512)S(1)} %add_rsqrt_fusion.1, ...), kind=kOutput, calls=%fused_computation.85 | convolution fusion | flops 3224895488 | bytes 13647872 | tf_op jit(solution)/shard_map/dot_general | solution.py:363
  223.0 44.7 %while.28 = (s32[]{:T(128)}, bf16[8,1,512,2,64]{2,4,3,1,0:T(8,128)(2,1)}, f32[8,1,2,512]{3,2,1,0:T(2,128)}, bf16[8,1,512,2,64]{2,4,3,1,0:T(8,128)(2,1)}, bf16[8,...) while((s32[]{:T(128)}, ...), condition=%wide.region_5.6_spmd.clone, body=%wide.region_2.5_spmd.clone.sunk | while | flops 140574208 | bytes 6853209 | solution.py:393
  271.5 3.7 fusion.97
  280.2 9.0 %collective-permute-done.47.refs_4_ = bf16[256,1024]{1,0:T(8,128)(2,1)S(1)} collective-permute-done((bf16[256,1024]{1,0:T(8,128)(2,1)S(1)}, bf16[256,1024]{1,0:T(8,128)(2,1)S(1)}, u32[]{:S(2)}, u32[]{:S(2)}) %collective-permute-start.47) | collective-permute-done | bytes 524320 | tf_op jit(solution)/shard_map/ppermute | solution.py:90
  290.4 4.2 assemble.6
  294.6 6.8 %fusion.247 = f32[512,4096]{1,0:T(8,128)} fusion(bf16[512,1024]{1,0:T(8,128)(2,1)S(1)} %fusion.99, bf16[1024,4096]{1,0:T(8,128)(2,1)S(1)} %assemble.6), kind=kOutput, calls=%fused_computation.515 | convolution fusion | flops 4294967296 | bytes 17825792 | tf_op jit(solution)/shard_map/dot_general | solution.py:401
  301.4 3.4 assemble.7
  304.9 17.4 %convert_reduce_fusion = (f32[4096]{0:T(1024)S(1)}, bf16[512,4096]{1,0:T(8,128)(2,1)}, bf16[512,4096]{1,0:T(8,128)(2,1)}) fusion(f32[512,4096]{1,0:T(8,128)} %fusion.247, f32[4096]{0:T(1024)S(1)} %bitcast.502, bf16[512,1024]{1,0:T(8,128)(2,1)S(1)} %copy-done.33, bf16[4096,1024]{1,0:T(8,128)(2,1)S(1)} %assemble.7), kind=kOutput, calls=%fused_computation.72 | convolution fusion | flops 4347392000 | bytes 26247168 | tf_op jit(solution)/shard_map/dot_general | solution.py:63
  322.2 9.3 %rows_by_block.3 = bf16[2048,1024]{1,0:T(8,128)(2,1)} custom-call(s32[16]{0:T(128)} %get-tuple-element.328.order_ref, bf16[512,4096]{1,0:T(8,128)(2,1)} %get-tuple-element.244.refs_0_.refs_1_, bf16[512,4096]{1,0:T(8,128)(2,1)} %get-tuple-element.244.refs_0_.refs_1_, bf16[512,1024]{1,0:T(8,128)(2,1)} %get-tuple-element.239.refs_2_), custom_call_target="tpu_custom_call" | custom-call | flops 2147483648 | bytes 7340032 | tf_op jit(solution)/shard_map/rows_by_block/pallas_call | solution.py:275
  332.1 10.5 %fusion.84 = (f32[1024]{0:T(1024)S(1)}, f32[512]{0:T(512)S(1)}, f32[1024]{0:T(1024)S(1)}, f32[512,1024]{1,0:T(8,128)S(1)}) fusion(f32[1,512,1024]{2,1,0:T(8,128)} %copy-done.21, f32[1024]{0:T(1024)S(1)} %reshape.1101, f32[1024]{0:T(1024)S(1)} %reshape.1100, f32[512]{0:T(512)S(1)} %add_rsqrt_fusion, f32[512]{0:T(512)S(1)} %broadcast_multiply_fusion.6, ...), kind=kOutput, calls=%fused_computation.122 | convolution fusion | flops 4301256192 | bytes 16803840 | tf_op jit(solution)/shard_map/dot_general | solution.py:63
  342.6 4.5 convolution_convert_fusion.1
  356.1 82.5 %while.29 = (s32[]{:T(128)}, f32[8,1,512,2,64]{2,4,3,1,0:T(8,128)S(1)}, f32[8,1,512,2,64]{2,4,3,1,0:T(8,128)}, bf16[8,1,512,2,64]{2,4,3,1,0:T(8,128)(2,1)}, bf16...) while((s32[]{:T(128)}, ...), condition=%wide.region_12.13_spmd.clone, body=%wide.region_10.12_spmd.clone.sunk | while | flops 340393472 | bytes 17459316 | solution.py:478
  445.8 4.5 fusion.66
  450.3 3.6 convolution_convert_fusion.2
  456.6 10.3 %fusion.89 = bf16[1,512,1024]{2,1,0:T(8,128)(2,1)} fusion(f32[1,512,1024]{2,1,0:T(8,128)S(1)} %copy-done.23, bf16[512,4096]{1,0:T(8,128)(2,1)} %get-tuple-element.244.refs_0_.refs_1_, bf16[4096,1024]{1,0:T(8,128)(2,1)} %copy-done.3, f32[1024]{0:T(1024)S(1)} %copy-done.58), kind=kOutput, calls=%fused_computation.131 | convolution fusion | flops 4296540160 | bytes 15732736 | tf_op jit(solution)/shard_map/dot_general | solution.py:403
  473.8 3.3 collective-permute-start.58
  477.1 9.1 %rows_by_block.2 = bf16[2048,1024]{1,0:T(8,128)(2,1)} custom-call(s32[16]{0:T(128)} %get-tuple-element.327.order_ref, bf16[512,4096]{1,0:T(8,128)(2,1)} %get-tuple-element.244.refs_0_.refs_1_, bf16[512,4096]{1,0:T(8,128)(2,1)} %get-tuple-element.244.refs_0_.refs_1_, bf16[512,1024]{1,0:T(8,128)(2,1)} %get-tuple-element.239.refs_2_), custom_call_target="tpu_custom_call" | custom-call | flops 2147483648 | bytes 7340032 | tf_op jit(solution)/shard_map/rows_by_block/pallas_call | solution.py:275
  492.0 3.6 collective-permute-done.69
  500.1 4.5 collective-permute-done.70
  513.9 3.7 add_convert_fusion.2
  521.2 7.0 %collective-permute-done.60 = bf16[2,32,3072]{2,1,0:T(8,128)(2,1)S(1)} collective-permute-done((bf16[2,32,3072]{2,1,0:T(8,128)(2,1)S(1)}, bf16[2,32,3072]{2,1,0:T(8,128)(2,1)S(1)}, u32[]{:S(2)}, u32[]{:S(2)}) %collective-permute-start.60) | collective-permute-done | bytes 393248 | tf_op jit(solution)/shard_map/ppermute | solution.py:90
  532.0 4.4 add_convert_fusion
  541.2 8.2 %collective-permute-done.61 = bf16[4,32,3072]{2,1,0:T(8,128)(2,1)} collective-permute-done((bf16[4,32,3072]{2,1,0:T(8,128)(2,1)S(1)}, bf16[4,32,3072]{2,1,0:T(8,128)(2,1)}, u32[]{:S(2)}, u32[]{:S(2)}) %collective-permute-start.61) | collective-permute-done | bytes 786464 | tf_op jit(solution)/shard_map/ppermute | solution.py:102
  557.1 3.6 collective-permute-done.64
  562.2 3.2 collective-permute-done.65
  571.1 4.5 collective-permute-done.78
  575.5 4.6 collective-permute-done.80
  584.4 22.4 %collective-permute-done.88 = bf16[4,128,1024]{2,1,0:T(8,128)(2,1)S(1)} collective-permute-done((bf16[4,128,1024]{2,1,0:T(8,128)(2,1)S(1)}, bf16[4,128,1024]{2,1,0:T(8,128)(2,1)S(1)}, u32[]{:S(2)}, u32[]{:S(2)}) %collective-permute-start.88) | collective-permute-done | bytes 1048608 | tf_op jit(solution)/shard_map/ppermute | solution.py:102
  608.0 3.4 collective-permute-start.92
  612.2 7.6 %collective-permute-done.79 = bf16[4,32,4096]{2,1,0:T(8,128)(2,1)S(1)} collective-permute-done((bf16[4,32,4096]{2,1,0:T(8,128)(2,1)S(1)}, bf16[4,32,4096]{2,1,0:T(8,128)(2,1)S(1)}, u32[]{:S(2)}, u32[]{:S(2)}) %collective-permute-start.79) | collective-permute-done | bytes 1048608 | tf_op jit(solution)/shard_map/ppermute | solution.py:102
  620.3 6.9 %collective-permute-start.82 = (bf16[32,4096]{1,0:T(8,128)(2,1)S(1)}, bf16[32,4096]{1,0:T(8,128)(2,1)S(1)}, u32[]{:S(2)}, u32[]{:S(2)}) collective-permute-start(bf16[32,4096]{1,0:T(8,128)(2,1)S(1)} %get-tuple-element.278), channel_id=1, source_target_pairs={{0,4},{1,5},{2,6},{3,7},{4,8},{5,9},{6,10},{7,11},{8,12},{9,13},{1... | collective-permute-start | bytes 786440 | tf_op jit(solution)/shard_map/ppermute | solution.py:90
  632.8 4.1 collective-permute-done.82
  636.9 7.5 %collective-permute-done.83 = bf16[32,4096]{1,0:T(8,128)(2,1)S(1)} collective-permute-done((bf16[32,4096]{1,0:T(8,128)(2,1)S(1)}, bf16[32,4096]{1,0:T(8,128)(2,1)S(1)}, u32[]{:S(2)}, u32[]{:S(2)}) %collective-permute-start.83) | collective-permute-done | bytes 262176 | tf_op jit(solution)/shard_map/ppermute | solution.py:90
  647.1 5.7 collective-permute-done.85
  (563 shorter events, 325.2 us)
Async XLA Ops:
  1.8 36.6 %collective-permute-start.5 = (bf16[32,3072]{1,0:T(8,128)(2,1)S(1)}, bf16[32,3072]{1,0:T(8,128)(2,1)S(1)}, u32[]{:S(2)}, u32[]{:S(2)}) collective-permute-start(bf16[32,3072]{1,0:T(8,128)(2,1)S(1)} %constant_dynamic-slice_fusion.8), channel_id=1, source_target_pairs={{0,4},{1,5},{2,6},{3,7},{4,8},{5,9},{6,10},{7,11},{8,12},{9,13},{1... | collective-permute-start | bytes 589832 | tf_op jit(solution)/shard_map/ppermute | solution.py:90
  4.9 37.6 %collective-permute-start.6 = (bf16[32,3072]{1,0:T(8,128)(2,1)S(1)}, bf16[32,3072]{1,0:T(8,128)(2,1)S(1)}, u32[]{:S(2)}, u32[]{:S(2)}) collective-permute-start(bf16[32,3072]{1,0:T(8,128)(2,1)S(1)} %constant_dynamic-slice_fusion.8), channel_id=1, source_target_pairs={{0,8},{1,9},{2,10},{3,11},{4,12},{5,13},{6,14},{7,15},{8,0},{9,1},... | collective-permute-start | bytes 589832 | tf_op jit(solution)/shard_map/ppermute | solution.py:90
  25.9 18.6 %collective-permute-start.21 = (bf16[128,1024]{1,0:T(8,128)(2,1)S(1)}, bf16[128,1024]{1,0:T(8,128)(2,1)S(1)}, u32[]{:S(2)}, u32[]{:S(2)}) collective-permute-start(bf16[128,1024]{1,0:T(8,128)(2,1)S(1)} %pad_maximum_fusion.13.refs_0_), channel_id=1, source_target_pairs={{0,2},{1,3},{2,0},{3,1},{4,6},{5,7},{6,4},{7,5},{8,10},{9,11},{10,... | collective-permute-start | bytes 786440 | tf_op jit(solution)/shard_map/ppermute | solution.py:90
  38.4 25.0 %collective-permute-start.30 = (bf16[32,4096]{1,0:T(8,128)(2,1)S(1)}, bf16[32,4096]{1,0:T(8,128)(2,1)S(1)}, u32[]{:S(2)}, u32[]{:S(2)}) collective-permute-start(bf16[32,4096]{1,0:T(8,128)(2,1)S(1)} %constant_dynamic-slice_fusion.6), channel_id=1, source_target_pairs={{0,8},{1,9},{2,10},{3,11},{4,12},{5,13},{6,14},{7,15},{8,0},{9,1},... | collective-permute-start | bytes 786440 | tf_op jit(solution)/shard_map/ppermute | solution.py:90
  42.5 31.2 %collective-permute-start.31 = (bf16[32,4096]{1,0:T(8,128)(2,1)S(1)}, bf16[32,4096]{1,0:T(8,128)(2,1)S(1)}, u32[]{:S(2)}, u32[]{:S(2)}) collective-permute-start(bf16[32,4096]{1,0:T(8,128)(2,1)S(1)} %constant_dynamic-slice_fusion.6), channel_id=1, source_target_pairs={{0,12},{1,13},{2,14},{3,15},{4,0},{5,1},{6,2},{7,3},{8,4},{9,5},{1... | collective-permute-start | bytes 786440 | tf_op jit(solution)/shard_map/ppermute | solution.py:90
  43.6 31.7 %collective-permute-start.41 = (bf16[128,1024]{1,0:T(8,128)(2,1)S(1)}, bf16[128,1024]{1,0:T(8,128)(2,1)S(1)}, u32[]{:S(2)}, u32[]{:S(2)}) collective-permute-start(bf16[128,1024]{1,0:T(8,128)(2,1)S(1)} %constant_dynamic-slice_fusion.5), channel_id=1, source_target_pairs={{0,4},{1,5},{2,6},{3,7},{4,8},{5,9},{6,10},{7,11},{8,12},{9,13},{1... | collective-permute-start | bytes 786440 | tf_op jit(solution)/shard_map/ppermute | solution.py:90
  44.5 30.7 %collective-permute-start.3 = (bf16[4,32,1024]{2,1,0:T(8,128)(2,1)S(1)}, bf16[4,32,1024]{2,1,0:T(8,128)(2,1)S(1)}, u32[]{:S(2)}, u32[]{:S(2)}) collective-permute-start(bf16[4,32,1024]{2,1,0:T(8,128)(2,1)S(1)} %get-tuple-element.304), channel_id=1, source_target_pairs={{0,2},{1,3},{2,0},{3,1},{4,6},{5,7},{6,4},{7,5},{8,10},{9,11},{10,... | collective-permute-start | bytes 786440 | tf_op jit(solution)/shard_map/ppermute | solution.py:90
  49.0 35.0 %collective-permute-start.42 = (bf16[128,1024]{1,0:T(8,128)(2,1)S(1)}, bf16[128,1024]{1,0:T(8,128)(2,1)S(1)}, u32[]{:S(2)}, u32[]{:S(2)}) collective-permute-start(bf16[128,1024]{1,0:T(8,128)(2,1)S(1)} %constant_dynamic-slice_fusion.5), channel_id=1, source_target_pairs={{0,8},{1,9},{2,10},{3,11},{4,12},{5,13},{6,14},{7,15},{8,0},{9,1},... | collective-permute-start | bytes 786440 | tf_op jit(solution)/shard_map/ppermute | solution.py:90
  63.4 20.7 %collective-permute-start.43 = (bf16[128,1024]{1,0:T(8,128)(2,1)S(1)}, bf16[128,1024]{1,0:T(8,128)(2,1)S(1)}, u32[]{:S(2)}, u32[]{:S(2)}) collective-permute-start(bf16[128,1024]{1,0:T(8,128)(2,1)S(1)} %constant_dynamic-slice_fusion.5), channel_id=1, source_target_pairs={{0,12},{1,13},{2,14},{3,15},{4,0},{5,1},{6,2},{7,3},{8,4},{9,5},{1... | collective-permute-start | bytes 786440 | tf_op jit(solution)/shard_map/ppermute | solution.py:90
  81.5 27.3 %collective-permute-start.9 = (bf16[128,3072]{1,0:T(8,128)(2,1)S(1)}, bf16[128,3072]{1,0:T(8,128)(2,1)}, u32[]{:S(2)}, u32[]{:S(2)}) collective-permute-start(bf16[128,3072]{1,0:T(8,128)(2,1)S(1)} %pad_maximum_fusion.8.refs_0_), channel_id=1, source_target_pairs={{0,2},{1,3},{2,0},{3,1},{4,6},{5,7},{6,4},{7,5},{8,10},{9,11},{10,... | collective-permute-start | bytes 2359304 | tf_op jit(solution)/shard_map/ppermute | solution.py:90
  84.0 24.4 %collective-permute-start.4 = (bf16[4,2,32,1024]{3,2,1,0:T(8,128)(2,1)S(1)}, bf16[4,2,32,1024]{3,2,1,0:T(8,128)(2,1)S(1)}, u32[]{:S(2)}, u32[]{:S(2)}) collective-permute-start(bf16[4,2,32,1024]{3,2,1,0:T(8,128)(2,1)S(1)} %get-tuple-element.295), channel_id=1, source_target_pairs={{0,1},{1,0},{2,3},{3,2},{4,5},{5,4},{6,7},{7,6},{8,9},{9,8},{10,11... | collective-permute-start | bytes 1572872 | tf_op jit(solution)/shard_map/ppermute | solution.py:90
  84.1 17.7 %collective-permute-start.23 = (bf16[64,1024]{1,0:T(8,128)(2,1)S(1)}, bf16[64,1024]{1,0:T(8,128)(2,1)S(1)}, u32[]{:S(2)}, u32[]{:S(2)}) collective-permute-start(bf16[64,1024]{1,0:T(8,128)(2,1)S(1)} %slice.474), channel_id=1, source_target_pairs={{0,2},{1,3},{2,0},{3,1},{4,6},{5,7},{6,4},{7,5},{8,10},{9,11},{10,... | collective-permute-start | bytes 393224 | tf_op jit(solution)/shard_map/ppermute | solution.py:90
  85.3 18.0 %collective-permute-start.25 = (bf16[128,1024]{1,0:T(8,128)(2,1)S(1)}, bf16[128,1024]{1,0:T(8,128)(2,1)S(1)}, u32[]{:S(2)}, u32[]{:S(2)}) collective-permute-start(bf16[128,1024]{1,0:T(8,128)(2,1)S(1)} %collective-permute-done.20.refs_1_), channel_id=1, source_target_pairs={{0,1},{1,0},{2,3},{3,2},{4,5},{5,4},{6,7},{7,6},{8,9},{9,8},{10,11... | collective-permute-start | bytes 786440 | tf_op jit(solution)/shard_map/ppermute | solution.py:90
  85.5 17.9 %collective-permute-start.26 = (bf16[128,1024]{1,0:T(8,128)(2,1)S(1)}, bf16[128,1024]{1,0:T(8,128)(2,1)S(1)}, u32[]{:S(2)}, u32[]{:S(2)}) collective-permute-start(bf16[128,1024]{1,0:T(8,128)(2,1)S(1)} %collective-permute-done.21.refs_2_), channel_id=1, source_target_pairs={{0,1},{1,0},{2,3},{3,2},{4,5},{5,4},{6,7},{7,6},{8,9},{9,8},{10,11... | collective-permute-start | bytes 786440 | tf_op jit(solution)/shard_map/ppermute | solution.py:90
  101.7 36.9 %collective-permute-start.33 = (bf16[128,4096]{1,0:T(8,128)(2,1)}, bf16[128,4096]{1,0:T(8,128)(2,1)}, u32[]{:S(2)}, u32[]{:S(2)}) collective-permute-start(bf16[128,4096]{1,0:T(8,128)(2,1)} %pad_maximum_fusion.2.refs_0_), channel_id=1, source_target_pairs={{0,2},{1,3},{2,0},{3,1},{4,6},{5,7},{6,4},{7,5},{8,10},{9,11},{10,... | collective-permute-start | bytes 3145736 | tf_op jit(solution)/shard_map/ppermute | solution.py:90
  105.7 31.3 %collective-permute-start.8 = (bf16[128,3072]{1,0:T(8,128)(2,1)S(1)}, bf16[128,3072]{1,0:T(8,128)(2,1)}, u32[]{:S(2)}, u32[]{:S(2)}) collective-permute-start(bf16[128,3072]{1,0:T(8,128)(2,1)S(1)} %pad_maximum_fusion.8.refs_0_), channel_id=1, source_target_pairs={{0,16},{16,0},{1,17},{17,1},{2,18},{18,2},{3,19},{19,3},{4,20},{20... | collective-permute-start | bytes 2359304 | tf_op jit(solution)/shard_map/ppermute | solution.py:102
  107.8 40.8 %collective-permute-start.32 = (bf16[128,4096]{1,0:T(8,128)(2,1)}, bf16[128,4096]{1,0:T(8,128)(2,1)}, u32[]{:S(2)}, u32[]{:S(2)}) collective-permute-start(bf16[128,4096]{1,0:T(8,128)(2,1)} %pad_maximum_fusion.2.refs_0_), channel_id=1, source_target_pairs={{0,16},{16,0},{1,17},{17,1},{2,18},{18,2},{3,19},{19,3},{4,20},{20... | collective-permute-start | bytes 3145736 | tf_op jit(solution)/shard_map/ppermute | solution.py:102
  108.4 40.3 %collective-permute-start.45 = (bf16[512,1024]{1,0:T(8,128)(2,1)}, bf16[512,1024]{1,0:T(8,128)(2,1)}, u32[]{:S(2)}, u32[]{:S(2)}) collective-permute-start(bf16[512,1024]{1,0:T(8,128)(2,1)} %pad_maximum_fusion.3.refs_0_), channel_id=1, source_target_pairs={{0,2},{1,3},{2,0},{3,1},{4,6},{5,7},{6,4},{7,5},{8,10},{9,11},{10,... | collective-permute-start | bytes 3145736 | tf_op jit(solution)/shard_map/ppermute | solution.py:90
  108.8 62.3 %collective-permute-start.44 = (bf16[512,1024]{1,0:T(8,128)(2,1)}, bf16[512,1024]{1,0:T(8,128)(2,1)}, u32[]{:S(2)}, u32[]{:S(2)}) collective-permute-start(bf16[512,1024]{1,0:T(8,128)(2,1)} %pad_maximum_fusion.3.refs_0_), channel_id=1, source_target_pairs={{0,16},{16,0},{1,17},{17,1},{2,18},{18,2},{3,19},{19,3},{4,20},{20... | collective-permute-start | bytes 3145736 | tf_op jit(solution)/shard_map/ppermute | solution.py:102
  137.0 41.6 %collective-permute-start.10 = (bf16[64,3072]{1,0:T(8,128)(2,1)S(1)}, bf16[64,3072]{1,0:T(8,128)(2,1)S(1)}, u32[]{:S(2)}, u32[]{:S(2)}) collective-permute-start(bf16[64,3072]{1,0:T(8,128)(2,1)S(1)} %slice.464), channel_id=1, source_target_pairs={{0,16},{16,0},{1,17},{17,1},{2,18},{18,2},{3,19},{19,3},{4,20},{20... | collective-permute-start | bytes 1179656 | tf_op jit(solution)/shard_map/ppermute | solution.py:102
  138.6 40.0 %collective-permute-start.11 = (bf16[64,3072]{1,0:T(8,128)(2,1)S(1)}, bf16[64,3072]{1,0:T(8,128)(2,1)}, u32[]{:S(2)}, u32[]{:S(2)}) collective-permute-start(bf16[64,3072]{1,0:T(8,128)(2,1)S(1)} %slice.465), channel_id=1, source_target_pairs={{0,2},{1,3},{2,0},{3,1},{4,6},{5,7},{6,4},{7,5},{8,10},{9,11},{10,... | collective-permute-start | bytes 1179656 | tf_op jit(solution)/shard_map/ppermute | solution.py:90
  148.7 42.9 %collective-permute-start.12 = (bf16[128,3072]{1,0:T(8,128)(2,1)S(1)}, bf16[128,3072]{1,0:T(8,128)(2,1)}, u32[]{:S(2)}, u32[]{:S(2)}) collective-permute-start(bf16[128,3072]{1,0:T(8,128)(2,1)S(1)} %pad_maximum_fusion.8.refs_0_), channel_id=1, source_target_pairs={{0,1},{1,0},{2,3},{3,2},{4,5},{5,4},{6,7},{7,6},{8,9},{9,8},{10,11... | collective-permute-start | bytes 2359304 | tf_op jit(solution)/shard_map/ppermute | solution.py:90
  148.7 45.0 %collective-permute-start.13 = (bf16[128,3072]{1,0:T(8,128)(2,1)}, bf16[128,3072]{1,0:T(8,128)(2,1)}, u32[]{:S(2)}, u32[]{:S(2)}) collective-permute-start(bf16[128,3072]{1,0:T(8,128)(2,1)} %collective-permute-done.8.refs_1_), channel_id=1, source_target_pairs={{0,1},{1,0},{2,3},{3,2},{4,5},{5,4},{6,7},{7,6},{8,9},{9,8},{10,11... | collective-permute-start | bytes 2359304 | tf_op jit(solution)/shard_map/ppermute | solution.py:90
  171.1 23.1 %collective-permute-start.14 = (bf16[128,3072]{1,0:T(8,128)(2,1)}, bf16[128,3072]{1,0:T(8,128)(2,1)}, u32[]{:S(2)}, u32[]{:S(2)}) collective-permute-start(bf16[128,3072]{1,0:T(8,128)(2,1)} %collective-permute-done.9.refs_2_), channel_id=1, source_target_pairs={{0,1},{1,0},{2,3},{3,2},{4,5},{5,4},{6,7},{7,6},{8,9},{9,8},{10,11... | collective-permute-start | bytes 2359304 | tf_op jit(solution)/shard_map/ppermute | solution.py:90
  191.6 79.4 %collective-permute-start.36 = (bf16[128,4096]{1,0:T(8,128)(2,1)}, bf16[128,4096]{1,0:T(8,128)(2,1)}, u32[]{:S(2)}, u32[]{:S(2)}) collective-permute-start(bf16[128,4096]{1,0:T(8,128)(2,1)} %pad_maximum_fusion.2.refs_0_), channel_id=1, source_target_pairs={{0,1},{1,0},{2,3},{3,2},{4,5},{5,4},{6,7},{7,6},{8,9},{9,8},{10,11... | collective-permute-start | bytes 3145736 | tf_op jit(solution)/shard_map/ppermute | solution.py:90
  191.6 83.6 %collective-permute-start.34 = (bf16[64,4096]{1,0:T(8,128)(2,1)}, bf16[64,4096]{1,0:T(8,128)(2,1)}, u32[]{:S(2)}, u32[]{:S(2)}) collective-permute-start(bf16[64,4096]{1,0:T(8,128)(2,1)} %slice.477), channel_id=1, source_target_pairs={{0,16},{16,0},{1,17},{17,1},{2,18},{18,2},{3,19},{19,3},{4,20},{20... | collective-permute-start | bytes 1572872 | tf_op jit(solution)/shard_map/ppermute | solution.py:102
  193.2 83.6 %collective-permute-start.35 = (bf16[64,4096]{1,0:T(8,128)(2,1)}, bf16[64,4096]{1,0:T(8,128)(2,1)}, u32[]{:S(2)}, u32[]{:S(2)}) collective-permute-start(bf16[64,4096]{1,0:T(8,128)(2,1)} %slice.478), channel_id=1, source_target_pairs={{0,2},{1,3},{2,0},{3,1},{4,6},{5,7},{6,4},{7,5},{8,10},{9,11},{10,... | collective-permute-start | bytes 1572872 | tf_op jit(solution)/shard_map/ppermute | solution.py:90
  193.6 83.1 %collective-permute-start.46 = (bf16[256,1024]{1,0:T(8,128)(2,1)}, bf16[256,1024]{1,0:T(8,128)(2,1)}, u32[]{:S(2)}, u32[]{:S(2)}) collective-permute-start(bf16[256,1024]{1,0:T(8,128)(2,1)} %slice.480), channel_id=1, source_target_pairs={{0,16},{16,0},{1,17},{17,1},{2,18},{18,2},{3,19},{19,3},{4,20},{20... | collective-permute-start | bytes 1572872 | tf_op jit(solution)/shard_map/ppermute | solution.py:102
  194.2 95.1 %collective-permute-start.37 = (bf16[128,4096]{1,0:T(8,128)(2,1)}, bf16[128,4096]{1,0:T(8,128)(2,1)}, u32[]{:S(2)}, u32[]{:S(2)}) collective-permute-start(bf16[128,4096]{1,0:T(8,128)(2,1)} %collective-permute-done.32.refs_1_), channel_id=1, source_target_pairs={{0,1},{1,0},{2,3},{3,2},{4,5},{5,4},{6,7},{7,6},{8,9},{9,8},{10,11... | collective-permute-start | bytes 3145736 | tf_op jit(solution)/shard_map/ppermute | solution.py:90
  271.0 18.8 %collective-permute-start.38 = (bf16[128,4096]{1,0:T(8,128)(2,1)}, bf16[128,4096]{1,0:T(8,128)(2,1)S(1)}, u32[]{:S(2)}, u32[]{:S(2)}) collective-permute-start(bf16[128,4096]{1,0:T(8,128)(2,1)} %collective-permute-done.33.refs_2_), channel_id=1, source_target_pairs={{0,1},{1,0},{2,3},{3,2},{4,5},{5,4},{6,7},{7,6},{8,9},{9,8},{10,11... | collective-permute-start | bytes 3145736 | tf_op jit(solution)/shard_map/ppermute | solution.py:90
  331.6 200.4 %collective-permute-start.86 = (bf16[2048,1024]{1,0:T(8,128)(2,1)}, bf16[2048,1024]{1,0:T(8,128)(2,1)}, u32[]{:S(2)}, u32[]{:S(2)}) collective-permute-start(bf16[2048,1024]{1,0:T(8,128)(2,1)} %rows_by_block.3), channel_id=1, source_target_pairs={{0,1},{1,0},{2,3},{3,2},{4,5},{5,4},{6,7},{7,6},{8,9},{9,8},{10,11... | collective-permute-start | bytes 12582920 | tf_op jit(solution)/shard_map/ppermute | solution.py:90
  353.7 133.6 %collective-permute-start.68 = (bf16[512,1024]{1,0:T(8,128)(2,1)}, bf16[512,1024]{1,0:T(8,128)(2,1)}, u32[]{:S(2)}, u32[]{:S(2)}) collective-permute-start(bf16[512,1024]{1,0:T(8,128)(2,1)} %convolution_convert_fusion.4), channel_id=1, source_target_pairs={{0,1},{1,0},{2,3},{3,2},{4,5},{5,4},{6,7},{7,6},{8,9},{9,8},{10,11... | collective-permute-start | bytes 3145736 | tf_op jit(solution)/shard_map/ppermute | solution.py:90
  486.2 27.7 %collective-permute-start.59 = (bf16[512,3072]{1,0:T(8,128)(2,1)}, bf16[512,3072]{1,0:T(8,128)(2,1)}, u32[]{:S(2)}, u32[]{:S(2)}) collective-permute-start(bf16[512,3072]{1,0:T(8,128)(2,1)} %convolution_convert_fusion.2), channel_id=1, source_target_pairs={{0,1},{1,0},{2,3},{3,2},{4,5},{5,4},{6,7},{7,6},{8,9},{9,8},{10,11... | collective-permute-start | bytes 9437192 | tf_op jit(solution)/shard_map/ppermute | solution.py:90
  511.5 27.0 %collective-permute-start.77 = (bf16[512,4096]{1,0:T(8,128)(2,1)S(1)}, bf16[512,4096]{1,0:T(8,128)(2,1)S(1)}, u32[]{:S(2)}, u32[]{:S(2)}) collective-permute-start(bf16[512,4096]{1,0:T(8,128)(2,1)S(1)} %copy-done.38), channel_id=1, source_target_pairs={{0,1},{1,0},{2,3},{3,2},{4,5},{5,4},{6,7},{7,6},{8,9},{9,8},{10,11... | collective-permute-start | bytes 12582920 | tf_op jit(solution)/shard_map/ppermute | solution.py:90
  528.8 20.6 %collective-permute-start.61 = (bf16[4,32,3072]{2,1,0:T(8,128)(2,1)S(1)}, bf16[4,32,3072]{2,1,0:T(8,128)(2,1)}, u32[]{:S(2)}, u32[]{:S(2)}) collective-permute-start(bf16[4,32,3072]{2,1,0:T(8,128)(2,1)S(1)} %pad_maximum_fusion.9), channel_id=1, source_target_pairs={{0,16},{16,0},{1,17},{17,1},{2,18},{18,2},{3,19},{19,3},{4,20},{20... | collective-permute-start | bytes 2359304 | tf_op jit(solution)/shard_map/ppermute | solution.py:102
  530.5 20.7 %collective-permute-start.63 = (bf16[4,32,3072]{2,1,0:T(8,128)(2,1)}, bf16[4,32,3072]{2,1,0:T(8,128)(2,1)}, u32[]{:S(2)}, u32[]{:S(2)}) collective-permute-start(bf16[4,32,3072]{2,1,0:T(8,128)(2,1)} %pad_maximum_fusion.10), channel_id=1, source_target_pairs={{0,2},{1,3},{2,0},{3,1},{4,6},{5,7},{6,4},{7,5},{8,10},{9,11},{10,... | collective-permute-start | bytes 2359304 | tf_op jit(solution)/shard_map/ppermute | solution.py:90
  536.6 31.0 %collective-permute-start.87 = (bf16[2,128,1024]{2,1,0:T(8,128)(2,1)S(1)}, bf16[2,128,1024]{2,1,0:T(8,128)(2,1)S(1)}, u32[]{:S(2)}, u32[]{:S(2)}) collective-permute-start(bf16[2,128,1024]{2,1,0:T(8,128)(2,1)S(1)} %get-tuple-element.252), channel_id=1, source_target_pairs={{0,2},{1,3},{2,0},{3,1},{4,6},{5,7},{6,4},{7,5},{8,10},{9,11},{10,... | collective-permute-start | bytes 1572872 | tf_op jit(solution)/shard_map/ppermute | solution.py:90
  537.2 30.4 %collective-permute-start.89 = (bf16[2,128,1024]{2,1,0:T(8,128)(2,1)S(1)}, bf16[2,128,1024]{2,1,0:T(8,128)(2,1)S(1)}, u32[]{:S(2)}, u32[]{:S(2)}) collective-permute-start(bf16[2,128,1024]{2,1,0:T(8,128)(2,1)S(1)} %get-tuple-element.251), channel_id=1, source_target_pairs={{0,16},{16,0},{1,17},{17,1},{2,18},{18,2},{3,19},{19,3},{4,20},{20... | collective-permute-start | bytes 1572872 | tf_op jit(solution)/shard_map/ppermute | solution.py:102
  566.8 17.6 %collective-permute-start.67 = (bf16[32,3072]{1,0:T(8,128)(2,1)S(1)}, bf16[32,3072]{1,0:T(8,128)(2,1)S(1)}, u32[]{:S(2)}, u32[]{:S(2)}) collective-permute-start(bf16[32,3072]{1,0:T(8,128)(2,1)S(1)} %fusion.141), channel_id=1, source_target_pairs={{0,16},{16,0},{1,17},{17,1},{2,18},{18,2},{3,19},{19,3},{4,20},{20... | collective-permute-start | bytes 589832 | tf_op jit(solution)/shard_map/ppermute | solution.py:102
  568.1 38.8 %collective-permute-start.88 = (bf16[4,128,1024]{2,1,0:T(8,128)(2,1)S(1)}, bf16[4,128,1024]{2,1,0:T(8,128)(2,1)S(1)}, u32[]{:S(2)}, u32[]{:S(2)}) collective-permute-start(bf16[4,128,1024]{2,1,0:T(8,128)(2,1)S(1)} %pad_maximum_fusion.6), channel_id=1, source_target_pairs={{0,16},{16,0},{1,17},{17,1},{2,18},{18,2},{3,19},{19,3},{4,20},{20... | collective-permute-start | bytes 3145736 | tf_op jit(solution)/shard_map/ppermute | solution.py:102
  569.5 37.3 %collective-permute-start.90 = (bf16[4,128,1024]{2,1,0:T(8,128)(2,1)S(1)}, bf16[4,128,1024]{2,1,0:T(8,128)(2,1)S(1)}, u32[]{:S(2)}, u32[]{:S(2)}) collective-permute-start(bf16[4,128,1024]{2,1,0:T(8,128)(2,1)S(1)} %pad_maximum_fusion.7), channel_id=1, source_target_pairs={{0,2},{1,3},{2,0},{3,1},{4,6},{5,7},{6,4},{7,5},{8,10},{9,11},{10,... | collective-permute-start | bytes 3145736 | tf_op jit(solution)/shard_map/ppermute | solution.py:90
  580.5 39.2 %collective-permute-start.79 = (bf16[4,32,4096]{2,1,0:T(8,128)(2,1)S(1)}, bf16[4,32,4096]{2,1,0:T(8,128)(2,1)S(1)}, u32[]{:S(2)}, u32[]{:S(2)}) collective-permute-start(bf16[4,32,4096]{2,1,0:T(8,128)(2,1)S(1)} %pad_maximum_fusion.4), channel_id=1, source_target_pairs={{0,16},{16,0},{1,17},{17,1},{2,18},{18,2},{3,19},{19,3},{4,20},{20... | collective-permute-start | bytes 3145736 | tf_op jit(solution)/shard_map/ppermute | solution.py:102
  582.0 37.8 %collective-permute-start.81 = (bf16[4,32,4096]{2,1,0:T(8,128)(2,1)S(1)}, bf16[4,32,4096]{2,1,0:T(8,128)(2,1)S(1)}, u32[]{:S(2)}, u32[]{:S(2)}) collective-permute-start(bf16[4,32,4096]{2,1,0:T(8,128)(2,1)S(1)} %pad_maximum_fusion.5), channel_id=1, source_target_pairs={{0,2},{1,3},{2,0},{3,1},{4,6},{5,7},{6,4},{7,5},{8,10},{9,11},{10,... | collective-permute-start | bytes 3145736 | tf_op jit(solution)/shard_map/ppermute | solution.py:90
  607.6 22.7 %collective-permute-start.91 = (bf16[128,1024]{1,0:T(8,128)(2,1)S(1)}, bf16[128,1024]{1,0:T(8,128)(2,1)S(1)}, u32[]{:S(2)}, u32[]{:S(2)}) collective-permute-start(bf16[128,1024]{1,0:T(8,128)(2,1)S(1)} %get-tuple-element.275), channel_id=1, source_target_pairs={{0,4},{1,5},{2,6},{3,7},{4,8},{5,9},{6,10},{7,11},{8,12},{9,13},{1... | collective-permute-start | bytes 786440 | tf_op jit(solution)/shard_map/ppermute | solution.py:90
  608.0 23.3 %collective-permute-start.92 = (bf16[128,1024]{1,0:T(8,128)(2,1)S(1)}, bf16[128,1024]{1,0:T(8,128)(2,1)S(1)}, u32[]{:S(2)}, u32[]{:S(2)}) collective-permute-start(bf16[128,1024]{1,0:T(8,128)(2,1)S(1)} %get-tuple-element.277), channel_id=1, source_target_pairs={{0,8},{1,9},{2,10},{3,11},{4,12},{5,13},{6,14},{7,15},{8,0},{9,1},... | collective-permute-start | bytes 786440 | tf_op jit(solution)/shard_map/ppermute | solution.py:90
  611.3 19.9 %collective-permute-start.93 = (bf16[128,1024]{1,0:T(8,128)(2,1)S(1)}, bf16[128,1024]{1,0:T(8,128)(2,1)S(1)}, u32[]{:S(2)}, u32[]{:S(2)}) collective-permute-start(bf16[128,1024]{1,0:T(8,128)(2,1)S(1)} %get-tuple-element.276), channel_id=1, source_target_pairs={{0,12},{1,13},{2,14},{3,15},{4,0},{5,1},{6,2},{7,3},{8,4},{9,5},{1... | collective-permute-start | bytes 786440 | tf_op jit(solution)/shard_map/ppermute | solution.py:90
  620.3 16.6 %collective-permute-start.82 = (bf16[32,4096]{1,0:T(8,128)(2,1)S(1)}, bf16[32,4096]{1,0:T(8,128)(2,1)S(1)}, u32[]{:S(2)}, u32[]{:S(2)}) collective-permute-start(bf16[32,4096]{1,0:T(8,128)(2,1)S(1)} %get-tuple-element.278), channel_id=1, source_target_pairs={{0,4},{1,5},{2,6},{3,7},{4,8},{5,9},{6,10},{7,11},{8,12},{9,13},{1... | collective-permute-start | bytes 786440 | tf_op jit(solution)/shard_map/ppermute | solution.py:90
  627.2 17.2 %collective-permute-start.83 = (bf16[32,4096]{1,0:T(8,128)(2,1)S(1)}, bf16[32,4096]{1,0:T(8,128)(2,1)S(1)}, u32[]{:S(2)}, u32[]{:S(2)}) collective-permute-start(bf16[32,4096]{1,0:T(8,128)(2,1)S(1)} %get-tuple-element.280), channel_id=1, source_target_pairs={{0,8},{1,9},{2,10},{3,11},{4,12},{5,13},{6,14},{7,15},{8,0},{9,1},... | collective-permute-start | bytes 786440 | tf_op jit(solution)/shard_map/ppermute | solution.py:90
  (111 other events, 1003.6 us)

commit v2 on v0

v2 whole, which is shorter than its diff:
```python
import functools
import math

import jax
import jax.numpy as jnp
from jax import lax
from jax.experimental import pallas as pl
from jax.experimental.pallas import tpu as pltpu
from jax.sharding import PartitionSpec as P

HD = 64
ZN = 4
PAIR = 128
LOG2E = math.log2(math.e)
ROOT = math.sqrt(2.0 / math.pi)
F32 = jnp.float32
BF16 = jnp.bfloat16


def normalize(values_in):
    center = values_in - jnp.mean(values_in, axis=-1, keepdims=True)
    inverse = lax.rsqrt(jnp.mean(center * center, axis=-1, keepdims=True) + 1e-05)
    return (center * inverse, inverse)


def norm_back(grad_hat, normed, inverse):
    return inverse * (
        grad_hat
        - jnp.mean(grad_hat, axis=-1, keepdims=True)
        - normed * jnp.mean(grad_hat * normed, axis=-1, keepdims=True)
    )


def rows_dot(left, right):
    return lax.dot_general(
        left, right, (((0,), (0,)), ((), ())), preferred_element_type=F32
    )


def back_dot(grad_in, weight):
    return lax.dot_general(
        grad_in, weight, (((1,), (1,)), ((), ())), preferred_element_type=F32
    )


def rotary_tables(length):
    half_size = HD // 2
    frequency = jnp.exp(
        jnp.arange(half_size, dtype=F32) * (-2.0 * math.log(10000.0) / HD)
    )
    angles = jnp.arange(length, dtype=F32)[:, None] * frequency[None, :]
    angles = jnp.concatenate([angles] * (PAIR // half_size), axis=-1)
    return (jnp.cos(angles), jnp.sin(angles))


class Order:
    def __init__(self):
        self.mark = ()

    def __call__(self, *arrays):
        out = lax.optimization_barrier((*arrays, *self.mark))[: len(arrays)]
        self.mark = (out[0],)
        return out[0] if len(out) == 1 else out

    def note(self, *arrays):
        self.mark = arrays
        return arrays[0] if len(arrays) == 1 else arrays


def scoped(name):
    def wrap(function):
        @functools.wraps(function)
        def inner(*args, **kwargs):
            with jax.named_scope(name):
                return function(*args, **kwargs)

        return inner

    return wrap


class Net:
    def __init__(self, dp, fs):
        self.dp, self.fs = dp, fs
        self.yn = fs // (2 * ZN)
        index = lax.axis_index("fsdp")
        self.me = index
        self.z0 = index // (2 * self.yn)
        self.y0 = (index // 2) % self.yn
        self.c0 = index % 2
        self.p0 = lax.axis_index("dp") % 2

    def perm(self, values_in, zx, dy, dc):
        pairs = []
        for i in range(self.fs):
            z, y, c = i // (2 * self.yn), (i // 2) % self.yn, i % 2
            to = ((z ^ zx) * self.yn + (y + dy) % self.yn) * 2 + (c ^ dc)
            pairs.append((i, to))
        return lax.ppermute(values_in, "fsdp", pairs)

    @scoped("z_hop")
    def z(self, values_in, k):
        return self.perm(values_in, k, 0, 0)

    @scoped("y_hop")
    def y(self, values_in, s):
        return self.perm(values_in, 0, s, 0)

    @scoped("core_hop")
    def c(self, values_in):
        return self.perm(values_in, 0, 0, 1)

    @scoped("x_hop")
    def x(self, values_in):
        return lax.ppermute(values_in, "dp", [(i, i ^ 1) for i in range(self.dp)])


def stack_kernel(*refs):
    at = 0
    for item in refs[:-1]:
        rows = item.shape[0]
        refs[-1][at : at + rows, :] = item[...]
        at += rows


def stack_rows(*items):
    rows = sum(item.shape[0] for item in items)
    return pl.pallas_call(
        stack_kernel,
        out_shape=jax.ShapeDtypeStruct((rows, items[0].shape[1]), items[0].dtype),
        cost_estimate=cost(),
        name="stack_rows",
    )(*items)


class Gather:
    def __init__(self, net, shard):
        self.net = net
        self.rows, self.columns = shard.shape
        self.half = self.rows // 2
        self.own = lax.dynamic_slice_in_dim(shard, net.p0 * self.half, self.half, 0)

    def along(self, own):
        self.own = own
        self.parts = [self.net.z(own, k) for k in range(1, ZN)]

    def join_line(self, order):
        self.line = stack_rows(*order(self.own, *self.parts))

    def across(self):
        net = self.net
        self.over = net.x(self.line)
        self.beside = [net.y(self.line, s) for s in range(1, net.yn)]

    def join_across(self, order):
        self.over, *self.beside = order(self.over, *self.beside)

    def corners(self):
        net = self.net
        mid = (ZN // 2) * self.half
        self.corner_one = [net.x(item[:mid]) for item in self.beside]
        self.corner_two = [net.y(self.over[mid:], s) for s in range(1, net.yn)]
        self.pieces = [self.line, self.over] + self.beside
        self.plan = [(0, 0, 0, ZN), (0, 1, 0, ZN)]
        self.plan += [(s, 0, 0, ZN) for s in range(1, net.yn)]
        self.moved = [net.c(item) for item in self.pieces]

    def finish(self, order):
        net = self.net
        late = order(*self.corner_one, *self.corner_two)
        plan = [(s, 1, 0, ZN // 2) for s in range(1, net.yn)]
        plan += [(s, 1, ZN // 2, ZN - ZN // 2) for s in range(1, net.yn)]
        pieces = self.pieces + list(late) + self.moved + [net.c(item) for item in late]
        plan = self.plan + plan
        full = [(s, q, side, first, count) for side in range(2) for s, q, first, count in plan]
        return full, pieces


def piece_spots(plan, where_ref, rows, half, yn):
    z0, y0, c0, p0 = where_ref[0], where_ref[1], where_ref[2], where_ref[3]
    spots = []
    for i, (s, q, side, first, count) in enumerate(plan):
        y = lax.rem(y0 + yn - s, yn)
        p = lax.rem(p0 + q, 2)
        c = lax.rem(c0 + side, 2)
        for k in range(count):
            z = lax.bitwise_xor(z0, jnp.int32(first + k))
            start = pl.multiple_of(((z * yn + y) * 2 + c) * rows + p * half, half)
            spots.append((i, k * half, first + k, start))
    return spots


def pack_kernel(*refs):
    time_ref, vectors, out_ref = refs[0], refs[1:-1], refs[-1]
    out_ref[...] = jnp.zeros_like(out_ref)
    rows = time_ref.shape[0]
    out_ref[:rows, :] = time_ref[...]
    for i, item in enumerate(vectors):
        out_ref[rows + i : rows + i + 1, : item.shape[1]] = item[...]


def small_kernel(rows, te_rows, sizes, yn, where_ref, embed_ref, own_ref, other_ref, *refs):
    scale_ref, all_ref, outs, held, sems = refs[0], refs[1], refs[2:-2], refs[-2], refs[-1]
    z0, y0, c0 = where_ref[0], where_ref[1], where_ref[2]
    copies = []
    for side, piece_ref in enumerate((own_ref, other_ref)):
        c = lax.rem(c0 + side, 2)
        for s in range(yn):
            y = lax.rem(y0 + yn - s, yn)
            for k in range(ZN):
                z = lax.bitwise_xor(z0, jnp.int32(k))
                copies.append(
                    pltpu.make_async_copy(
                        piece_ref.at[s * ZN + k],
                        held.at[(z * yn + y) * 2 + c],
                        sems.at[len(copies)],
                    )
                )
    for copy in copies:
        copy.start()
    for copy in copies:
        copy.wait()
    fs = held.shape[0]
    scale = jnp.ones_like(scale_ref)
    whole = jnp.concatenate([held[f, :te_rows, :] for f in range(fs)], axis=0)
    scale_ref[...] = scale + jnp.dot(embed_ref[...], whole, preferred_element_type=F32)
    for i, (size, out_ref) in enumerate(zip(sizes, outs)):
        pieces = [
            held[f, te_rows + i : te_rows + i + 1, :size].astype(F32) for f in range(fs)
        ]
        out_ref[...] = jnp.concatenate(pieces, axis=1)
    last, wide = te_rows + len(sizes), embed_ref.shape[1]
    all_ref[...] = jnp.concatenate(
        [held[f, last : last + 1, :wide].astype(F32) for f in range(fs)], axis=0
    )


class SmallGather:
    def __init__(self, net, time_weight, vectors, embed):
        self.net, self.sizes = net, [item.shape[0] for item in vectors]
        self.te_rows, self.width = time_weight.shape
        self.rows = self.te_rows + len(vectors) + 1
        self.rows += -self.rows % 16
        self.packed = pl.pallas_call(
            pack_kernel,
            out_shape=jax.ShapeDtypeStruct((self.rows, self.width), BF16),
            cost_estimate=cost(),
            name="pack_small",
        )(time_weight, *[item.reshape(1, -1) for item in vectors], embed)
        self.parts = [net.z(self.packed, k) for k in range(1, ZN)]

    def across(self, order):
        net = self.net
        self.line = jnp.stack(order(self.packed, *self.parts))
        self.beside = [net.y(self.line, s) for s in range(1, net.yn)]

    def other(self, order):
        self.line, *self.beside = order(self.line, *self.beside)
        self.sides = jnp.concatenate([self.line] + self.beside, axis=0)
        self.moved = self.net.c(self.sides)

    def finish(self, order, embed):
        net, fs = self.net, self.net.fs
        moved = order(self.moved)
        where = jnp.stack([net.z0, net.y0, net.c0]).astype(jnp.int32)
        shapes = [(1, self.width), (fs, embed.shape[1])]
        shapes += [(1, size * fs) for size in self.sizes]
        outs = pl.pallas_call(
            functools.partial(small_kernel, self.rows, self.te_rows, self.sizes, net.yn),
            out_shape=[jax.ShapeDtypeStruct(shape, F32) for shape in shapes],
            grid_spec=pltpu.PrefetchScalarGridSpec(
                num_scalar_prefetch=1,
                grid=(1,),
                in_specs=[pl.BlockSpec(embed.shape, lambda i, r: (0, 0))]
                + [pl.BlockSpec(memory_space=pl.ANY)] * 2,
                out_specs=[whole_spec(shape) for shape in shapes],
                scratch_shapes=[
                    pltpu.VMEM((fs, self.rows, self.width), BF16),
                    pltpu.SemaphoreType.DMA((fs,)),
                ],
            ),
            cost_estimate=cost(),
            name="small_join",
        )(where, embed, self.sides, moved)
        order.note(outs[0])
        return outs


def relative_order(net, rows, total):
    half = rows // 2
    d = jnp.arange(total, dtype=jnp.int32)
    f, i = d // rows, d % rows
    z, y, c = f // (2 * net.yn), (f // 2) % net.yn, f % 2
    p, j = i // half, i % half
    c, y, p, z = c ^ net.c0, (y - net.y0) % net.yn, p ^ net.p0, z ^ net.z0
    return (((c * net.yn + y) * 2 + p) * ZN + z) * half + j


def add_low(*items):
    total = items[0].astype(F32)
    for item in items[1:]:
        total = total + item.astype(F32)
    return total.astype(BF16)


def sum_kernel(counts, keep, *refs):
    total = sum(counts)
    kept_ref, sent_ref = refs[total], refs[total + 1]
    at, column = 0, 0
    for count in counts:
        items = refs[at : at + count]
        at += count
        wide = items[0].shape[1]
        value = items[0][...].astype(F32)
        for item in items[1:]:
            value = value + item[...].astype(F32)
        kept_ref[:, column : column + wide] = value[:keep, :]
        sent_ref[:, column : column + wide] = value[keep:, :].astype(BF16)
        column += wide


def sum_split(groups, keep):
    rows = groups[0][0].shape[0]
    columns = sum(group[0].shape[1] for group in groups)
    return pl.pallas_call(
        functools.partial(sum_kernel, [len(group) for group in groups], keep),
        out_shape=[
            jax.ShapeDtypeStruct((keep, columns), F32),
            jax.ShapeDtypeStruct((rows - keep, columns), BF16),
        ],
        cost_estimate=cost(),
        name="sum_split",
    )(*[item for group in groups for item in group])


class Scatter:
    def __init__(self, net, by_x):
        self.net, self.by_x = net, by_x

    def core(self, send):
        self.sent = self.net.c(send)

    def join_core(self, order):
        self.sent = order(self.sent)
        return self.sent

    def corners(self, own, over, *rest):
        net = self.net
        self.own, self.over, self.side = own, over, list(rest[0::2])
        if self.by_x:
            self.came = [net.x(item) for item in rest[1::2]]
        else:
            self.came = [net.y(item, s + 1) for s, item in enumerate(rest[1::2])]

    def across(self, order):
        net = self.net
        came = order(*self.came) if len(self.came) > 1 else [order(*self.came)]
        if self.by_x:
            self.side = [add_low(a, b) for a, b in zip(self.side, came)]
        else:
            self.over = add_low(self.over, *came)
        self.over = net.x(self.over)
        self.side = [net.y(item, s + 1) for s, item in enumerate(self.side)]

    def group(self, order):
        return [self.own, *order(self.over, *self.side)]


class Line:
    def __init__(self, net, half, groups):
        self.net, self.half = net, half
        self.kept, far = sum_split(groups, (ZN // 2) * half)
        self.far = net.z(far, 2)

    def nearer(self, order):
        self.here, near = sum_split([[self.kept, order(self.far)]], self.half)
        self.near = self.net.z(near, 1)

    def last(self, order):
        net = self.net
        mine = add_low(self.here, order(self.near))
        if net.dp > 2:
            groups = [list(range(q, net.dp, 2)) for q in range(2)]
            mine = lax.psum(mine, "dp", axis_index_groups=groups)
        self.mine, self.other = mine, net.x(mine)

    def finish(self, order):
        mine, other = self.mine, order(self.other)
        first = jnp.where(self.net.p0 == 0, mine, other)
        second = jnp.where(self.net.p0 == 0, other, mine)
        return jnp.concatenate([first, second], axis=0).astype(F32)


def kept_parts(yn, half):
    line = ZN * half
    return [(i * line, line) for i in range(2 * yn)]


def cost():
    return pl.CostEstimate(flops=1000, bytes_accessed=1000, transcendentals=0)


def weight_copies(plan, where_ref, rows, half, yn, pieces, targets, sems):
    spots = piece_spots(plan, where_ref, rows, half, yn)
    groups, count, column = [], 0, 0
    for target, first, wide in targets:
        group = []
        for i, row, shift, start in spots:
            group.append(
                pltpu.make_async_copy(
                    pieces[i].at[pl.ds(row, half), pl.ds(column, wide)],
                    target.at[pl.ds(start, half), pl.ds(first, wide)],
                    sems.at[count],
                )
            )
            count += 1
        column += wide
        groups.append(group)
    for group in groups:
        for copy in group:
            copy.start()
    return groups


def finish_copies(copies):
    for copy in copies:
        copy.wait()


def back_copy(held, out, first, wide, sem):
    spot = pl.ds(first, wide)
    copy = pltpu.make_async_copy(held.at[:, spot], out.at[:, spot], sem)
    copy.start()
    return copy


def qkv_kernel(plan, rows, half, yn, where_ref, x_ref, cos_ref, sin_ref, *refs):
    pieces = refs[: len(plan)]
    out_ref, wq_ref, wo_ref, wq, wo, low, sems, back_sems = refs[len(plan) :]
    wide = wo.shape[1]
    targets = [(wq, part * wide, wide) for part in range(3)] + [(wo, 0, wide)]
    groups = weight_copies(plan, where_ref, rows, half, yn, pieces, targets, sems)
    cosine, sine = cos_ref[...], sin_ref[...]
    front = lax.broadcasted_iota(jnp.int32, cosine.shape, 1) % HD < HD // 2
    backs = []
    for part in range(3):
        finish_copies(groups[part])
        backs.append(back_copy(wq, wq_ref, part * wide, wide, back_sems.at[part]))
        for j in range(wide // (2 * PAIR)):
            first = part * wide + j * 2 * PAIR
            acc = jnp.dot(
                x_ref[...], wq[:, first : first + 2 * PAIR], preferred_element_type=F32
            )
            for i in range(2):
                piece = acc[:, i * PAIR : (i + 1) * PAIR]
                if part < 2:
                    turned = jnp.where(
                        front,
                        -pltpu.roll(piece, PAIR - HD // 2, 1),
                        pltpu.roll(piece, HD // 2, 1),
                    )
                    piece = piece * cosine + turned * sine
                low[:, first + i * PAIR : first + (i + 1) * PAIR] = piece.astype(BF16)
        backs.append(back_copy(low, out_ref, part * wide, wide, back_sems.at[4 + part]))
    finish_copies(groups[3])
    backs.append(back_copy(wo, wo_ref, 0, wide, back_sems.at[3]))
    finish_copies(backs)


def where_of(net):
    return jnp.stack([net.z0, net.y0, net.c0, net.p0]).astype(jnp.int32)


ANY = pl.BlockSpec(memory_space=pl.ANY)


def whole_spec(shape):
    return pl.BlockSpec(shape, lambda i, r: (0, 0))


def qkv_rotated(net, x, plan, pieces, rows, cosine, sine):
    tokens, depth = x.shape
    total = net.fs * rows
    blocks = sum(entry[4] for entry in plan)
    half = rows // 2
    return pl.pallas_call(
        functools.partial(qkv_kernel, plan, rows, half, net.yn),
        grid_spec=pltpu.PrefetchScalarGridSpec(
            num_scalar_prefetch=1,
            grid=(1,),
            in_specs=[whole_spec(x.shape), whole_spec(cosine.shape), whole_spec(sine.shape)]
            + [ANY] * len(pieces),
            out_specs=[ANY] * 3,
            scratch_shapes=[
                pltpu.VMEM((total, 3 * depth), BF16),
                pltpu.VMEM((total, depth), BF16),
                pltpu.VMEM((tokens, 3 * depth), BF16),
                pltpu.SemaphoreType.DMA((4 * blocks,)),
                pltpu.SemaphoreType.DMA((7,)),
            ],
        ),
        out_shape=[
            jax.ShapeDtypeStruct((tokens, 3 * depth), BF16),
            jax.ShapeDtypeStruct((total, 3 * depth), BF16),
            jax.ShapeDtypeStruct((total, depth), BF16),
        ],
        compiler_params=pltpu.CompilerParams(vmem_limit_bytes=32 * 2**20),
        cost_estimate=cost(),
        name="qkv_rotated",
    )(where_of(net), x, cosine, sine, *pieces)


def up_kernel(x_ref, w_ref, b_ref, act_ref, slope_ref):
    wide = w_ref.shape[1]
    step = min(256, wide)
    for first in range(0, wide, step):
        spot = slice(first, first + step)
        v = jnp.dot(x_ref[...], w_ref[:, spot], preferred_element_type=F32) + b_ref[:, spot]
        square = v * v
        bend = jnp.tanh(v * (ROOT + ROOT * 0.044715 * square))
        half_up = 0.5 + 0.5 * bend
        act_ref[:, spot] = (v * half_up).astype(BF16)
        rise = 0.5 * ROOT + (1.5 * 0.044715 * ROOT) * square
        slope_ref[:, spot] = (half_up + v * (1.0 - bend * bend) * rise).astype(BF16)


def up_gelu(x, w, bias):
    rows, depth = x.shape
    total = w.shape[1]
    wide = min(1024, total)
    return pl.pallas_call(
        up_kernel,
        grid=(total // wide,),
        in_specs=[
            pl.BlockSpec((rows, depth), lambda j: (0, 0)),
            pl.BlockSpec((depth, wide), lambda j: (0, j)),
            pl.BlockSpec((1, wide), lambda j: (0, j)),
        ],
        out_specs=[pl.BlockSpec((rows, wide), lambda j: (0, j))] * 2,
        out_shape=[jax.ShapeDtypeStruct((rows, total), BF16)] * 2,
        cost_estimate=cost(),
        name="up_gelu",
    )(x, w, bias)


def down_kernel(plan, rows, half, yn, where_ref, g_ref, slope_ref, *refs):
    pieces = refs[: len(plan)]
    out_ref, sum_ref, w_ref, w, slope, low, sems, slope_sems, back_sems = refs[len(plan) :]
    spots = piece_spots(plan, where_ref, rows, half, yn)
    group_rows = w.shape[0] // ZN
    step = min(256, group_rows)
    z0 = where_ref[0]
    groups = [[] for _ in range(ZN)]
    for count, (i, row, shift, start) in enumerate(spots):
        copy = pltpu.make_async_copy(
            pieces[i].at[pl.ds(row, half), :], w.at[pl.ds(start, half), :], sems.at[count]
        )
        groups[shift].append(copy)
    slopes = []
    for k in range(ZN):
        at = pl.multiple_of(lax.bitwise_xor(z0, jnp.int32(k)) * group_rows, group_rows)
        for copy in groups[k]:
            copy.start()
        copy = pltpu.make_async_copy(
            slope_ref.at[:, pl.ds(at, group_rows)], slope.at[k], slope_sems.at[k]
        )
        copy.start()
        slopes.append(copy)
    backs = []
    for k in range(ZN):
        at = pl.multiple_of(lax.bitwise_xor(z0, jnp.int32(k)) * group_rows, group_rows)
        finish_copies(groups[k])
        slopes[k].wait()
        here = pl.ds(at, group_rows)
        copy = pltpu.make_async_copy(w.at[here, :], w_ref.at[here, :], back_sems.at[2 * k])
        copy.start()
        backs.append(copy)
        for j in range(group_rows // step):
            spot = slice(j * step, (j + 1) * step)
            inner = pl.multiple_of(at + j * step, step)
            acc = lax.dot_general(
                g_ref[...],
                w[pl.ds(inner, step), :],
                (((1,), (1,)), ((), ())),
                preferred_element_type=F32,
            )
            rounded = (acc * slope[k, :, spot].astype(F32)).astype(BF16)
            low[k, :, spot] = rounded
            sum_ref[:, pl.ds(inner, step)] = jnp.sum(
                rounded.astype(F32), axis=0, keepdims=True
            )
        copy = pltpu.make_async_copy(low.at[k], out_ref.at[:, here], back_sems.at[2 * k + 1])
        copy.start()
        backs.append(copy)
    finish_copies(backs)


def down_back(net, grad, plan, pieces, rows, slope):
    tokens, depth = grad.shape
    total = slope.shape[1]
    blocks = sum(entry[4] for entry in plan)
    return pl.pallas_call(
        functools.partial(down_kernel, plan, rows, rows // 2, net.yn),
        grid_spec=pltpu.PrefetchScalarGridSpec(
            num_scalar_prefetch=1,
            grid=(1,),
            in_specs=[whole_spec(grad.shape), ANY] + [ANY] * len(pieces),
            out_specs=[ANY, pl.BlockSpec((1, total), lambda i, r: (0, 0)), ANY],
            scratch_shapes=[
                pltpu.VMEM((total, depth), BF16),
                pltpu.VMEM((ZN, tokens, total // ZN), BF16),
                pltpu.VMEM((ZN, tokens, total // ZN), BF16),
                pltpu.SemaphoreType.DMA((blocks,)),
                pltpu.SemaphoreType.DMA((ZN,)),
                pltpu.SemaphoreType.DMA((2 * ZN,)),
            ],
        ),
        out_shape=[
            jax.ShapeDtypeStruct((tokens, total), BF16),
            jax.ShapeDtypeStruct((1, total), F32),
            jax.ShapeDtypeStruct((total, depth), BF16),
        ],
        compiler_params=pltpu.CompilerParams(vmem_limit_bytes=40 * 2**20),
        cost_estimate=cost(),
        name="down_back",
    )(where_of(net), grad, slope, *pieces)


def attend_kernel(len_ref, q_ref, k_ref, v_ref, out_ref):
    q, k, v = q_ref[...], k_ref[...], v_ref[...]
    length = k.shape[0]
    first = lax.broadcasted_iota(jnp.int32, q.shape, 1) < HD
    valid = lax.broadcasted_iota(jnp.int32, (1, length), 1) < len_ref[0]
    zero = jnp.zeros_like(q)
    outs = []
    for h in range(2):
        one = jnp.where(first, q, zero) if h == 0 else jnp.where(first, zero, q)
        scores = lax.dot_general(
            one, k, (((1,), (1,)), ((), ())), preferred_element_type=F32
        )
        scores = jnp.where(valid, scores * HD**-0.5, -1000000000.0)
        top = jnp.max(scores, axis=1, keepdims=True)
        exponent = jnp.exp2((scores - top) * LOG2E)
        total = jnp.sum(exponent, axis=1, keepdims=True)
        mixed = jnp.dot(exponent.astype(BF16), v, preferred_element_type=F32)
        outs.append(mixed * (1.0 / total))
    out_ref[...] = jnp.where(first, outs[0], outs[1]).astype(BF16)


def attend(length, qkv, first_pair, pairs):
    rows, total = qkv.shape
    count = total // 3 // PAIR

    def pick(part):
        return pl.BlockSpec((rows, PAIR), lambda j, r: (0, part * count + first_pair + j))

    return pl.pallas_call(
        attend_kernel,
        grid_spec=pltpu.PrefetchScalarGridSpec(
            num_scalar_prefetch=1,
            grid=(pairs,),
            in_specs=[pick(0), pick(1), pick(2)],
            out_specs=pl.BlockSpec((rows, PAIR), lambda j, r: (0, j)),
        ),
        out_shape=jax.ShapeDtypeStruct((rows, pairs * PAIR), BF16),
        cost_estimate=cost(),
        name="attend",
    )(length, qkv, qkv, qkv)


def attend_back_kernel(len_ref, q_ref, k_ref, v_ref, g_ref, cos_ref, sin_ref, out_ref):
    q, k, v, g = q_ref[...], k_ref[...], v_ref[...], g_ref[...]
    length = k.shape[0]
    lane = lax.broadcasted_iota(jnp.int32, q.shape, 1)
    first = lane < HD
    valid = lax.broadcasted_iota(jnp.int32, (length, length), 0) < len_ref[0]
    zero = jnp.zeros_like(q)
    grads = []
    for h in range(2):
        key = jnp.where(first, k, zero) if h == 0 else jnp.where(first, zero, k)
        value = jnp.where(first, v, zero) if h == 0 else jnp.where(first, zero, v)
        scores = lax.dot_general(
            key, q, (((1,), (1,)), ((), ())), preferred_element_type=F32
        )
        scores = jnp.where(valid, scores * HD**-0.5, -1000000000.0)
        top = jnp.max(scores, axis=0, keepdims=True)
        exponent = jnp.exp2((scores - top) * LOG2E)
        total = jnp.sum(exponent, axis=0, keepdims=True)
        probs = exponent * (1.0 / total)
        grad_probs = lax.dot_general(
            value, g, (((1,), (1,)), ((), ())), preferred_element_type=F32
        )
        delta = jnp.sum(grad_probs * probs, axis=0, keepdims=True)
        grad_scores = (probs * (grad_probs - delta)).astype(BF16)
        grads.append(
            (
                lax.dot_general(
                    grad_scores, k, (((0,), (0,)), ((), ())), preferred_element_type=F32
                ),
                jnp.dot(grad_scores, q, preferred_element_type=F32),
                jnp.dot(probs.astype(BF16), g, preferred_element_type=F32),
            )
        )
    front = lane % HD < HD // 2
    cosine, sine = cos_ref[...] * HD**-0.5, sin_ref[...] * HD**-0.5
    for i in range(2):
        grad = jnp.where(first, grads[0][i], grads[1][i])
        sined = grad * sine
        turned = jnp.where(
            front, pltpu.roll(sined, PAIR - HD // 2, 1), -pltpu.roll(sined, HD // 2, 1)
        )
        out_ref[i] = (grad * cosine + turned).astype(BF16)
    out_ref[2] = jnp.where(first, grads[0][2], grads[1][2]).astype(BF16)


def attend_back(length, qkv, grad, cosine, sine, first_pair, pairs):
    rows, total = qkv.shape
    count = total // 3 // PAIR

    def pick(part):
        return pl.BlockSpec((rows, PAIR), lambda j, r: (0, part * count + first_pair + j))

    table = pl.BlockSpec((rows, PAIR), lambda j, r: (0, 0))
    return pl.pallas_call(
        attend_back_kernel,
        grid_spec=pltpu.PrefetchScalarGridSpec(
            num_scalar_prefetch=1,
            grid=(pairs,),
            in_specs=[pick(0), pick(1), pick(2), pick(0), table, table],
            out_specs=pl.BlockSpec((3, rows, PAIR), lambda j, r: (0, 0, j)),
        ),
        out_shape=jax.ShapeDtypeStruct((3, rows, pairs * PAIR), BF16),
        cost_estimate=cost(),
        name="attend_back",
    )(length, qkv, qkv, qkv, grad, cosine, sine)


def tall_kernel(left_ref, grad_ref, out_ref):
    out_ref[...] = lax.dot_general(
        left_ref[...], grad_ref[...], (((0,), (0,)), ((), ())), preferred_element_type=F32
    ).astype(BF16)


def tall_rows_dot(left, grad):
    depth, columns = grad.shape
    total = left.shape[1]
    tall = min(1024, total)
    return pl.pallas_call(
        tall_kernel,
        grid=(total // tall,),
        in_specs=[
            pl.BlockSpec((depth, tall), lambda i: (0, i)),
            pl.BlockSpec((depth, columns), lambda i: (0, 0)),
        ],
        out_specs=pl.BlockSpec((tall, columns), lambda i: (i, 0)),
        out_shape=jax.ShapeDtypeStruct((total, columns), BF16),
        cost_estimate=cost(),
        name="tall_rows_dot",
    )(left, grad)


def wide_kernel(bounds, parts, *refs):
    step = pl.program_id(0)
    operands, rest = refs[: 2 * len(bounds)], refs[2 * len(bounds) :]

    def write(left_ref, grad_ref):
        grad = grad_ref[0] if len(grad_ref.shape) == 3 else grad_ref[...]
        acc = jnp.dot(left_ref[...], grad, preferred_element_type=F32)
        if parts is None:
            rest[-1][...] = acc.astype(BF16)
            return
        acc = acc + rest[0][...].astype(F32)
        for (first, rows), out_ref in zip(parts, rest[1:]):
            out_ref[...] = acc[first : first + rows, :].astype(BF16)

    for i, (low, high) in enumerate(bounds):

        @pl.when((step >= low) & (step < high))
        def _(i=i):
            write(operands[2 * i], operands[2 * i + 1])


def wide_rows_dot(at, rows, pairs, extra=None, parts=None):
    in_specs, args, bounds, done = [], [], [], 0
    wide = min(min(1024, grad.shape[-1]) for _, grad in pairs)
    for left, grad in pairs:
        depth = left.shape[1]
        count = grad.shape[0] if grad.ndim == 3 else grad.shape[1] // wide
        in_specs.append(pl.BlockSpec((rows, depth), lambda j: (at, 0)))

        def clip(j, done=done, count=count):
            return jnp.clip(j - done, 0, count - 1)

        if grad.ndim == 3:
            in_specs.append(pl.BlockSpec((1, depth, wide), lambda j, clip=clip: (clip(j), 0, 0)))
        else:
            in_specs.append(pl.BlockSpec((depth, wide), lambda j, clip=clip: (0, clip(j))))
        args += [left, grad]
        bounds.append((done, done + count))
        done += count
    spec = pl.BlockSpec((rows, wide), lambda j: (0, j))
    columns = done * wide
    if parts is None:
        out_specs, out_shape = spec, jax.ShapeDtypeStruct((rows, columns), BF16)
    else:
        in_specs.append(spec)
        args.append(extra)
        out_specs = [pl.BlockSpec((count, wide), lambda j: (0, j)) for _, count in parts]
        out_shape = [jax.ShapeDtypeStruct((count, columns), BF16) for _, count in parts]
    return pl.pallas_call(
        functools.partial(wide_kernel, bounds, parts),
        grid=(done,),
        in_specs=in_specs,
        out_specs=out_specs,
        out_shape=out_shape,
        cost_estimate=cost(),
        name="wide_rows_dot",
    )(*args)


def per_device(
    dp,
    fs,
    tokens,
    lengths,
    time_embed,
    cotangent,
    time_weight,
    attn_gain,
    attn_shift,
    qkv_weight,
    out_weight,
    mlp_gain,
    mlp_shift,
    up_weight,
    up_bias,
    down_weight,
    down_bias,
):
    net = Net(dp, fs)
    length, width = tokens.shape[1:]
    tokens, cotangent = tokens.reshape(length, width), cotangent.reshape(length, width)
    order = Order()
    wide_rows, tall_rows = qkv_weight.shape[0], down_weight.shape[0]
    te_rows = time_weight.shape[0]
    heads = width // HD
    half = width // 2
    with jax.named_scope("up_gather"):
        up_full = lax.all_gather(up_weight, "fsdp", axis=0, tiled=True)
    with jax.named_scope("small_gather"):
        small = SmallGather(
            net,
            time_weight,
            [attn_gain, attn_shift, mlp_gain, mlp_shift, down_bias, up_bias],
            time_embed,
        )
    order.note(small.packed)
    with jax.named_scope("attn_gather"):
        attn_net = Gather(net, jnp.concatenate([qkv_weight, out_weight], axis=1))
        attn_net.along(order(attn_net.own))
    down_net = Gather(net, down_weight)
    residual = tokens.astype(F32)
    normed_one, inverse_one = normalize(residual)
    ready = order(inverse_one, down_net.own)
    down_net.own = ready[1]
    with jax.named_scope("small_gather"):
        small.across(order)
    with jax.named_scope("attn_gather"):
        attn_net.join_line(order)
        order.note(attn_net.line)
        attn_net.across()
    with jax.named_scope("small_gather"):
        small.other(order)
    with jax.named_scope("down_gather"):
        down_net.along(order(down_net.own))
    with jax.named_scope("small_gather"):
        (
            time_scale,
            embeds,
            gain_one,
            shift_one,
            gain_two,
            shift_two,
            down_bias_full,
            up_bias_full,
        ) = small.finish(order, time_embed)

    place = relative_order(net, wide_rows, width)
    permute = (jnp.arange(width, dtype=jnp.int32)[:, None] == place[None, :]).astype(BF16)

    def turn(values_in):
        return back_dot(permute, values_in).astype(BF16)

    key_mask = jnp.arange(length, dtype=jnp.int32)[:, None] < lengths[None, :]
    affine_one = normed_one * gain_one + shift_one
    attn_in = (affine_one * time_scale).astype(BF16)
    cosine, sine = rotary_tables(length)
    order.note(attn_in, cosine, sine)
    turned_one = order.note(turn(order(attn_in)))
    with jax.named_scope("attn_gather"):
        attn_net.join_across(order)
        attn_net.corners()
    with jax.named_scope("down_gather"):
        down_net.join_line(order)
        order.note(down_net.line)
        down_net.across()
    with jax.named_scope("attn_gather"):
        plan, pieces = attn_net.finish(order)
    qkv, qkv_full, out_full = qkv_rotated(net, attn_in, plan, pieces, wide_rows, cosine, sine)
    order.note(qkv)
    pairs = heads // 2
    part = pairs // 2
    with jax.named_scope("down_gather"):
        down_net.join_across(order)
        down_net.corners()
    context = order.note(attend(lengths, order(qkv), 0, pairs))
    context = order(context)
    hidden = residual + jnp.dot(context, out_full, preferred_element_type=F32)
    normed_two, inverse_two = normalize(hidden)
    affine_two = normed_two * gain_two + shift_two
    mlp_in = (affine_two * time_scale).astype(BF16)
    order.note(mlp_in)
    active, slope = up_gelu(order(mlp_in), up_full, up_bias_full)
    order.note(active)

    grad_out = cotangent.astype(F32) * key_mask.astype(F32)
    grad_branch = grad_out.astype(BF16)
    with jax.named_scope("down_grad"):
        tall = order.note(tall_rows_dot(order(active), grad_branch))
        down_mine = lax.psum_scatter(tall, "fsdp", scatter_dimension=0, tiled=True)
    down_bias_grad = jnp.sum(grad_branch.astype(F32), axis=0, keepdims=True)
    with jax.named_scope("down_gather"):
        plan, pieces = down_net.finish(order)
    grad_pre, up_bias_grad, down_full = down_back(
        net, order(grad_branch), plan, pieces, tall_rows, slope
    )
    grad_pre = order(order.note(grad_pre))
    grad_mlp_in = back_dot(grad_pre, up_full)
    grad_affine_two = grad_mlp_in * time_scale
    grad_scale = jnp.sum(grad_mlp_in * affine_two, axis=0, keepdims=True)
    mlp_gain_grad = jnp.sum(grad_affine_two * normed_two, axis=0, keepdims=True)
    mlp_shift_grad = jnp.sum(grad_affine_two, axis=0, keepdims=True)
    grad_hidden = grad_out + norm_back(grad_affine_two * gain_two, normed_two, inverse_two)
    grad_attn = order.note(grad_hidden.astype(BF16))
    turned_ctx = order.note(turn(order(context)))
    turned_two = order.note(turn(order(mlp_in)))
    wide_half = wide_rows // 2
    wide_parts = kept_parts(net.yn, wide_half)
    up_red, low_red, high_red = Scatter(net, True), Scatter(net, False), Scatter(net, True)
    up_pairs = [(turned_two, grad_pre), (turned_ctx, grad_attn)]
    with jax.named_scope("up_grad"):
        order(grad_pre)
        up_red.core(order.note(wide_rows_dot(1, half, up_pairs)))
    grad_context = order.note(back_dot(order(grad_attn), out_full).astype(BF16))
    with jax.named_scope("up_grad"):
        sent = up_red.join_core(order)
        kept = wide_rows_dot(0, half, up_pairs, sent, wide_parts)
        order.note(kept[0])
        up_red.corners(*kept)
    low = attend_back(lengths, qkv, order(grad_context), cosine, sine, 0, part)
    order.note(low)
    with jax.named_scope("qkv_grad"):
        low_red.core(order.note(wide_rows_dot(1, half, [(turned_one, order(low))])))
    with jax.named_scope("up_grad"):
        up_red.across(order)
    high = attend_back(lengths, qkv, order(grad_context), cosine, sine, part, pairs - part)
    order.note(high)
    with jax.named_scope("qkv_grad"):
        sent = low_red.join_core(order)
        kept = wide_rows_dot(0, half, [(turned_one, low)], sent, wide_parts)
        order.note(kept[0])
        low_red.corners(*kept)
        high_red.core(order.note(wide_rows_dot(1, half, [(turned_one, order(high))])))
        sent = high_red.join_core(order)
        kept = wide_rows_dot(0, half, [(turned_one, high)], sent, wide_parts)
        order.note(kept[0])
        high_red.corners(*kept)
    with jax.named_scope("up_grad"):
        up_line = Line(net, wide_half, [up_red.group(order)])
        order.note(up_line.kept)
    with jax.named_scope("qkv_grad"):
        low_red.across(order)
    grad_qkv = jnp.concatenate([item for i in range(3) for item in (low[i], high[i])], axis=1)
    grad_attn_in = back_dot(order(grad_qkv), qkv_full)
    grad_affine_one = grad_attn_in * time_scale
    grad_scale = grad_scale + jnp.sum(grad_attn_in * affine_one, axis=0, keepdims=True)
    attn_gain_grad = jnp.sum(grad_affine_one * normed_one, axis=0, keepdims=True)
    attn_shift_grad = jnp.sum(grad_affine_one, axis=0, keepdims=True)
    token_grad = (
        grad_hidden + norm_back(grad_affine_one * gain_one, normed_one, inverse_one)
    ).astype(BF16)
    order.note(token_grad, grad_scale)
    with jax.named_scope("qkv_grad"):
        high_red.across(order)
    with jax.named_scope("small_sums"):
        sums = jnp.concatenate(
            [
                attn_gain_grad,
                attn_shift_grad,
                mlp_gain_grad,
                mlp_shift_grad,
                down_bias_grad,
                up_bias_grad.reshape(-1, width),
            ],
            axis=0,
        )
        count = sums.shape[0]
        spots = jnp.arange(fs, dtype=jnp.int32)[:, None] == net.me
        packed = jnp.concatenate([sums, jnp.where(spots, grad_scale, 0.0)], axis=0)
        moved = net.c(packed)
    with jax.named_scope("up_grad"):
        up_line.nearer(order)
    with jax.named_scope("small_sums"):
        packed = packed + order(moved)
        moved = [net.y(packed, s) for s in range(1, net.yn)]
    branch_out = jnp.dot(order(active), down_full, preferred_element_type=F32) + down_bias_full
    layer_out = (hidden + branch_out).astype(BF16)
    order.note(layer_out)
    with jax.named_scope("small_sums"):
        for item in moved:
            packed = packed + order(item)
        moved = net.z(packed, 1)
    with jax.named_scope("qkv_grad"):
        qkv_line = Line(net, wide_half, [low_red.group(order), high_red.group(order)])
    with jax.named_scope("small_sums"):
        packed = packed + order(moved)
        moved = net.z(packed, 2)
    with jax.named_scope("up_grad"):
        up_line.last(order)
    with jax.named_scope("qkv_grad"):
        qkv_line.nearer(order)
    with jax.named_scope("small_sums"):
        packed = packed + order(moved)
        mine = lax.dynamic_slice_in_dim(embeds, net.me * te_rows, te_rows, 1)
        time_part = lax.dot_general(
            mine,
            packed[count:],
            (((0,), (0,)), ((), ())),
            precision=lax.Precision.HIGHEST,
            preferred_element_type=F32,
        )
        each = attn_gain.shape[0]
        vector_part = lax.dynamic_slice_in_dim(packed[:5], net.me * each, each, 1)
        bias_part = lax.dynamic_slice_in_dim(
            packed[5:count].reshape(1, -1), net.me * up_bias.shape[0], up_bias.shape[0], 1
        )
        packed = jnp.concatenate(
            [
                time_part,
                jnp.pad(vector_part, ((0, 0), (0, width - each))),
                jnp.pad(bias_part, ((0, 0), (0, width - up_bias.shape[0]))),
            ],
            axis=0,
        )
        if dp > 2:
            packed = lax.psum(packed, "dp")
        else:
            packed = packed + net.x(packed)
        time_weight_grad = packed[:te_rows]
        vector_grads = [packed[te_rows + i, :each] for i in range(5)]
        up_bias_out = packed[te_rows + 5, : up_bias.shape[0]]
    with jax.named_scope("down_grad"):
        down_mine = order(down_mine)
        if dp > 2:
            down_weight_grad = lax.psum(down_mine, "dp").astype(F32)
        else:
            down_other = net.x(down_mine)
    with jax.named_scope("qkv_grad"):
        qkv_line.last(order)
        whole = qkv_line.finish(order)
    with jax.named_scope("up_grad"):
        both = up_line.finish(order)
        ups = grad_pre.shape[1]
        up_weight_grad, out_weight_grad = both[:, :ups], both[:, ups:]
    if dp == 2:
        down_weight_grad = down_mine.astype(F32) + down_other.astype(F32)
    wide_low, wide_high = low.shape[2], high.shape[2]
    low_part, high_part = whole[:, : 3 * wide_low], whole[:, 3 * wide_low :]
    qkv_weight_grad = jnp.concatenate(
        [
            item
            for i in range(3)
            for item in (
                low_part[:, i * wide_low : (i + 1) * wide_low],
                high_part[:, i * wide_high : (i + 1) * wide_high],
            )
        ],
        axis=1,
    )
    return (
        layer_out[None],
        token_grad[None],
        time_weight_grad,
        vector_grads[0],
        vector_grads[1],
        qkv_weight_grad,
        out_weight_grad,
        vector_grads[2],
        vector_grads[3],
        up_weight_grad,
        up_bias_out,
        down_weight_grad,
        vector_grads[4],
    )


def solution(mesh):
    return jax.shard_map(
        functools.partial(per_device, mesh.shape["dp"], mesh.shape["fsdp"]),
        mesh=mesh,
        in_specs=(
            P(("dp", "fsdp"), None, None),
            P(("dp", "fsdp")),
            P(("dp", "fsdp"), None),
            P(("dp", "fsdp"), None, None),
            P("fsdp", None),
            P("fsdp"),
            P("fsdp"),
            P("fsdp", None),
            P("fsdp", None),
            P("fsdp"),
            P("fsdp"),
            P("fsdp", None),
            P("fsdp"),
            P("fsdp", None),
            P("fsdp"),
        ),
        out_specs=(
            P(("dp", "fsdp"), None, None),
            P(("dp", "fsdp"), None, None),
            P("fsdp", None),
            P("fsdp"),
            P("fsdp"),
            P("fsdp", None),
            P("fsdp", None),
            P("fsdp"),
            P("fsdp"),
            P("fsdp", None),
            P("fsdp"),
            P("fsdp", None),
            P("fsdp"),
        ),
        check_vma=False,
    )
```

time: 828 us -> 501 us (0.61)
  waiting for transfers between devices: 384 us -> 206 us
  matrix products: 199 us -> 41.2 us
  blocking collectives: 146 us -> 0 us
  Pallas kernels: 0 us -> 132 us
  starting transfers between devices: 0.86 us -> 46.1 us
  other arithmetic: 51.5 us -> 25.1 us
    reduce_scatter x5 -> x1, waiting for transfers between devices: 243 us -> 0.01 us  [per_device(): down_mine = lax.psum_scatter(tall, 'fsdp', scatter_dimension=0, tiled=True)]
    ppermute x0 -> x53, waiting for transfers between devices: none -> 206 us  [the longest x40 161 us: perm(): return lax.ppermute(values_in, 'fsdp', pairs)]
    dot_general x65 -> x3, matrix products: 167 us -> 13.7 us  [the longest x1 10.1 us: per_device(): jnp.dot(order(active), down_full, preferred_element_type=F32)]
    pallas_call x0 -> x21, Pallas kernels: none -> 132 us  [the longest x6 35.1 us: wide_rows_dot(): pl.pallas_call(functools.partial(wide_kernel, bounds, parts), grid=(done,...]
    all_gather x4 -> x1, waiting for transfers between devices: 99.1 us -> 0.01 us  [per_device(): up_full = lax.all_gather(up_weight, 'fsdp', axis=0, tiled=True)]
    unnamed x2 -> x0, blocking collectives: 97.1 us -> none
    ppermute x0 -> x53, starting transfers between devices: none -> 46 us  [the longest x40 31.5 us: perm(): return lax.ppermute(values_in, 'fsdp', pairs)]
    psum x1 -> x0, waiting for transfers between devices: 39.9 us -> none  [per_device(): lax.psum(attn_parts[3].astype(jnp.bfloat16), 'dp').astype(jnp.float32)]
  transfers between devices with their start and end apart: 10 -> 55, of which waited for: 6 -> 22; matrix products, arithmetic and copies ran while one was open for 28% -> 13% of each run, Pallas kernels for 0% -> 23%
where the time goes in v2:
time: 501 us; the launch traced here: 491 us
  waiting for transfers between devices  206 us (41%)
  Pallas kernels  132 us (26%)
  starting transfers between devices  46.1 us (9%)
  matrix products  41.2 us (8%)
  other arithmetic  25.1 us (5%)
  local copies, waits for them, and re-layouts  24.1 us (5%)
  between operations  15.9 us (3%)
    ppermute x40, waiting for transfers between devices, perm(): return lax.ppermute(values_in, 'fsdp', pairs)  161 us
    ppermute x13, waiting for transfers between devices, x(): return lax.ppermute(values_in, 'dp', [(i, i ^ 1) for i in range(self.dp)])  45 us
    pallas_call x6, Pallas kernels, wide_rows_dot(): pl.pallas_call(functools.partial(wide_kernel, bounds, parts), grid=(done,...  35.1 us
    ppermute x40, starting transfers between devices, perm(): return lax.ppermute(values_in, 'fsdp', pairs)  31.5 us
    dot_general x6, matrix products, back_dot(): lax.dot_general(grad_in, weight, (((1,), (1,)), ((), ())), preferred_elem...  27.5 us
    pallas_call x2, Pallas kernels, attend_back(): pl.pallas_call(attend_back_kernel, grid_spec=pltpu.PrefetchScalarGridSpec...  24.2 us
    ppermute x13, starting transfers between devices, x(): return lax.ppermute(values_in, 'dp', [(i, i ^ 1) for i in range(self.dp)])  14.5 us
    pallas_call x1, Pallas kernels, up_gelu(): pl.pallas_call(up_kernel, grid=(total // wide,), in_specs=[pl.BlockSpec((...  12.8 us
  transfers between devices with their start and end apart: 55, of which 22 were waited for; matrix products, arithmetic and copies ran while one was open for 13% of the time, Pallas kernels for 23%

profile of v2, /device:TPU:0, one launch (start us, length us, event | category | flops | bytes accessed | tf_op | source)
XLA Modules:
  0.0 491.0 jit_solution(15559348712291636237)
XLA Ops:
  10.7 5.1 %collective-permute-start.2 = (bf16[32,1024]{1,0:T(8,128)(2,1)}, bf16[32,1024]{1,0:T(8,128)(2,1)S(1)}, u32[]{:S(2)}, u32[]{:S(2)}) collective-permute-start(bf16[32,1024]{1,0:T(8,128)(2,1)} %pack_small.1), channel_id=1, source_target_pairs={{0,12},{1,13},{2,14},{3,15},{4,8},{5,9},{6,10},{7,11},{8,4},{9,5},... | collective-permute-start | bytes 196616 | tf_op jit(solution)/shard_map/small_gather/z_hop/ppermute | solution.py:99
  17.3 3.8 collective-permute-start.6
  24.1 6.2 %collective-permute-done.1 = bf16[32,1024]{1,0:T(8,128)(2,1)S(1)} collective-permute-done((bf16[32,1024]{1,0:T(8,128)(2,1)}, bf16[32,1024]{1,0:T(8,128)(2,1)S(1)}, u32[]{:S(2)}, u32[]{:S(2)}) %collective-permute-start.1) | collective-permute-done | bytes 65568 | tf_op jit(solution)/shard_map/small_gather/z_hop/ppermute | solution.py:99
  30.4 2.7 collective-permute-done.6.refs_3_
  33.1 28.0 %collective-permute-done.5.refs_2_ = bf16[32,4096]{1,0:T(8,128)(2,1)} collective-permute-done((bf16[32,4096]{1,0:T(8,128)(2,1)S(1)}, bf16[32,4096]{1,0:T(8,128)(2,1)}, u32[]{:S(2)}, u32[]{:S(2)}) %collective-permute-start.5) | collective-permute-done | bytes 262176 | tf_op jit(solution)/shard_map/attn_gather/z_hop/ppermute | solution.py:99
  69.7 2.6 collective-permute-start.14
  73.1 3.5 small_join.1
  78.4 2.3 fusion.28.refs_0_
  80.7 30.8 %collective-permute-done.9.refs_2_ = bf16[128,4096]{1,0:T(8,128)(2,1)} collective-permute-done((bf16[128,4096]{1,0:T(8,128)(2,1)}, bf16[128,4096]{1,0:T(8,128)(2,1)}, u32[]{:S(2)}, u32[]{:S(2)}) %collective-permute-start.9) | collective-permute-done | bytes 1048608 | tf_op jit(solution)/shard_map/attn_gather/y_hop/ppermute | solution.py:99
  117.7 11.6 %collective-permute-done.12.refs_1_ = bf16[128,1024]{1,0:T(8,128)(2,1)S(1)} collective-permute-done((bf16[128,1024]{1,0:T(8,128)(2,1)S(1)}, bf16[128,1024]{1,0:T(8,128)(2,1)S(1)}, u32[]{:S(2)}, u32[]{:S(2)}) %collective-permute-start.12) | collective-permute-done | bytes 262176 | tf_op jit(solution)/shard_map/down_gather/z_hop/ppermute | solution.py:99
  136.5 2.5 convert_reduce_fusion.1
  140.2 9.5 %qkv_rotated.1 = (bf16[512,3072]{1,0:T(8,128)(2,1)S(1)}, bf16[1024,3072]{1,0:T(8,128)(2,1)S(1)}, bf16[1024,1024]{1,0:T(8,128)(2,1)S(1)}) custom-call(s32[4]{0:T(128)S(1)} %pad_add_fusion.where_ref, bf16[512,1024]{1,0:T(8,128)(2,1)S(1)} %fusion.14.x_ref, f32[512,128]{1,0:T(8,128)S(1)} %get-tuple-element.230.cos_ref, ...), custom_call_target="tpu_custom_call" | custom-call | flops 1000 | bytes 1000 | tf_op jit(solution)/shard_map/qkv_rotated/pallas_call | solution.py:486
  151.4 6.7 %collective-permute-done.21.refs_2_ = bf16[512,1024]{1,0:T(8,128)(2,1)} collective-permute-done((bf16[512,1024]{1,0:T(8,128)(2,1)}, bf16[512,1024]{1,0:T(8,128)(2,1)}, u32[]{:S(2)}, u32[]{:S(2)}) %collective-permute-start.21) | collective-permute-done | bytes 1048608 | tf_op jit(solution)/shard_map/down_gather/y_hop/ppermute | solution.py:99
  165.6 11.1 %attend.1 = bf16[512,1024]{1,0:T(8,128)(2,1)} custom-call(s32[1]{0:T(128)} %copy.40.len_ref, bf16[512,3072]{1,0:T(8,128)(2,1)} %copy-done.2, bf16[512,3072]{1,0:T(8,128)(2,1)} %copy-done.2, bf16[512,3072]{1,0:T(8,128)(2,1)} %copy-done.2), custom_call_target="tpu_custom_call" | custom-call | flops 1000 | bytes 1000 | tf_op jit(solution)/shard_map/attend/pallas_call | solution.py:657
  176.7 3.3 fusion.87
  182.7 12.8 %up_gelu.1 = (bf16[512,4096]{1,0:T(8,128)(2,1)}, bf16[512,4096]{1,0:T(8,128)(2,1)}) custom-call(bf16[512,1024]{1,0:T(8,128)(2,1)} %multiply_convert_fusion.x_ref, bf16[1024,4096]{1,0:T(8,128)(2,1)} %all-gather.2.cloned.1.call-done.w_ref, f32[1,4096]{1,0:T(1,128)} %get-tuple-element.145.b_ref), custom_call_target="tpu_custom_call" | custom-call | flops 1000 | bytes 1000 | tf_op jit(solution)/shard_map/up_gelu/pallas_call | solution.py:531
  195.5 9.0 %tall_rows_dot.1 = bf16[4096,1024]{1,0:T(8,128)(2,1)} custom-call(bf16[512,4096]{1,0:T(8,128)(2,1)} %get-tuple-element.184.left_ref, bf16[512,1024]{1,0:T(8,128)(2,1)} %get-tuple-element.150.grad_ref.g_ref), custom_call_target="tpu_custom_call" | custom-call | flops 1000 | bytes 1000 | tf_op jit(solution)/shard_map/down_grad/tall_rows_dot/pallas_call | solution.py:748
  207.3 9.8 %down_back.1 = (bf16[512,4096]{1,0:T(8,128)(2,1)S(1)}, f32[1,4096]{1,0:T(1,128)S(1)}, bf16[4096,1024]{1,0:T(8,128)(2,1)}) custom-call(s32[4]{0:T(128)S(1)} %pad_add_fusion.where_ref, bf16[512,1024]{1,0:T(8,128)(2,1)S(1)} %copy-done.4, bf16[512,4096]{1,0:T(8,128)(2,1)} %get-tuple-element.151.slope_ref, bf16[512,1024]{1,0:T(8,128)(2,1)} %stack_rows.3.refs_0_, ...), custom_call_target="tpu_custom_call" | custom-call | flops 1000 | bytes 1000 | tf_op jit(solution)/shard_map/down_back/pallas_call | solution.py:602
  217.1 9.7 %multiply_reduce_fusion = (f32[1024]{0:T(1024)S(1)}, f32[512]{0:T(512)S(1)}, f32[1024]{0:T(1024)S(1)}, f32[512]{0:T(512)S(1)}, f32[1024]{0:T(1024)S(1)}, /*index=5*/f32[512,1024]{1,0:T(8,128)S(1)}) fusion(f32[512,1024]{1,0:T(8,128)S(1)} %copy-done.16, f32[1024]{0:T(1024)S(1)} %bitcast.150, f32[1024]{0:T(1024)S(1)} %bitcast.145, f32[512]{0:T(512)S(1)} %add_rsqrt_fusion, ...), kind=kOutput, calls=%fused_computation.31 | convolution fusion | flops 4302303232 | bytes 16809984 | tf_op jit(solution)/shard_map/dot_general | solution.py:41
  226.9 2.3 fusion.85
  229.2 2.3 fusion.29.refs_2_
  233.7 7.6 %wide_rows_dot.6 = bf16[512,5120]{1,0:T(8,128)(2,1)} custom-call(bf16[1024,512]{1,0:T(8,128)(2,1)} %fusion.30.refs_0_, bf16[512,4096]{1,0:T(8,128)(2,1)} %copy-done.3, bf16[1024,512]{1,0:T(8,128)(2,1)} %fusion.29.refs_2_, bf16[512,1024]{1,0:T(8,128)(2,1)} %get-tuple-element.156.refs_3_), custom_call_target="tpu_custom_call" | custom-call | flops 1000 | bytes 1000 | tf_op jit(solution)/shard_map/up_grad/wide_rows_dot/pallas_call | solution.py:810
  242.9 3.5 convolution_convert_fusion.g_ref
  246.4 6.2 %collective-permute-done.29.refs_4_ = bf16[512,5120]{1,0:T(8,128)(2,1)} collective-permute-done((bf16[512,5120]{1,0:T(8,128)(2,1)}, bf16[512,5120]{1,0:T(8,128)(2,1)}, u32[]{:S(2)}, u32[]{:S(2)}) %collective-permute-start.29) | collective-permute-done | bytes 5242912 | tf_op jit(solution)/shard_map/up_grad/core_hop/ppermute | solution.py:99
  252.6 10.1 %wide_rows_dot.7 = (bf16[128,5120]{1,0:T(8,128)(2,1)}, bf16[128,5120]{1,0:T(8,128)(2,1)}, bf16[128,5120]{1,0:T(8,128)(2,1)}, bf16[128,5120]{1,0:T(8,128)(2,1)}) custom-call(bf16[1024,512]{1,0:T(8,128)(2,1)} %fusion.30.refs_0_, bf16[512,4096]{1,0:T(8,128)(2,1)} %copy-done.3, bf16[1024,512]{1,0:T(8,128)(2,1)} %fusion.29.refs_2_, ...), custom_call_target="tpu_custom_call" | custom-call | flops 1000 | bytes 1000 | tf_op jit(solution)/shard_map/up_grad/wide_rows_dot/pallas_call | solution.py:810
  262.7 12.1 %attend_back.2.refs_1_ = bf16[3,512,512]{2,1,0:T(8,128)(2,1)} custom-call(s32[1]{0:T(128)} %copy.40.len_ref, bf16[512,3072]{1,0:T(8,128)(2,1)} %copy-done.2, bf16[512,3072]{1,0:T(8,128)(2,1)} %copy-done.2, bf16[512,3072]{1,0:T(8,128)(2,1)} %copy-done.2, bf16[512,1024]{1,0:T(8,128)(2,1)} %convolution_convert_fusion.g_ref, f32[512,128]{1,0:T(8,128)} %copy-done.6, ...), custom_call_target="tpu_custom_call" | custom-call | flops 1000 | bytes 1000 | tf_op jit(solution)/shard_map/attend_back/pallas_call | solution.py:724
  274.7 4.1 wide_rows_dot.8
  282.3 28.6 %collective-permute-done.30 = bf16[128,5120]{1,0:T(8,128)(2,1)} collective-permute-done((bf16[128,5120]{1,0:T(8,128)(2,1)}, bf16[128,5120]{1,0:T(8,128)(2,1)}, u32[]{:S(2)}, u32[]{:S(2)}) %collective-permute-start.30) | collective-permute-done | bytes 1310752 | tf_op jit(solution)/shard_map/up_grad/x_hop/ppermute | solution.py:115
  311.0 12.2 %attend_back.3.refs_1_ = bf16[3,512,512]{2,1,0:T(8,128)(2,1)} custom-call(s32[1]{0:T(128)} %copy.40.len_ref, bf16[512,3072]{1,0:T(8,128)(2,1)} %copy-done.2, bf16[512,3072]{1,0:T(8,128)(2,1)} %copy-done.2, bf16[512,3072]{1,0:T(8,128)(2,1)} %copy-done.2, bf16[512,1024]{1,0:T(8,128)(2,1)} %convolution_convert_fusion.g_ref, f32[512,128]{1,0:T(8,128)} %copy-done.6, ...), custom_call_target="tpu_custom_call" | custom-call | flops 1000 | bytes 1000 | tf_op jit(solution)/shard_map/attend_back/pallas_call | solution.py:724
  324.4 4.5 wide_rows_dot.9
  328.9 4.2 wide_rows_dot.10
  333.1 3.3 add_convert_fusion
  341.9 4.6 wide_rows_dot.11
  346.5 21.8 %collective-permute-done.34.refs_2_ = bf16[128,5120]{1,0:T(8,128)(2,1)} collective-permute-done((bf16[128,5120]{1,0:T(8,128)(2,1)}, bf16[128,5120]{1,0:T(8,128)(2,1)}, u32[]{:S(2)}, u32[]{:S(2)}) %collective-permute-start.34) | collective-permute-done | bytes 1310752 | tf_op jit(solution)/shard_map/up_grad/y_hop/ppermute | solution.py:99
  368.3 3.7 sum_split.4
  372.0 4.7 collective-permute-done.32
  380.7 3.4 collective-permute-start.37
  384.2 7.6 %fusion.17 = (f32[512]{0:T(512)S(1)}, f32[1024]{0:T(1024)S(1)}, f32[1024]{0:T(1024)S(1)}, f32[512]{0:T(512)S(1)}, f32[1024]{0:T(1024)S(1)}, /*index=5*/f32[512,1024]{1,0:T(8,128)S(1)}) fusion(bf16[1,512,1024]{2,1,0:T(8,128)(2,1)S(1)} %copy-done.20, f32[1024]{0:T(1024)S(1)} %bitcast.134, f32[1024]{0:T(1024)S(1)} %bitcast.141, f32[512]{0:T(512)S(1)} %add_rsqrt_fusion.1, ...), kind=kOutput, calls=%fused_computation.21 | convolution fusion | flops 3229085696 | bytes 12615680 | tf_op jit(solution)/shard_map/dot_general | solution.py:41
  394.3 5.1 %collective-permute-done.38 = bf16[128,1536]{1,0:T(8,128)(2,1)} collective-permute-done((bf16[128,1536]{1,0:T(8,128)(2,1)}, bf16[128,1536]{1,0:T(8,128)(2,1)}, u32[]{:S(2)}, u32[]{:S(2)}) %collective-permute-start.38) | collective-permute-done | bytes 393248 | tf_op jit(solution)/shard_map/qkv_grad/x_hop/ppermute | solution.py:115
  400.6 11.1 %collective-permute-done.37.refs_1_ = bf16[64,5120]{1,0:T(8,128)(2,1)S(1)} collective-permute-done((bf16[64,5120]{1,0:T(8,128)(2,1)}, bf16[64,5120]{1,0:T(8,128)(2,1)S(1)}, u32[]{:S(2)}, u32[]{:S(2)}) %collective-permute-start.37) | collective-permute-done | bytes 655392 | tf_op jit(solution)/shard_map/up_grad/z_hop/ppermute | solution.py:99
  413.8 10.1 %add_convert_fusion.1 = bf16[512,1024]{1,0:T(8,128)(2,1)} fusion(f32[512,1024]{1,0:T(8,128)S(1)} %copy-done.17, bf16[512,4096]{1,0:T(8,128)(2,1)} %get-tuple-element.184.left_ref, bf16[4096,1024]{1,0:T(8,128)(2,1)} %get-tuple-element.185, f32[1024]{0:T(1024)S(1)} %bitcast.161), kind=kOutput, calls=%fused_computation.30 | convolution fusion | flops 4296540160 | bytes 15732736 | tf_op jit(solution)/shard_map/dot_general | solution.py:1016
  425.1 2.8 sum_split.5
  427.9 2.5 sum_split.6
  432.7 17.5 %collective-permute-done.40 = f32[25,1024]{1,0:T(8,128)S(1)} collective-permute-done((f32[25,1024]{1,0:T(8,128)S(1)}, f32[25,1024]{1,0:T(8,128)S(1)}, u32[]{:S(2)}, u32[]{:S(2)}) %collective-permute-start.40) | collective-permute-done | bytes 102432 | tf_op jit(solution)/shard_map/small_sums/z_hop/ppermute | solution.py:99
  450.7 6.3 %collective-permute-done.45 = f32[25,1024]{1,0:T(8,128)S(1)} collective-permute-done((f32[25,1024]{1,0:T(8,128)S(1)}, f32[25,1024]{1,0:T(8,128)S(1)}, u32[]{:S(2)}, u32[]{:S(2)}) %collective-permute-start.45) | collective-permute-done | bytes 102432 | tf_op jit(solution)/shard_map/small_sums/z_hop/ppermute | solution.py:99
  464.1 3.7 collective-permute-done.49
  471.4 5.2 %collective-permute-done.50 = bf16[32,3072]{1,0:T(8,128)(2,1)S(1)} collective-permute-done((bf16[32,3072]{1,0:T(8,128)(2,1)S(1)}, bf16[32,3072]{1,0:T(8,128)(2,1)S(1)}, u32[]{:S(2)}, u32[]{:S(2)}) %collective-permute-start.50) | collective-permute-done | bytes 196640 | tf_op jit(solution)/shard_map/qkv_grad/x_hop/ppermute | solution.py:115
  478.7 3.8 collective-permute-done.52
  (270 shorter events, 89.1 us)
Async XLA Ops:
  7.2 175.5 %all-gather.2.cloned.1.call-start = ((), (), s32[]{:S(2)}) async-start(), calls=%async_computation.1 | async-start | bytes 8912896 | tf_op jit(solution)/shard_map/up_gather/all_gather | solution.py:849
  7.9 456.2 %reduce-scatter.2.cloned.1.call-start = ((), (), s32[]{:S(2)}) async-start(), calls=%async_computation.2 | async-start | bytes 8912896 | tf_op jit(solution)/shard_map/down_grad/reduce_scatter | solution.py:930
  10.7 12.7 %collective-permute-start.2 = (bf16[32,1024]{1,0:T(8,128)(2,1)}, bf16[32,1024]{1,0:T(8,128)(2,1)S(1)}, u32[]{:S(2)}, u32[]{:S(2)}) collective-permute-start(bf16[32,1024]{1,0:T(8,128)(2,1)} %pack_small.1), channel_id=1, source_target_pairs={{0,12},{1,13},{2,14},{3,15},{4,8},{5,9},{6,10},{7,11},{8,4},{9,5},... | collective-permute-start | bytes 196616 | tf_op jit(solution)/shard_map/small_gather/z_hop/ppermute | solution.py:99
  15.8 14.5 %collective-permute-start.1 = (bf16[32,1024]{1,0:T(8,128)(2,1)}, bf16[32,1024]{1,0:T(8,128)(2,1)S(1)}, u32[]{:S(2)}, u32[]{:S(2)}) collective-permute-start(bf16[32,1024]{1,0:T(8,128)(2,1)} %pack_small.1), channel_id=1, source_target_pairs={{0,8},{1,9},{2,10},{3,11},{4,12},{5,13},{6,14},{7,15},{8,0},{9,1},... | collective-permute-start | bytes 196616 | tf_op jit(solution)/shard_map/small_gather/z_hop/ppermute | solution.py:99
  15.8 14.5 %collective-permute-start = (bf16[32,1024]{1,0:T(8,128)(2,1)}, bf16[32,1024]{1,0:T(8,128)(2,1)S(1)}, u32[]{:S(2)}, u32[]{:S(2)}) collective-permute-start(bf16[32,1024]{1,0:T(8,128)(2,1)} %pack_small.1), channel_id=1, source_target_pairs={{0,4},{1,5},{2,6},{3,7},{4,0},{5,1},{6,2},{7,3},{8,12},{9,13},{10,... | collective-permute-start | bytes 196616 | tf_op jit(solution)/shard_map/small_gather/z_hop/ppermute | solution.py:99
  17.3 15.8 %collective-permute-start.6 = (bf16[32,4096]{1,0:T(8,128)(2,1)S(1)}, bf16[32,4096]{1,0:T(8,128)(2,1)S(1)}, u32[]{:S(2)}, u32[]{:S(2)}) collective-permute-start(bf16[32,4096]{1,0:T(8,128)(2,1)S(1)} %fusion.38.refs_0_), channel_id=1, source_target_pairs={{0,12},{1,13},{2,14},{3,15},{4,8},{5,9},{6,10},{7,11},{8,4},{9,5},... | collective-permute-start | bytes 786440 | tf_op jit(solution)/shard_map/attn_gather/z_hop/ppermute | solution.py:99
  21.2 39.9 %collective-permute-start.5 = (bf16[32,4096]{1,0:T(8,128)(2,1)S(1)}, bf16[32,4096]{1,0:T(8,128)(2,1)}, u32[]{:S(2)}, u32[]{:S(2)}) collective-permute-start(bf16[32,4096]{1,0:T(8,128)(2,1)S(1)} %fusion.38.refs_0_), channel_id=1, source_target_pairs={{0,8},{1,9},{2,10},{3,11},{4,12},{5,13},{6,14},{7,15},{8,0},{9,1},... | collective-permute-start | bytes 786440 | tf_op jit(solution)/shard_map/attn_gather/z_hop/ppermute | solution.py:99
  23.4 37.7 %collective-permute-start.4 = (bf16[32,4096]{1,0:T(8,128)(2,1)S(1)}, bf16[32,4096]{1,0:T(8,128)(2,1)S(1)}, u32[]{:S(2)}, u32[]{:S(2)}) collective-permute-start(bf16[32,4096]{1,0:T(8,128)(2,1)S(1)} %fusion.38.refs_0_), channel_id=1, source_target_pairs={{0,4},{1,5},{2,6},{3,7},{4,0},{5,1},{6,2},{7,3},{8,12},{9,13},{10,... | collective-permute-start | bytes 786440 | tf_op jit(solution)/shard_map/attn_gather/z_hop/ppermute | solution.py:99
  30.3 36.8 %collective-permute-start.3 = (bf16[4,32,1024]{2,1,0:T(8,128)(2,1)S(1)}, bf16[4,32,1024]{2,1,0:T(8,128)(2,1)}, u32[]{:S(2)}, u32[]{:S(2)}) collective-permute-start(bf16[4,32,1024]{2,1,0:T(8,128)(2,1)S(1)} %pad_maximum_fusion.1), channel_id=1, source_target_pairs={{0,2},{1,3},{2,0},{3,1},{4,6},{5,7},{6,4},{7,5},{8,10},{9,11},{10,... | collective-permute-start | bytes 786440 | tf_op jit(solution)/shard_map/small_gather/y_hop/ppermute | solution.py:99
  64.0 47.4 %collective-permute-start.9 = (bf16[128,4096]{1,0:T(8,128)(2,1)}, bf16[128,4096]{1,0:T(8,128)(2,1)}, u32[]{:S(2)}, u32[]{:S(2)}) collective-permute-start(bf16[128,4096]{1,0:T(8,128)(2,1)} %stack_rows.2.refs_0_), channel_id=1, source_target_pairs={{0,2},{1,3},{2,0},{3,1},{4,6},{5,7},{6,4},{7,5},{8,10},{9,11},{10,... | collective-permute-start | bytes 3145736 | tf_op jit(solution)/shard_map/attn_gather/y_hop/ppermute | solution.py:99
  65.6 45.9 %collective-permute-start.8 = (bf16[128,4096]{1,0:T(8,128)(2,1)}, bf16[128,4096]{1,0:T(8,128)(2,1)}, u32[]{:S(2)}, u32[]{:S(2)}) collective-permute-start(bf16[128,4096]{1,0:T(8,128)(2,1)} %stack_rows.2.refs_0_), channel_id=1, source_target_pairs={{0,16},{16,0},{1,17},{17,1},{2,18},{18,2},{3,19},{19,3},{4,20},{20... | collective-permute-start | bytes 3145736 | tf_op jit(solution)/shard_map/attn_gather/x_hop/ppermute | solution.py:115
  69.2 66.1 %collective-permute-start.15 = (bf16[128,4096]{1,0:T(8,128)(2,1)S(1)}, bf16[128,4096]{1,0:T(8,128)(2,1)}, u32[]{:S(2)}, u32[]{:S(2)}) collective-permute-start(bf16[128,4096]{1,0:T(8,128)(2,1)S(1)} %copy-done.7), channel_id=1, source_target_pairs={{0,1},{1,0},{2,3},{3,2},{4,5},{5,4},{6,7},{7,6},{8,9},{9,8},{10,11... | collective-permute-start | bytes 3145736 | tf_op jit(solution)/shard_map/attn_gather/core_hop/ppermute | solution.py:99
  69.7 46.0 %collective-permute-start.14 = (bf16[128,1024]{1,0:T(8,128)(2,1)}, bf16[128,1024]{1,0:T(8,128)(2,1)}, u32[]{:S(2)}, u32[]{:S(2)}) collective-permute-start(bf16[128,1024]{1,0:T(8,128)(2,1)} %constant_dynamic-slice_fusion.2.refs_0_), channel_id=1, source_target_pairs={{0,12},{1,13},{2,14},{3,15},{4,8},{5,9},{6,10},{7,11},{8,4},{9,5},... | collective-permute-start | bytes 786440 | tf_op jit(solution)/shard_map/down_gather/z_hop/ppermute | solution.py:99
  73.1 44.3 %collective-permute-start.13 = (bf16[128,1024]{1,0:T(8,128)(2,1)}, bf16[128,1024]{1,0:T(8,128)(2,1)}, u32[]{:S(2)}, u32[]{:S(2)}) collective-permute-start(bf16[128,1024]{1,0:T(8,128)(2,1)} %constant_dynamic-slice_fusion.2.refs_0_), channel_id=1, source_target_pairs={{0,8},{1,9},{2,10},{3,11},{4,12},{5,13},{6,14},{7,15},{8,0},{9,1},... | collective-permute-start | bytes 786440 | tf_op jit(solution)/shard_map/down_gather/z_hop/ppermute | solution.py:99
  113.4 21.8 %collective-permute-start.17 = (bf16[128,4096]{1,0:T(8,128)(2,1)}, bf16[128,4096]{1,0:T(8,128)(2,1)}, u32[]{:S(2)}, u32[]{:S(2)}) collective-permute-start(bf16[128,4096]{1,0:T(8,128)(2,1)} %collective-permute-done.9.refs_2_), channel_id=1, source_target_pairs={{0,1},{1,0},{2,3},{3,2},{4,5},{5,4},{6,7},{7,6},{8,9},{9,8},{10,11... | collective-permute-start | bytes 3145736 | tf_op jit(solution)/shard_map/attn_gather/core_hop/ppermute | solution.py:99
  115.3 17.0 %collective-permute-start.11 = (bf16[64,4096]{1,0:T(8,128)(2,1)}, bf16[64,4096]{1,0:T(8,128)(2,1)S(1)}, u32[]{:S(2)}, u32[]{:S(2)}) collective-permute-start(bf16[64,4096]{1,0:T(8,128)(2,1)} %slice.93), channel_id=1, source_target_pairs={{0,2},{1,3},{2,0},{3,1},{4,6},{5,7},{6,4},{7,5},{8,10},{9,11},{10,... | collective-permute-start | bytes 1572872 | tf_op jit(solution)/shard_map/attn_gather/y_hop/ppermute | solution.py:99
  115.7 18.1 %collective-permute-start.10 = (bf16[64,4096]{1,0:T(8,128)(2,1)}, bf16[64,4096]{1,0:T(8,128)(2,1)}, u32[]{:S(2)}, u32[]{:S(2)}) collective-permute-start(bf16[64,4096]{1,0:T(8,128)(2,1)} %slice.92), channel_id=1, source_target_pairs={{0,16},{16,0},{1,17},{17,1},{2,18},{18,2},{3,19},{19,3},{4,20},{20... | collective-permute-start | bytes 1572872 | tf_op jit(solution)/shard_map/attn_gather/x_hop/ppermute | solution.py:115
  117.4 11.9 %collective-permute-start.12 = (bf16[128,1024]{1,0:T(8,128)(2,1)S(1)}, bf16[128,1024]{1,0:T(8,128)(2,1)S(1)}, u32[]{:S(2)}, u32[]{:S(2)}) collective-permute-start(bf16[128,1024]{1,0:T(8,128)(2,1)S(1)} %copy-done.28), channel_id=1, source_target_pairs={{0,4},{1,5},{2,6},{3,7},{4,0},{5,1},{6,2},{7,3},{8,12},{9,13},{10,... | collective-permute-start | bytes 786440 | tf_op jit(solution)/shard_map/down_gather/z_hop/ppermute | solution.py:99
  130.0 9.0 %collective-permute-start.16 = (bf16[128,4096]{1,0:T(8,128)(2,1)}, bf16[128,4096]{1,0:T(8,128)(2,1)}, u32[]{:S(2)}, u32[]{:S(2)}) collective-permute-start(bf16[128,4096]{1,0:T(8,128)(2,1)} %collective-permute-done.8.refs_1_), channel_id=1, source_target_pairs={{0,1},{1,0},{2,3},{3,2},{4,5},{5,4},{6,7},{7,6},{8,9},{9,8},{10,11... | collective-permute-start | bytes 3145736 | tf_op jit(solution)/shard_map/attn_gather/core_hop/ppermute | solution.py:99
  132.3 25.8 %collective-permute-start.21 = (bf16[512,1024]{1,0:T(8,128)(2,1)}, bf16[512,1024]{1,0:T(8,128)(2,1)}, u32[]{:S(2)}, u32[]{:S(2)}) collective-permute-start(bf16[512,1024]{1,0:T(8,128)(2,1)} %stack_rows.3.refs_0_), channel_id=1, source_target_pairs={{0,2},{1,3},{2,0},{3,1},{4,6},{5,7},{6,4},{7,5},{8,10},{9,11},{10,... | collective-permute-start | bytes 3145736 | tf_op jit(solution)/shard_map/down_gather/y_hop/ppermute | solution.py:99
  133.9 25.5 %collective-permute-start.20 = (bf16[512,1024]{1,0:T(8,128)(2,1)}, bf16[512,1024]{1,0:T(8,128)(2,1)}, u32[]{:S(2)}, u32[]{:S(2)}) collective-permute-start(bf16[512,1024]{1,0:T(8,128)(2,1)} %stack_rows.3.refs_0_), channel_id=1, source_target_pairs={{0,16},{16,0},{1,17},{17,1},{2,18},{18,2},{3,19},{19,3},{4,20},{20... | collective-permute-start | bytes 3145736 | tf_op jit(solution)/shard_map/down_gather/x_hop/ppermute | solution.py:115
  139.0 66.1 %collective-permute-start.24 = (bf16[512,1024]{1,0:T(8,128)(2,1)}, bf16[512,1024]{1,0:T(8,128)(2,1)}, u32[]{:S(2)}, u32[]{:S(2)}) collective-permute-start(bf16[512,1024]{1,0:T(8,128)(2,1)} %stack_rows.3.refs_0_), channel_id=1, source_target_pairs={{0,1},{1,0},{2,3},{3,2},{4,5},{5,4},{6,7},{7,6},{8,9},{9,8},{10,11... | collective-permute-start | bytes 3145736 | tf_op jit(solution)/shard_map/down_gather/core_hop/ppermute | solution.py:99
  163.0 42.1 %collective-permute-start.26 = (bf16[512,1024]{1,0:T(8,128)(2,1)}, bf16[512,1024]{1,0:T(8,128)(2,1)S(1)}, u32[]{:S(2)}, u32[]{:S(2)}) collective-permute-start(bf16[512,1024]{1,0:T(8,128)(2,1)} %collective-permute-done.21.refs_2_), channel_id=1, source_target_pairs={{0,1},{1,0},{2,3},{3,2},{4,5},{5,4},{6,7},{7,6},{8,9},{9,8},{10,11... | collective-permute-start | bytes 3145736 | tf_op jit(solution)/shard_map/down_gather/core_hop/ppermute | solution.py:99
  163.1 42.1 %collective-permute-start.25 = (bf16[512,1024]{1,0:T(8,128)(2,1)}, bf16[512,1024]{1,0:T(8,128)(2,1)}, u32[]{:S(2)}, u32[]{:S(2)}) collective-permute-start(bf16[512,1024]{1,0:T(8,128)(2,1)} %collective-permute-done.20.refs_1_), channel_id=1, source_target_pairs={{0,1},{1,0},{2,3},{3,2},{4,5},{5,4},{6,7},{7,6},{8,9},{9,8},{10,11... | collective-permute-start | bytes 3145736 | tf_op jit(solution)/shard_map/down_gather/core_hop/ppermute | solution.py:99
  163.6 41.0 %collective-permute-start.23 = (bf16[256,1024]{1,0:T(8,128)(2,1)}, bf16[256,1024]{1,0:T(8,128)(2,1)S(1)}, u32[]{:S(2)}, u32[]{:S(2)}) collective-permute-start(bf16[256,1024]{1,0:T(8,128)(2,1)} %slice.95), channel_id=1, source_target_pairs={{0,2},{1,3},{2,0},{3,1},{4,6},{5,7},{6,4},{7,5},{8,10},{9,11},{10,... | collective-permute-start | bytes 1572872 | tf_op jit(solution)/shard_map/down_gather/y_hop/ppermute | solution.py:99
  164.1 40.4 %collective-permute-start.22 = (bf16[256,1024]{1,0:T(8,128)(2,1)}, bf16[256,1024]{1,0:T(8,128)(2,1)S(1)}, u32[]{:S(2)}, u32[]{:S(2)}) collective-permute-start(bf16[256,1024]{1,0:T(8,128)(2,1)} %slice.94), channel_id=1, source_target_pairs={{0,16},{16,0},{1,17},{17,1},{2,18},{18,2},{3,19},{19,3},{4,20},{20... | collective-permute-start | bytes 1572872 | tf_op jit(solution)/shard_map/down_gather/x_hop/ppermute | solution.py:115
  241.3 11.3 %collective-permute-start.29 = (bf16[512,5120]{1,0:T(8,128)(2,1)}, bf16[512,5120]{1,0:T(8,128)(2,1)}, u32[]{:S(2)}, u32[]{:S(2)}) collective-permute-start(bf16[512,5120]{1,0:T(8,128)(2,1)} %wide_rows_dot.6), channel_id=1, source_target_pairs={{0,1},{1,0},{2,3},{3,2},{4,5},{5,4},{6,7},{7,6},{8,9},{9,8},{10,11... | collective-permute-start | bytes 15728648 | tf_op jit(solution)/shard_map/up_grad/core_hop/ppermute | solution.py:99
  278.9 44.3 %collective-permute-start.31 = (bf16[512,1536]{1,0:T(8,128)(2,1)}, bf16[512,1536]{1,0:T(8,128)(2,1)S(1)}, u32[]{:S(2)}, u32[]{:S(2)}) collective-permute-start(bf16[512,1536]{1,0:T(8,128)(2,1)} %wide_rows_dot.8), channel_id=1, source_target_pairs={{0,1},{1,0},{2,3},{3,2},{4,5},{5,4},{6,7},{7,6},{8,9},{9,8},{10,11... | collective-permute-start | bytes 4718600 | tf_op jit(solution)/shard_map/qkv_grad/core_hop/ppermute | solution.py:99
  279.0 32.0 %collective-permute-start.30 = (bf16[128,5120]{1,0:T(8,128)(2,1)}, bf16[128,5120]{1,0:T(8,128)(2,1)}, u32[]{:S(2)}, u32[]{:S(2)}) collective-permute-start(bf16[128,5120]{1,0:T(8,128)(2,1)} %get-tuple-element.160), channel_id=1, source_target_pairs={{0,16},{16,0},{1,17},{17,1},{2,18},{18,2},{3,19},{19,3},{4,20},{20... | collective-permute-start | bytes 3932168 | tf_op jit(solution)/shard_map/up_grad/x_hop/ppermute | solution.py:115
  280.2 66.2 %collective-permute-start.33 = (bf16[128,5120]{1,0:T(8,128)(2,1)}, bf16[128,5120]{1,0:T(8,128)(2,1)S(1)}, u32[]{:S(2)}, u32[]{:S(2)}) collective-permute-start(bf16[128,5120]{1,0:T(8,128)(2,1)} %get-tuple-element.166), channel_id=1, source_target_pairs={{0,16},{16,0},{1,17},{17,1},{2,18},{18,2},{3,19},{19,3},{4,20},{20... | collective-permute-start | bytes 3932168 | tf_op jit(solution)/shard_map/up_grad/x_hop/ppermute | solution.py:115
  333.1 8.8 %collective-permute-start.35 = (bf16[512,1536]{1,0:T(8,128)(2,1)}, bf16[512,1536]{1,0:T(8,128)(2,1)}, u32[]{:S(2)}, u32[]{:S(2)}) collective-permute-start(bf16[512,1536]{1,0:T(8,128)(2,1)} %wide_rows_dot.10), channel_id=1, source_target_pairs={{0,1},{1,0},{2,3},{3,2},{4,5},{5,4},{6,7},{7,6},{8,9},{9,8},{10,11... | collective-permute-start | bytes 4718600 | tf_op jit(solution)/shard_map/qkv_grad/core_hop/ppermute | solution.py:99
  336.4 32.0 %collective-permute-start.34 = (bf16[128,5120]{1,0:T(8,128)(2,1)}, bf16[128,5120]{1,0:T(8,128)(2,1)}, u32[]{:S(2)}, u32[]{:S(2)}) collective-permute-start(bf16[128,5120]{1,0:T(8,128)(2,1)} %add_convert_fusion), channel_id=1, source_target_pairs={{0,2},{1,3},{2,0},{3,1},{4,6},{5,7},{6,4},{7,5},{8,10},{9,11},{10,... | collective-permute-start | bytes 3932168 | tf_op jit(solution)/shard_map/up_grad/y_hop/ppermute | solution.py:99
  338.0 38.8 %collective-permute-start.32 = (bf16[128,1536]{1,0:T(8,128)(2,1)}, bf16[128,1536]{1,0:T(8,128)(2,1)}, u32[]{:S(2)}, u32[]{:S(2)}) collective-permute-start(bf16[128,1536]{1,0:T(8,128)(2,1)} %get-tuple-element.165), channel_id=1, source_target_pairs={{0,2},{1,3},{2,0},{3,1},{4,6},{5,7},{6,4},{7,5},{8,10},{9,11},{10,... | collective-permute-start | bytes 1179656 | tf_op jit(solution)/shard_map/qkv_grad/y_hop/ppermute | solution.py:99
  340.5 84.6 %collective-permute-start.44 = (bf16[128,1536]{1,0:T(8,128)(2,1)}, bf16[128,1536]{1,0:T(8,128)(2,1)}, u32[]{:S(2)}, u32[]{:S(2)}) collective-permute-start(bf16[128,1536]{1,0:T(8,128)(2,1)} %get-tuple-element.192), channel_id=1, source_target_pairs={{0,2},{1,3},{2,0},{3,1},{4,6},{5,7},{6,4},{7,5},{8,10},{9,11},{10,... | collective-permute-start | bytes 1179656 | tf_op jit(solution)/shard_map/qkv_grad/y_hop/ppermute | solution.py:99
  378.6 46.4 %collective-permute-start.43 = (bf16[128,1536]{1,0:T(8,128)(2,1)}, bf16[128,1536]{1,0:T(8,128)(2,1)}, u32[]{:S(2)}, u32[]{:S(2)}) collective-permute-start(bf16[128,1536]{1,0:T(8,128)(2,1)} %add_convert_fusion.2), channel_id=1, source_target_pairs={{0,16},{16,0},{1,17},{17,1},{2,18},{18,2},{3,19},{19,3},{4,20},{20... | collective-permute-start | bytes 1179656 | tf_op jit(solution)/shard_map/qkv_grad/x_hop/ppermute | solution.py:115
  378.7 20.6 %collective-permute-start.38 = (bf16[128,1536]{1,0:T(8,128)(2,1)}, bf16[128,1536]{1,0:T(8,128)(2,1)}, u32[]{:S(2)}, u32[]{:S(2)}) collective-permute-start(bf16[128,1536]{1,0:T(8,128)(2,1)} %get-tuple-element.180), channel_id=1, source_target_pairs={{0,16},{16,0},{1,17},{17,1},{2,18},{18,2},{3,19},{19,3},{4,20},{20... | collective-permute-start | bytes 1179656 | tf_op jit(solution)/shard_map/qkv_grad/x_hop/ppermute | solution.py:115
  380.7 44.4 %collective-permute-start.41 = (bf16[128,1536]{1,0:T(8,128)(2,1)}, bf16[128,1536]{1,0:T(8,128)(2,1)}, u32[]{:S(2)}, u32[]{:S(2)}) collective-permute-start(bf16[128,1536]{1,0:T(8,128)(2,1)} %get-tuple-element.189), channel_id=1, source_target_pairs={{0,16},{16,0},{1,17},{17,1},{2,18},{18,2},{3,19},{19,3},{4,20},{20... | collective-permute-start | bytes 1179656 | tf_op jit(solution)/shard_map/qkv_grad/x_hop/ppermute | solution.py:115
  380.7 30.9 %collective-permute-start.37 = (bf16[64,5120]{1,0:T(8,128)(2,1)}, bf16[64,5120]{1,0:T(8,128)(2,1)S(1)}, u32[]{:S(2)}, u32[]{:S(2)}) collective-permute-start(bf16[64,5120]{1,0:T(8,128)(2,1)} %get-tuple-element.179), channel_id=1, source_target_pairs={{0,8},{1,9},{2,10},{3,11},{4,12},{5,13},{6,14},{7,15},{8,0},{9,1},... | collective-permute-start | bytes 1966088 | tf_op jit(solution)/shard_map/up_grad/z_hop/ppermute | solution.py:99
  399.4 13.1 %collective-permute-start.36 = (f32[25,1024]{1,0:T(8,128)S(1)}, f32[25,1024]{1,0:T(8,128)S(1)}, u32[]{:S(2)}, u32[]{:S(2)}) collective-permute-start(f32[25,1024]{1,0:T(8,128)S(1)} %concatenate.31), channel_id=1, source_target_pairs={{0,1},{1,0},{2,3},{3,2},{4,5},{5,4},{6,7},{7,6},{8,9},{9,8},{10,11... | collective-permute-start | bytes 307208 | tf_op jit(solution)/shard_map/small_sums/core_hop/ppermute | solution.py:99
  411.7 13.4 %collective-permute-start.42 = (bf16[128,1536]{1,0:T(8,128)(2,1)S(1)}, bf16[128,1536]{1,0:T(8,128)(2,1)}, u32[]{:S(2)}, u32[]{:S(2)}) collective-permute-start(bf16[128,1536]{1,0:T(8,128)(2,1)S(1)} %add_convert_fusion.3), channel_id=1, source_target_pairs={{0,2},{1,3},{2,0},{3,1},{4,6},{5,7},{6,4},{7,5},{8,10},{9,11},{10,... | collective-permute-start | bytes 1179656 | tf_op jit(solution)/shard_map/qkv_grad/y_hop/ppermute | solution.py:99
  412.5 12.6 %collective-permute-start.39 = (f32[25,1024]{1,0:T(8,128)S(1)}, f32[25,1024]{1,0:T(8,128)S(1)}, u32[]{:S(2)}, u32[]{:S(2)}) collective-permute-start(f32[25,1024]{1,0:T(8,128)S(1)} %add.256), channel_id=1, source_target_pairs={{0,2},{1,3},{2,0},{3,1},{4,6},{5,7},{6,4},{7,5},{8,10},{9,11},{10,... | collective-permute-start | bytes 307208 | tf_op jit(solution)/shard_map/small_sums/y_hop/ppermute | solution.py:99
  427.9 22.8 %collective-permute-start.46 = (bf16[64,3072]{1,0:T(8,128)(2,1)}, bf16[64,3072]{1,0:T(8,128)(2,1)S(1)}, u32[]{:S(2)}, u32[]{:S(2)}) collective-permute-start(bf16[64,3072]{1,0:T(8,128)(2,1)} %get-tuple-element.198), channel_id=1, source_target_pairs={{0,8},{1,9},{2,10},{3,11},{4,12},{5,13},{6,14},{7,15},{8,0},{9,1},... | collective-permute-start | bytes 1179656 | tf_op jit(solution)/shard_map/qkv_grad/z_hop/ppermute | solution.py:99
  430.4 20.3 %collective-permute-start.47 = (bf16[32,5120]{1,0:T(8,128)(2,1)}, bf16[32,5120]{1,0:T(8,128)(2,1)S(1)}, u32[]{:S(2)}, u32[]{:S(2)}) collective-permute-start(bf16[32,5120]{1,0:T(8,128)(2,1)} %get-tuple-element.199), channel_id=1, source_target_pairs={{0,4},{1,5},{2,6},{3,7},{4,0},{5,1},{6,2},{7,3},{8,12},{9,13},{10,... | collective-permute-start | bytes 983048 | tf_op jit(solution)/shard_map/up_grad/z_hop/ppermute | solution.py:99
  432.6 17.6 %collective-permute-start.40 = (f32[25,1024]{1,0:T(8,128)S(1)}, f32[25,1024]{1,0:T(8,128)S(1)}, u32[]{:S(2)}, u32[]{:S(2)}) collective-permute-start(f32[25,1024]{1,0:T(8,128)S(1)} %add.257), channel_id=1, source_target_pairs={{0,4},{1,5},{2,6},{3,7},{4,0},{5,1},{6,2},{7,3},{8,12},{9,13},{10,... | collective-permute-start | bytes 307208 | tf_op jit(solution)/shard_map/small_sums/z_hop/ppermute | solution.py:99
  450.2 6.8 %collective-permute-start.45 = (f32[25,1024]{1,0:T(8,128)S(1)}, f32[25,1024]{1,0:T(8,128)S(1)}, u32[]{:S(2)}, u32[]{:S(2)}) collective-permute-start(f32[25,1024]{1,0:T(8,128)S(1)} %add.260), channel_id=1, source_target_pairs={{0,8},{1,9},{2,10},{3,11},{4,12},{5,13},{6,14},{7,15},{8,0},{9,1},... | collective-permute-start | bytes 307208 | tf_op jit(solution)/shard_map/small_sums/z_hop/ppermute | solution.py:99
  458.2 18.5 %collective-permute-start.51 = (bf16[32,5120]{1,0:T(8,128)(2,1)S(1)}, bf16[32,5120]{1,0:T(8,128)(2,1)S(1)}, u32[]{:S(2)}, u32[]{:S(2)}) collective-permute-start(bf16[32,5120]{1,0:T(8,128)(2,1)S(1)} %add_convert_fusion.4), channel_id=1, source_target_pairs={{0,16},{16,0},{1,17},{17,1},{2,18},{18,2},{3,19},{19,3},{4,20},{20... | collective-permute-start | bytes 983048 | tf_op jit(solution)/shard_map/up_grad/x_hop/ppermute | solution.py:115
  468.8 7.8 %collective-permute-start.50 = (bf16[32,3072]{1,0:T(8,128)(2,1)S(1)}, bf16[32,3072]{1,0:T(8,128)(2,1)S(1)}, u32[]{:S(2)}, u32[]{:S(2)}) collective-permute-start(bf16[32,3072]{1,0:T(8,128)(2,1)S(1)} %add_convert_fusion.5), channel_id=1, source_target_pairs={{0,16},{16,0},{1,17},{17,1},{2,18},{18,2},{3,19},{19,3},{4,20},{20... | collective-permute-start | bytes 589832 | tf_op jit(solution)/shard_map/qkv_grad/x_hop/ppermute | solution.py:115
  469.8 12.7 %collective-permute-start.52 = (bf16[256,1024]{1,0:T(8,128)(2,1)}, bf16[256,1024]{1,0:T(8,128)(2,1)S(1)}, u32[]{:S(2)}, u32[]{:S(2)}) collective-permute-start(bf16[256,1024]{1,0:T(8,128)(2,1)} %reduce-scatter.2.cloned.1.call-done), channel_id=1, source_target_pairs={{0,16},{16,0},{1,17},{17,1},{2,18},{18,2},{3,19},{19,3},{4,20},{20... | collective-permute-start | bytes 1572872 | tf_op jit(solution)/shard_map/down_grad/x_hop/ppermute | solution.py:115
  (57 other events, 801.4 us)
Sparse Core Ops, SparseCore 0:
  10.2 118.2 all-gather.1
  241.6 102.9 reduce-scatter.1
